TPU v7x, 256 devices: a whole 4x4x8 slice. The times are simulated.
256 devices in a mesh: row: 16 (over y, x), col: 8 (over z), chan: 2 (over core).
Axes of the slice: x: 4, y: 4, z: 8, core: 2. Of those that a mesh axis runs over, the one named last changes fastest.
Arguments:
- samples: bfloat16 [8192, 2, 8192], P(('chan', 'col'), None, 'row'), parts along dimension 0, may hold values from -6 to 6
- sky_model: bfloat16 [8192, 2, 4096], P(('chan', 'row'), None, 'col'), parts along dimension 0, may hold values from -128 to 128, as said below
- initial_gains: float32 [2, 8192], P(None, ('chan', 'row', 'col')), parts along dimension 1, may hold values from -3 to 3, as said below
Outputs:
- calibrated: float32 [2, 8192], P(None, ('chan', 'row', 'col')), parts along dimension 1
There are 2 independent parts, one for each index of `chan`. A program takes and returns all parts, laid end to end along the dimension named above; each array names one. Nothing has to cross between parts.
Inputs may be any that keep to these rules, and one draw needn't show every extreme that they name: sky_model is Hermitian: sky_model[q,0,p] = sky_model[p,0,q] and sky_model[q,1,p] = -sky_model[p,1,q]. `initial_gains`: every initial gain has magnitude between 0.3 and 3.
All inputs are finite; a program needn't handle non-finite values.
Results may differ from a plain program's by a relative error of at most 0.0003.
Values may be sent and summed in bfloat16 or wider, within the bound.
No kernel may reach another device: no remote copies, remote signals or barrier semaphores. Data moves between devices by JAX's collectives and lax.ppermute only.
A program may use at most 192 MiB of HBM per device.

v0:
```python
import jax
import jax.numpy as jnp
from jax import lax
from jax.sharding import PartitionSpec as P

ITERS = 3


def body(samples, sky_model, initial_gains):
    row_count = lax.axis_size("row")
    column_count = lax.axis_size("col")
    row_index = lax.axis_index("row")
    column_index = lax.axis_index("col")
    block_column = samples.shape[0]
    block_row = sky_model.shape[0]
    share_size = initial_gains.shape[1]
    contract_last = (((1,), (1,)), ((), ()))
    upper_limit = lax.Precision.HIGHEST
    own_start = (row_index * column_count + column_index) * share_size
    flattened = samples.reshape(block_column, -1)
    rotated = jnp.concatenate([-samples[:, 1, :], samples[:, 0, :]], axis=1)
    right_side = jnp.concatenate([flattened, rotated], axis=0)
    all_antennas = lax.all_gather(flattened, "col", axis=0, tiled=True)
    vis_tile = lax.psum_scatter(
        lax.dot_general(
            all_antennas, right_side, contract_last, preferred_element_type=jnp.float32
        ),
        "row",
        scatter_dimension=0,
        tiled=True,
    )
    vis_real = vis_tile[:, :block_column]
    vis_imag = vis_tile[:, block_column:]
    model_real = sky_model[:, 0, :].astype(jnp.float32)
    model_imag = sky_model[:, 1, :].astype(jnp.float32)
    global_rows = row_index * block_row + lax.broadcasted_iota(
        jnp.int32, (block_row, block_column), 0
    )
    global_columns = column_index * block_column + lax.broadcasted_iota(
        jnp.int32, (block_row, block_column), 1
    )
    cross_mask = (global_rows != global_columns).astype(jnp.float32)
    weight_real = (vis_real * model_real + vis_imag * model_imag) * cross_mask
    weight_imag = (vis_real * model_imag - vis_imag * model_real) * cross_mask
    model_power = (model_real * model_real + model_imag * model_imag) * cross_mask
    stacked = jnp.concatenate([weight_real, weight_imag], axis=0)
    row_gains = lax.all_gather(initial_gains, "col", axis=1, tiled=True)
    everything = row_gains
    for iteration in range(ITERS):
        gain_real = row_gains[0]
        gain_imag = row_gains[1]
        left_rows = jnp.stack(
            [jnp.concatenate([gain_real, -gain_imag]), jnp.concatenate([gain_imag, gain_real])]
        )
        totals = jnp.dot(left_rows, stacked, precision=upper_limit)
        energy = jnp.dot(
            gain_real * gain_real + gain_imag * gain_imag, model_power, precision=upper_limit
        )
        totals, energy = (totals, energy)
        totals, energy = (
            lax.psum_scatter(totals, "row", scatter_dimension=1, tiled=True),
            lax.psum_scatter(energy, "row", scatter_dimension=0, tiled=True),
        )
        updated = totals / energy[None, :]
        if iteration == 1:
            previous = lax.dynamic_slice_in_dim(
                everything, (column_index * row_count + row_index) * share_size, share_size, 1
            )
            updated = 0.5 * (updated + previous)
        gain_block = lax.all_gather(updated, "row", axis=1, tiled=True)
        everything = lax.all_gather(gain_block, "col", axis=1, tiled=True)
        row_gains = lax.dynamic_slice_in_dim(everything, row_index * block_row, block_row, 1)
    return lax.dynamic_slice_in_dim(everything, own_start, share_size, 1)


def solution(mesh):
    return jax.shard_map(
        body,
        mesh=mesh,
        in_specs=(
            P(("chan", "col"), None, "row"),
            P(("chan", "row"), None, "col"),
            P(None, ("chan", "row", "col")),
        ),
        out_specs=P(None, ("chan", "row", "col")),
        check_vma=False,
    )
```

profile of v0, /device:TPU:64, one launch (start us, length us, event | category | flops | bytes accessed | tf_op | source)
XLA Modules:
  0.0 626.5 jit_solution(196961169140078920)
XLA Ops:
  6.5 2.5 copy.41
  9.2 1.5 fusion.48
  10.8 93.0 %all-gather.6.cloned.1.call-done = bf16[4096,1024]{1,0:T(8,128)(2,1)} async-done(((bf16[512,1024]{1,0:T(8,128)(2,1)}), bf16[4096,1024]{1,0:T(8,128)(2,1)}) %all-gather.6.cloned.1.call-update) | async-done | bytes 8388624 | tf_op jit(solution)/shard_map/all_gather | solution.py:23
  103.8 14.5 %convolution_bitcast_fusion = f32[4096,1024]{0,1:T(8,128)} fusion(bf16[4096,1024]{1,0:T(8,128)(2,1)} %all-gather.6.cloned.1.call-done, bf16[512,512]{1,0:T(8,128)(2,1)S(1)} %get-tuple-element.23, bf16[512,512]{1,0:T(8,128)(2,1)S(1)} %get-tuple-element.24, bf16[512,1024]{1,0:T(8,128)(2,1)S(1)} %bitcast.104), kind=kOutput, calls=%fused_computation | convolution fusion | flops 8596226048 | bytes 27262976 | tf_op jit(solution)/shard_map/dot_general | solution.py:25
  118.4 1.0 copy-done.2
  119.3 0.7 fusion.49
  121.1 14.9 %all-gather = f32[8,32,2]{1,2,0:T(2,128)S(1)} all-gather(f32[1,32,2]{1,2,0:T(2,128)S(1)} %bitcast.131), channel_id=1, replica_groups=mesh['row'=16,'col'=8,'chan'=2] {'col'}, dimensions={0}, use_global_device_ids=true | all-gather | bytes 2304 | tf_op jit(solution)/shard_map/all_gather | solution.py:47
  136.0 98.7 %reduce-scatter.11.cloned.1.call-done = f32[256,1024]{0,1:T(8,128)} async-done(((f32[4096,1024]{0,1:T(8,128)}), f32[256,1024]{0,1:T(8,128)}) %reduce-scatter.11.cloned.1.call-update) | async-done | bytes 1048592 | tf_op jit(solution)/shard_map/reduce_scatter | solution.py:24
  234.7 1.4 compare_select_fusion.1
  236.1 1.7 convolution_bitcast_fusion.3
  237.9 0.7 fusion.28
  238.5 0.6 dynamic-slice
  239.8 38.1 %all-reduce = f32[512]{0:T(512)S(1)} all-reduce(f32[512]{0:T(512)S(1)} %bitcast.128), channel_id=4, replica_groups=mesh['row'=16,'col'=8,'chan'=2] {'row'}, use_global_device_ids=true, to_apply=%region_2.0.clone | all-reduce | flops 512 | bytes 4096
  278.0 37.9 %reduce-scatter.13.cloned.1.call-done = f32[32,2]{1,0:T(8,128)} async-done(((f32[512,2]{1,0:T(8,128)}), f32[32,2]{1,0:T(8,128)}) %reduce-scatter.13.cloned.1.call-update) | async-done | bytes 272
  315.8 0.8 copy.32
  316.6 22.7 %all-gather.1 = f32[16,32,2]{1,2,0:T(2,128)S(1)} all-gather(f32[1,32,2]{1,2,0:T(2,128)S(1)} %divide_bitcast_fusion.1), channel_id=1, replica_groups=mesh['row'=16,'col'=8,'chan'=2] {'row'}, dimensions={0}, use_global_device_ids=true | all-gather | bytes 4352 | tf_op jit(solution)/shard_map/all_gather | solution.py:70
  339.4 25.7 %all_gather.27 = f32[2,4096]{1,0:T(2,128)S(1)} all-gather(f32[2,512]{1,0:T(2,128)S(1)} %bitcast.105), channel_id=1, replica_groups=mesh['row'=16,'col'=8,'chan'=2] {'col'}, dimensions={1}, use_global_device_ids=true | all-gather | bytes 36864 | tf_op jit(solution)/shard_map/all_gather | solution.py:71
  365.3 1.7 convolution_bitcast_fusion.2
  367.0 0.6 fusion.26
  367.6 38.1 %all-reduce.1 = f32[512]{0:T(512)S(1)} all-reduce(f32[512]{0:T(512)S(1)} %bitcast.130), channel_id=6, replica_groups=mesh['row'=16,'col'=8,'chan'=2] {'row'}, use_global_device_ids=true, to_apply=%region_4.0.clone | all-reduce | flops 512 | bytes 4096
  405.9 37.0 %reduce-scatter.15.cloned.1.call-done = f32[32,2]{1,0:T(8,128)} async-done(((f32[512,2]{1,0:T(8,128)}), f32[32,2]{1,0:T(8,128)}) %reduce-scatter.15.cloned.1.call-update) | async-done | bytes 272
  442.9 0.8 copy.34
  443.8 22.7 %all-gather.2 = f32[16,32,2]{1,2,0:T(2,128)S(1)} all-gather(f32[1,32,2]{1,2,0:T(2,128)S(1)} %multiply_bitcast_fusion), channel_id=1, replica_groups=mesh['row'=16,'col'=8,'chan'=2] {'row'}, dimensions={0}, use_global_device_ids=true | all-gather | bytes 4352 | tf_op jit(solution)/shard_map/all_gather | solution.py:70
  466.6 25.7 %all_gather.29 = f32[2,4096]{1,0:T(2,128)S(1)} all-gather(f32[2,512]{1,0:T(2,128)S(1)} %bitcast.106), channel_id=1, replica_groups=mesh['row'=16,'col'=8,'chan'=2] {'col'}, dimensions={1}, use_global_device_ids=true | all-gather | bytes 36864 | tf_op jit(solution)/shard_map/all_gather | solution.py:71
  492.4 1.7 convolution_bitcast_fusion.1
  494.1 0.6 fusion.24
  494.7 38.1 %all-reduce.2 = f32[512]{0:T(512)S(1)} all-reduce(f32[512]{0:T(512)S(1)} %bitcast.129), channel_id=8, replica_groups=mesh['row'=16,'col'=8,'chan'=2] {'row'}, use_global_device_ids=true, to_apply=%region_6.0.clone | all-reduce | flops 512 | bytes 4096
  532.9 37.1 %reduce-scatter.17.cloned.1.call-done = f32[32,2]{1,0:T(8,128)} async-done(((f32[512,2]{1,0:T(8,128)}), f32[32,2]{1,0:T(8,128)}) %reduce-scatter.17.cloned.1.call-update) | async-done | bytes 272
  570.0 0.8 copy.36
  570.8 22.7 %all-gather.3 = f32[16,32,2]{1,2,0:T(2,128)S(1)} all-gather(f32[1,32,2]{1,2,0:T(2,128)S(1)} %divide_bitcast_fusion), channel_id=1, replica_groups=mesh['row'=16,'col'=8,'chan'=2] {'row'}, dimensions={0}, use_global_device_ids=true | all-gather | bytes 4352 | tf_op jit(solution)/shard_map/all_gather | solution.py:70
  593.6 25.7 %all_gather.31 = f32[2,4096]{1,0:T(2,128)S(1)} all-gather(f32[2,512]{1,0:T(2,128)S(1)} %bitcast.107), channel_id=1, replica_groups=mesh['row'=16,'col'=8,'chan'=2] {'col'}, dimensions={1}, use_global_device_ids=true | all-gather | bytes 36864 | tf_op jit(solution)/shard_map/all_gather | solution.py:71
  619.3 0.6 constant_dynamic-slice_fusion.1
  (47 shorter events, 2.2 us)
Async XLA Ops:
  6.5 2.6 copy-start
  6.5 97.2 %all-gather.6.cloned.1.call-start = ((), (), s32[]{:S(2)}) async-start(), calls=%async_computation.4 | async-start | bytes 9437184 | tf_op jit(solution)/shard_map/all_gather | solution.py:23
  9.1 94.7 %copy-start.1 = (bf16[64,8,2,512]{3,1,2,0:T(8,128)(2,1)S(1)}, bf16[64,8,2,512]{3,1,2,0:T(8,128)(2,1)}, u32[]{:S(2)}) copy-start(bf16[64,8,2,512]{3,1,2,0:T(8,128)(2,1)} %copy.41) | copy-start | bytes 3145732
  9.1 225.6 %reduce-scatter.11.cloned.1.call-start = ((), (), s32[]{:S(2)}) async-start(), calls=%async_computation.5 | async-start | bytes 17825792 | tf_op jit(solution)/shard_map/reduce_scatter | solution.py:24
  118.3 1.0 copy-start.2
  118.3 2.7 copy-start.3
  118.3 197.5 %reduce-scatter.13.cloned.1.call-start = ((), (), s32[]{:S(2)}) async-start(), calls=%async_computation.6 | async-start | bytes 278528
  119.3 119.2 %copy-start.4 = (u32[256]{0:T(256)S(1)}, u32[256]{0:T(256)}, u32[]{:S(2)}) copy-start(u32[256]{0:T(256)} %constant.34) | copy-start | bytes 3076
  237.8 205.1 %reduce-scatter.15.cloned.1.call-start = ((), (), s32[]{:S(2)}) async-start(), calls=%async_computation.7 | async-start | bytes 278528
  367.0 203.0 %reduce-scatter.17.cloned.1.call-start = ((), (), s32[]{:S(2)}) async-start(), calls=%async_computation.8 | async-start | bytes 278528
Sparse Core Ops, SparseCore 0:
  9.2 94.5 all-gather.5
  118.4 116.2 reduce-scatter.10
  238.2 77.6 reduce-scatter.12
  367.1 75.7 reduce-scatter.14
  494.2 75.7 reduce-scatter.16
where the time goes:
time: 627 us; the launch traced here: 626 us
  waiting for transfers between devices  304 us (48%)
  blocking collectives  275 us (44%)
  matrix products  21.5 us (3%)
  between operations  13.9 us (2%)
  local copies, waits for them, and re-layouts  11 us (2%)
    unnamed x3, blocking collectives  114 us
    unnamed x8, waiting for transfers between devices  112 us
    reduce_scatter x1, waiting for transfers between devices, body(): lax.psum_scatter(lax.dot_general(all_antennas, right_side, contract_last,...  98.7 us
    all_gather x1, waiting for transfers between devices, body(): all_antennas = lax.all_gather(flattened, 'col', axis=0, tiled=True)  93 us
    all_gather x3, blocking collectives, body(): everything = lax.all_gather(gain_block, 'col', axis=1, tiled=True)  77.2 us
    all_gather x3, blocking collectives, body(): gain_block = lax.all_gather(updated, 'row', axis=1, tiled=True)  68.1 us
    all_gather x1, blocking collectives, body(): row_gains = lax.all_gather(initial_gains, 'col', axis=1, tiled=True)  14.9 us
    dot_general x1, matrix products, body(): lax.dot_general(all_antennas, right_side, contract_last, preferred_elemen...  14.5 us
  transfers between devices with their start and end apart: 5, of which 5 were waited for; matrix products, arithmetic and copies ran while one was open for 1% of the time, Pallas kernels for 0%

commit v1 on v0

v1 whole, which is shorter than its diff:
```python
import jax
import jax.numpy as jnp
from jax import lax
from jax.sharding import PartitionSpec as P


def vis_tiles(samples):
    block_column = samples.shape[0]
    flattened = samples.reshape(block_column, -1)
    rotated = jnp.concatenate([-samples[:, 1, :], samples[:, 0, :]], axis=1)
    right_side = jnp.concatenate([flattened, rotated], axis=0)
    all_antennas = lax.all_gather(flattened, "col", axis=0, tiled=True)
    vis_tile = lax.psum_scatter(
        lax.dot_general(
            all_antennas, right_side, (((1,), (1,)), ((), ())), preferred_element_type=jnp.float32
        ),
        "row",
        scatter_dimension=0,
        tiled=True,
    )
    return vis_tile[:, :block_column], vis_tile[:, block_column:]


def exchange(parts, axis):
    count = lax.axis_size(axis)
    copies = jnp.broadcast_to(parts[None], (count,) + parts.shape)
    return lax.all_to_all(copies, axis, 0, 0)


def columns_to_rows(weight_real, weight_imag, power, gain):
    real = gain[0][None, :]
    imag = gain[1][None, :]
    return jnp.stack(
        [
            jnp.sum(weight_real * real + weight_imag * imag, axis=1),
            jnp.sum(weight_real * imag - weight_imag * real, axis=1),
            jnp.sum(power * (real * real + imag * imag), axis=1),
        ]
    )


def rows_to_columns(weight_real, weight_imag, power, gain):
    real = gain[0][:, None]
    imag = gain[1][:, None]
    return jnp.stack(
        [
            jnp.sum(weight_real * real - weight_imag * imag, axis=0),
            jnp.sum(weight_real * imag + weight_imag * real, axis=0),
            jnp.sum(power * (real * real + imag * imag), axis=0),
        ]
    )


def body(samples, sky_model, initial_gains):
    row_count = lax.axis_size("row")
    column_count = lax.axis_size("col")
    row_index = lax.axis_index("row")
    column_index = lax.axis_index("col")
    block_column = samples.shape[0]
    block_row = sky_model.shape[0]
    share_size = initial_gains.shape[1]
    blocks = block_column // block_row
    everything = lax.all_gather(initial_gains, ("row", "col"), axis=1, tiled=True)
    gain = lax.dynamic_slice_in_dim(everything, column_index * block_column, block_column, 1)
    vis_real, vis_imag = vis_tiles(samples)
    model_real = sky_model[:, 0, :].astype(jnp.float32)
    model_imag = sky_model[:, 1, :].astype(jnp.float32)
    global_rows = row_index * block_row + lax.broadcasted_iota(
        jnp.int32, (block_row, block_column), 0
    )
    global_columns = column_index * block_column + lax.broadcasted_iota(
        jnp.int32, (block_row, block_column), 1
    )
    cross_mask = (global_rows != global_columns).astype(jnp.float32)
    weight_real = (vis_real * model_real + vis_imag * model_imag) * cross_mask
    weight_imag = (vis_real * model_imag - vis_imag * model_real) * cross_mask
    power = (model_real * model_real + model_imag * model_imag) * cross_mask

    parts = columns_to_rows(weight_real, weight_imag, power, gain)
    sums = jnp.sum(exchange(parts, "col"), axis=0)
    gain = sums[:2] / sums[2:]

    parts = rows_to_columns(weight_real, weight_imag, power, gain)
    message = jnp.concatenate([parts.reshape(-1), gain.reshape(-1)])
    message = message.reshape(-1, 128)
    received = exchange(message, "row").reshape(row_count, -1)
    sums = jnp.sum(received[:, : 3 * block_column], axis=0).reshape(3, block_column)
    previous = lax.dynamic_slice_in_dim(
        received[:, 3 * block_column :], column_index * blocks, blocks, 0
    )
    previous = previous.reshape(blocks, 2, block_row).transpose(1, 0, 2).reshape(2, block_column)
    gain = 0.5 * (sums[:2] / sums[2:] + previous)

    parts = columns_to_rows(weight_real, weight_imag, power, gain)
    shares = parts.reshape(3, column_count, share_size).transpose(1, 0, 2)
    sums = jnp.sum(lax.all_to_all(shares, "col", 0, 0), axis=0)
    return sums[:2] / sums[2:]


def solution(mesh):
    return jax.shard_map(
        body,
        mesh=mesh,
        in_specs=(
            P(("chan", "col"), None, "row"),
            P(("chan", "row"), None, "col"),
            P(None, ("chan", "row", "col")),
        ),
        out_specs=P(None, ("chan", "row", "col")),
        check_vma=False,
    )
```

time: 627 us -> 510 us (0.81)
  waiting for transfers between devices: 304 us -> 101 us
  blocking collectives: 275 us -> 364 us
  matrix products: 21.5 us -> 14.5 us
    all_gather x7 -> x1, blocking collectives: 160 us -> 339 us  [body(): lax.all_gather(initial_gains, ('row', 'col'), axis=1, tiled=True)]
    unnamed x3 -> x0, blocking collectives: 114 us -> none
    unnamed x8 -> x2, waiting for transfers between devices: 112 us -> 0.03 us
    reduce_scatter x1, waiting for transfers between devices: 98.7 us -> 0.02 us  [vis_tiles(): lax.psum_scatter(lax.dot_general(all_antennas, right_side, (((1,), (1,)),...]
    all_to_all x0 -> x2, blocking collectives: none -> 25.1 us  [the longest x1 14.8 us: exchange(): return lax.all_to_all(copies, axis, 0, 0)]
    all_to_all x0 -> x1, waiting for transfers between devices: none -> 7.95 us  [exchange(): return lax.all_to_all(copies, axis, 0, 0)]
    dot_general x4 -> x1, matrix products: 16.5 us -> 14.5 us  [vis_tiles(): lax.dot_general(all_antennas, right_side, (((1,), (1,)), ((), ())), prefe...]
  transfers between devices with their start and end apart: 5 -> 3, of which waited for: 5 -> 2; matrix products, arithmetic and copies ran while one was open for 1% -> 1% of each run, Pallas kernels for 0% -> 0%
where the time goes in v1:
time: 510 us; the launch traced here: 508 us
  blocking collectives  364 us (71%)
  waiting for transfers between devices  101 us (20%)
  matrix products  14.5 us (3%)
  between operations  13.7 us (3%)
  local copies, waits for them, and re-layouts  7.56 us (1%)
    all_gather x1, blocking collectives, body(): lax.all_gather(initial_gains, ('row', 'col'), axis=1, tiled=True)  339 us
    all_gather x1, waiting for transfers between devices, vis_tiles(): all_antennas = lax.all_gather(flattened, 'col', axis=0, tiled=True)  93 us
    all_to_all x1, blocking collectives, exchange(): return lax.all_to_all(copies, axis, 0, 0)  14.8 us
    dot_general x1, matrix products, vis_tiles(): lax.dot_general(all_antennas, right_side, (((1,), (1,)), ((), ())), prefe...  14.5 us
    all_to_all x1, blocking collectives, body(): sums = jnp.sum(lax.all_to_all(shares, 'col', 0, 0), axis=0)  10.3 us
  transfers between devices with their start and end apart: 3, of which 2 were waited for; matrix products, arithmetic and copies ran while one was open for 1% of the time, Pallas kernels for 0%

profile of v1, /device:TPU:64, one launch (start us, length us, event | category | flops | bytes accessed | tf_op | source)
XLA Modules:
  0.0 508.1 jit_solution(4030947531042781336)
XLA Ops:
  6.5 0.0 all-gather.3.cloned.1.call-start
  6.5 2.6 copy.35
  9.1 0.0 all-gather.3.cloned.1.call-update
  9.1 0.0 reduce-scatter.2.cloned.1.call-start
  9.2 0.0 copy-done
  9.2 1.5 fusion.11
  10.7 0.1 copy_bitcast_fusion
  10.8 93.0 %all-gather.3.cloned.1.call-done = bf16[4096,1024]{1,0:T(8,128)(2,1)} async-done(((bf16[512,1024]{1,0:T(8,128)(2,1)}), bf16[4096,1024]{1,0:T(8,128)(2,1)}) %all-gather.3.cloned.1.call-update) | async-done | bytes 8388624 | tf_op jit(solution)/shard_map/all_gather | solution.py:12
  103.8 14.5 %convolution_bitcast_fusion = f32[4096,1024]{0,1:T(8,128)} fusion(bf16[4096,1024]{1,0:T(8,128)(2,1)} %all-gather.3.cloned.1.call-done, bf16[512,512]{1,0:T(8,128)(2,1)S(1)} %get-tuple-element.26, bf16[512,512]{1,0:T(8,128)(2,1)S(1)} %get-tuple-element.27, bf16[512,1024]{1,0:T(8,128)(2,1)S(1)} %bitcast.75), kind=kOutput, calls=%fused_computation | convolution fusion | flops 8596226048 | bytes 27262976 | tf_op jit(solution)/shard_map/dot_general | solution.py:14
  118.3 0.0 reduce-scatter.2.cloned.1.call-update
  118.3 0.6 copy-done.3
  119.0 339.4 %all-gather = f32[128,32,2]{1,2,0:T(2,128)S(1)} all-gather(f32[1,32,2]{1,2,0:T(2,128)S(1)} %bitcast.99), channel_id=1, replica_groups=mesh['row'=16,'col'=8,'chan'=2] {'row','col'}, dimensions={0}, use_global_device_ids=true | all-gather | bytes 33024 | tf_op jit(solution)/shard_map/all_gather | solution.py:63
  458.3 0.1 reshape.71
  458.4 0.0 copy-done.2
  458.5 0.7 fusion.12
  459.2 0.5 copy.31
  459.7 0.5 copy.32
  460.2 0.0 reduce-scatter.2.cloned.1.call-done
  460.2 1.7 add_reduce_fusion.2
  461.9 14.8 %all_to_all.15 = f32[8,3,256]{2,1,0:T(4,128)S(1)} all-to-all(f32[8,3,256]{2,1,0:T(4,128)S(1)} %broadcast_in_dim.6), channel_id=1, replica_groups=mesh['row'=16,'col'=8,'chan'=2] {'col'}, dimensions={0} | all-to-all | bytes 49152 | tf_op jit(solution)/shard_map/all_to_all | solution.py:27
  476.8 0.2 multiply_reduce_fusion.1
  477.1 0.3 subtract_reduce_fusion.1
  477.4 0.6 broadcast_in_dim.15
  478.0 3.5 all-to-all-start.1
  481.5 8.0 %all-to-all-done.1 = f32[16,16,128]{2,1,0:T(8,128)S(1)} async-done(((f32[16,16,128]{2,1,0:T(8,128)}), f32[16,16,128]{2,1,0:T(8,128)S(1)}, u32[]{:S(2)}, u32[]{:S(2)}) %all-to-all-start.1) | async-done | bytes 131104 | tf_op jit(solution)/shard_map/all_to_all | solution.py:27
  489.7 0.2 add_reduce_fusion
  489.9 0.1 stack.44
  490.0 0.1 stack.45
  490.1 0.2 multiply_reduce_fusion
  490.3 0.1 stack.46
  490.4 10.3 %all_to_all.16 = f32[8,3,32]{2,1,0:T(4,128)S(1)} all-to-all(f32[8,3,32]{2,1,0:T(4,128)S(1)} %maximum_bitcast_fusion), channel_id=1, replica_groups=mesh['row'=16,'col'=8,'chan'=2] {'col'}, dimensions={0} | all-to-all | bytes 6144 | tf_op jit(solution)/shard_map/all_to_all | solution.py:96
  500.7 0.6 slice_divide_fusion.1
  (35 shorter events, 0.3 us)
Async XLA Ops:
  6.5 2.6 copy-start
  6.5 97.3 %all-gather.3.cloned.1.call-start = ((), (), s32[]{:S(2)}) async-start(), calls=%async_computation.4 | async-start | bytes 9437184 | tf_op jit(solution)/shard_map/all_gather | solution.py:12
  9.1 94.7 %copy-start.1 = (bf16[64,8,2,512]{3,1,2,0:T(8,128)(2,1)S(1)}, bf16[64,8,2,512]{3,1,2,0:T(8,128)(2,1)}, u32[]{:S(2)}) copy-start(bf16[64,8,2,512]{3,1,2,0:T(8,128)(2,1)} %copy.35) | copy-start | bytes 3145732
  9.1 451.1 %reduce-scatter.2.cloned.1.call-start = ((), (), s32[]{:S(2)}) async-start(), calls=%async_computation.5 | async-start | bytes 17825792 | tf_op jit(solution)/shard_map/reduce_scatter | solution.py:13
  118.3 0.7 copy-start.3
  118.3 340.2 %copy-start.2 = (bf16[256,2,512]{2,1,0:T(2,128)(2,1)S(1)}, bf16[256,2,512]{2,1,0:T(2,128)(2,1)}, u32[]{:S(2)}) copy-start(bf16[256,2,512]{2,1,0:T(2,128)(2,1)} %param.4) | copy-start | bytes 1572868
  478.0 11.5 %all-to-all-start.1 = ((f32[16,16,128]{2,1,0:T(8,128)}), f32[16,16,128]{2,1,0:T(8,128)S(1)}, u32[]{:S(2)}, u32[]{:S(2)}) async-start(f32[16,16,128]{2,1,0:T(8,128)} %broadcast_in_dim.15), calls=%async_computation.2 | async-start | bytes 262144 | tf_op jit(solution)/shard_map/all_to_all | solution.py:27
Sparse Core Ops, SparseCore 0:
  9.2 94.5 all-gather.2
  118.4 116.2 reduce-scatter.1

commit v2 on v1

--- a/solution.py
+++ b/solution.py
@@ -1,24 +1,254 @@
 import jax
 import jax.numpy as jnp
+import numpy as np
 from jax import lax
+from jax.experimental import pallas as pl
+from jax.experimental.pallas import tpu as pltpu
 from jax.sharding import PartitionSpec as P
 
 
-def vis_tiles(samples):
-    block_column = samples.shape[0]
-    flattened = samples.reshape(block_column, -1)
-    rotated = jnp.concatenate([-samples[:, 1, :], samples[:, 0, :]], axis=1)
-    right_side = jnp.concatenate([flattened, rotated], axis=0)
-    all_antennas = lax.all_gather(flattened, "col", axis=0, tiled=True)
-    vis_tile = lax.psum_scatter(
-        lax.dot_general(
-            all_antennas, right_side, (((1,), (1,)), ((), ())), preferred_element_type=jnp.float32
-        ),
-        "row",
-        scatter_dimension=0,
-        tiled=True,
-    )
-    return vis_tile[:, :block_column], vis_tile[:, block_column:]
+SIDE = 4
+PLANES = 8
+
+OFFSETS = {0: (0, 0), 1: (0, 1), 2: (-1, 1), 3: (-1, 2), 4: (-2, 2)}
+EARLY = [(d, h, k) for d in (1, 2) for h in (0, 1) for k in (0, 1)]
+LATE = [(3, h, k) for h in (0, 1) for k in (0, 1)] + [(4, 0, 0), (4, 1, 1), (0, 0, 0), (0, 0, 1)]
+PLACE = [
+    [7, 0, 2, 5, 13, 10, 8, 15, 14, 6, 3, 12, 11, 9, 1, 4],
+    [15, 10, 8, 2, 0, 7, 5, 13, 9, 4, 1, 14, 6, 11, 12, 3],
+    [13, 8, 5, 10, 2, 0, 7, 15, 11, 14, 3, 1, 12, 9, 6, 4],
+    [10, 13, 15, 2, 0, 8, 7, 5, 11, 4, 14, 9, 1, 12, 3, 6],
+    [15, 8, 13, 10, 2, 5, 7, 0, 11, 6, 4, 14, 3, 1, 12, 9],
+    [2, 10, 15, 0, 8, 5, 7, 13, 11, 12, 14, 9, 3, 1, 6, 4],
+    [15, 0, 2, 13, 5, 8, 10, 7, 9, 14, 3, 11, 6, 4, 1, 12],
+    [2, 5, 7, 10, 8, 0, 15, 13, 3, 12, 9, 1, 4, 6, 11, 14],
+]
+
+
+def targets(chunk, c):
+    d, h, k = chunk
+    a, b = [(c + offset) % PLANES for offset in OFFSETS[d]]
+    if d == 0 and k == 0:
+        return (2 * c, c, 0), (2 * c + 1, c, 1), 0
+    if d == 0:
+        return (2 * c + 1, c, 0), (2 * c, c, 1), 1
+    if d == 4:
+        k = h if c < PLANES // 2 else 1 - h
+    plain, mirror = (2 * a + h, b, k), (2 * b + k, a, h)
+    if d == 4 or h == k:
+        return plain, mirror, 0
+    return mirror, plain, 1
+
+
+def tables():
+    rows = SIDE * SIDE
+    devices = rows * PLANES
+    first, second = [], []
+    early = np.zeros((devices, 2, SIDE, 2), np.int32)
+    late = np.zeros((devices, 2, SIDE, 2), np.int32)
+    ahead = np.zeros((devices, 2, SIDE), np.int32)
+    flags = np.zeros((devices, 2), np.int32)
+    half = np.zeros(devices, np.int32)
+    for c in range(PLANES):
+        for chunk, r in zip(EARLY + LATE, PLACE[c]):
+            one, two, conjugated = targets(chunk, c)
+            first.append((r * PLANES + c, one[0] * PLANES + one[1]))
+            second.append((r * PLANES + c, two[0] * PLANES + two[1]))
+            flags[r * PLANES + c] = conjugated, chunk == (0, 0, 0)
+            half[one[0] * PLANES + one[1]] = one[2]
+        for i, owner in enumerate(PLACE[c]):
+            v, u = owner // SIDE, owner % SIDE
+            order, index = (early, i) if i < len(EARLY) else (late, i - len(EARLY))
+            for r in range(rows):
+                y, x = r // SIDE, r % SIDE
+                order[r * PLANES + c, 0, (u - x) % SIDE, v // 2] = index
+                order[r * PLANES + c, 1, (v - y) % SIDE, u // 2] = index
+        for r in range(rows):
+            y, x = r // SIDE, r % SIDE
+            for t in range(SIDE):
+                v, u = (y + t) % SIDE, (x + t) % SIDE
+                ahead[r * PLANES + c, 0, t] = (v + x) % 2 * 2 + v // 2
+                ahead[r * PLANES + c, 1, t] = (u + y) % 2 * 2 + u // 2
+    return first, second, early, late, ahead, flags, half
+
+
+def matmul(lhs, rhs):
+    return lax.dot_general(lhs, rhs, (((1,), (1,)), ((), ())), preferred_element_type=jnp.float32)
+
+
+def real_part(lhs, rhs):
+    return matmul(lhs, rhs)
+
+
+def imag_part(lhs, rhs):
+    times = lhs.shape[1] // 2
+    return matmul(lhs[:, times:], rhs[:, :times]) - matmul(lhs[:, :times], rhs[:, times:])
+
+
+def diagonal_kernel(here, out):
+    quarter = here.shape[0] // 2
+
+    @pl.loop(0, 3)
+    def _(i):
+        low = pl.ds(pl.multiple_of(jnp.where(i == 1, quarter, 0), quarter), quarter)
+        other = pl.ds(pl.multiple_of(jnp.where(i == 0, 0, quarter), quarter), quarter)
+        lhs, rhs = here[low, :], here[other, :]
+        out[2 * i] = real_part(lhs, rhs)
+        out[2 * i + 1] = imag_part(lhs, rhs)
+
+
+def stores(right, left, up, down, own):
+    return {
+        (0, 0): own.at[0],
+        (0, 1): own.at[1],
+        (1, 0): up,
+        (1, 1): right.at[1],
+        (2, 0): right.at[0],
+        (2, 1): left.at[0],
+        (3, 0): left.at[1],
+        (3, 1): down,
+    }
+
+
+ORDER = ((2, 0), (1, 1), (2, 1), (3, 0), (1, 0), (3, 1), (0, 0), (0, 1))
+
+
+def early_kernel(device, table, here, above, below, *outs):
+    quarter = here.shape[0] // 2
+    for t, j in ORDER:
+        for color, part in enumerate((real_part, imag_part)):
+            index = table[device[0] * 16 + color * 8 + t * 2 + j]
+            low = pl.ds(pl.multiple_of((index // 2 % 2) * quarter, quarter), quarter)
+            other = pl.ds(pl.multiple_of((index % 2) * quarter, quarter), quarter)
+            lhs = jnp.where(index < 4, here[low, :], below[low, :])
+            stores(*outs[5 * color : 5 * color + 5])[t, j][...] = part(lhs, above[other, :])
+
+
+def late_kernel(device, table, diagonal, below, above2, below2, *refs):
+    outs, found = refs[:-1], refs[-1]
+    quarter = below.shape[0] // 2
+    upper = (device[1] >= PLANES // 2).astype(jnp.int32)
+
+    @pl.loop(0, 2 * SIDE)
+    def _(place):
+        for color, part in enumerate((real_part, imag_part)):
+            index = table[device[0] * 16 + color * 8 + place]
+            out = found.at[color * 8 + place]
+
+            @pl.when(index < 6)
+            def _():
+                near = index < 4
+                h = jnp.where(near, index // 2, index - 4)
+                k = jnp.where(near, index % 2, (h + upper) % 2)
+                low = pl.ds(pl.multiple_of(h * quarter, quarter), quarter)
+                other = pl.ds(pl.multiple_of(k * quarter, quarter), quarter)
+                lhs = jnp.where(near, below[low, :], below2[low, :])
+                out[...] = part(lhs, above2[other, :])
+
+            @pl.when(index >= 6)
+            def _():
+                packed = diagonal[2 * color] + diagonal[2 * color + 1]
+                out[...] = jnp.where(index == 6, packed, diagonal[4 + color])
+
+    for color in range(2):
+        places = stores(*outs[5 * color : 5 * color + 5])
+        for t, j in ORDER:
+            places[t, j][...] = found[color * 8 + t * 2 + j]
+
+
+def finish_kernel(device, ahead, *refs):
+    ins, outs, sums = refs[:20], refs[20:30], refs[30]
+    quarter = sums.shape[-1]
+    half = quarter // 2
+    for color in range(2):
+        for group in range(2):
+            own, right, left, right2, left2 = ins[10 * color + 5 * group :][:5]
+            sums[2 * group] = own[0] + right2[...] + left[1]
+            sums[2 * group + 1] = own[1] + right[1] + left2[...]
+        right, left, up, down, own = outs[5 * color : 5 * color + 5]
+        entry = [sums.at[ahead[device[0] * 8 + color * 4 + t]] for t in range(SIDE)]
+        own[...] = entry[0][...]
+        up[...] = entry[1][:half, :]
+        right[1] = entry[1][half:, :]
+        right[0] = entry[2][:half, :]
+        left[0] = entry[2][half:, :]
+        left[1] = entry[3][:half, :]
+        down[...] = entry[3][half:, :]
+
+
+def mirror_kernel(device, flags, *refs):
+    total = []
+    for own, right, left, right2, left2 in (refs[:5], refs[5:10]):
+        half = right2.shape[0]
+        total.append(
+            jnp.concatenate(
+                [
+                    own[:half, :] + right2[...] + left[1],
+                    own[half:, :] + right[1] + left2[...],
+                ]
+            )
+        )
+    first, second = refs[10:]
+    p, q = total
+    pt, qt = p.T, q.T
+    flip = flags[device[0] * 2] == 1
+    diagonal = flags[device[0] * 2 + 1] == 1
+    first[0] = jnp.where(diagonal, 0.5 * (p + pt), jnp.where(flip, pt, p))
+    first[1] = jnp.where(diagonal, 0.5 * (p - pt), jnp.where(flip, -qt, q))
+    second[0] = jnp.where(diagonal, 0.5 * (q + qt), jnp.where(flip, p, pt))
+    second[1] = jnp.where(diagonal, 0.5 * (q - qt), jnp.where(flip, q, -qt))
+
+
+def kernel_call(kernel, scalars, blocks, shapes, flops=0, scratch=()):
+    shapes = [jax.ShapeDtypeStruct(shape, jnp.float32) for shape in shapes]
+    vmem = pl.BlockSpec(memory_space=pltpu.VMEM)
+    smem = pl.BlockSpec(memory_space=pltpu.SMEM)
+    moved = sum(v.size * v.dtype.itemsize for v in blocks) + sum(4 * v.size for v in shapes)
+    return pl.pallas_call(
+        kernel,
+        out_shape=shapes,
+        in_specs=[smem] * len(scalars) + [vmem] * len(blocks),
+        out_specs=[vmem] * len(shapes),
+        scratch_shapes=scratch,
+        cost_estimate=pl.CostEstimate(flops=flops, bytes_accessed=moved, transcendentals=0),
+    )(*scalars, *blocks)
+
+
+def message_shapes(rows, columns):
+    return [(2, rows, columns)] * 2 + [(rows, columns)] * 2
+
+
+def shift_x(value, step):
+    pairs = [
+        (y * SIDE + x, y * SIDE + (x + step) % SIDE) for y in range(SIDE) for x in range(SIDE)
+    ]
+    return lax.ppermute(value, "row", pairs)
+
+
+def shift_y(value, step):
+    pairs = [
+        (y * SIDE + x, (y + step) % SIDE * SIDE + x) for y in range(SIDE) for x in range(SIDE)
+    ]
+    return lax.ppermute(value, "row", pairs)
+
+
+def shift_z(value, step):
+    return lax.ppermute(value, "col", [(c, (c + step) % PLANES) for c in range(PLANES)])
+
+
+def ring_start(outs, shift):
+    right, left, up, down, own = outs
+    right, left = shift(right, 1), shift(left, -1)
+    return own, right, left, up + right[0], down + left[0]
+
+
+def ring_end(parts, shift):
+    own, right, left, up, down = parts
+    return own, right, left, shift(up, 1), shift(down, -1)
+
+
+def ring(outs, shift):
+    return ring_end(ring_start(outs, shift), shift)
 
 
 def exchange(parts, axis):
@@ -51,6 +281,77 @@
     )
 
 
+def vis_tiles(samples, gain):
+    row_index = lax.axis_index("row")
+    column_index = lax.axis_index("col")
+    first, second, early, late, ahead, flags, half = tables()
+    device_index = row_index * PLANES + column_index
+    device = jnp.stack([device_index, column_index]).astype(jnp.int32)
+    here = samples.reshape(samples.shape[0], -1)
+    antennas, times = here.shape
+    quarter = antennas // 2
+    product = 2 * quarter * quarter * times
+    above, below = shift_z(here, -1), shift_z(here, 1)
+    gain, free = lax.optimization_barrier((gain, here))
+    (diagonal,) = kernel_call(diagonal_kernel, (), (free,), [(6, quarter, quarter)], 6 * product)
+    above, below, diagonal = lax.optimization_barrier((above, below, diagonal))
+    above2, below2 = shift_z(above, -1), shift_z(below, 1)
+    shapes = 2 * (message_shapes(quarter, quarter) + [(2, quarter, quarter)])
+    outs = kernel_call(
+        early_kernel,
+        (device, jnp.asarray(early.reshape(-1))),
+        (here, above, below),
+        shapes,
+        16 * product,
+    )
+    along_x, along_y = ring_start(outs[:5], shift_x), ring_start(outs[5:], shift_y)
+    sums = along_x[3:] + along_y[3:]
+    *_, above2, below2 = lax.optimization_barrier((*sums, above2, below2))
+    early_parts = ring_end(along_x, shift_x), ring_end(along_y, shift_y)
+    outs = kernel_call(
+        late_kernel,
+        (device, jnp.asarray(late.reshape(-1))),
+        (diagonal, below, above2, below2),
+        shapes,
+        12 * product,
+        scratch=(pltpu.VMEM((16, quarter, quarter), jnp.float32),),
+    )
+    late_parts = ring(outs[:5], shift_x), ring(outs[5:], shift_y)
+    outs = kernel_call(
+        finish_kernel,
+        (device, jnp.asarray(ahead.reshape(-1))),
+        early_parts[0] + late_parts[0] + early_parts[1] + late_parts[1],
+        2 * (message_shapes(quarter // 2, quarter) + [(quarter, quarter)]),
+        scratch=(pltpu.VMEM((4, quarter, quarter), jnp.float32),),
+    )
+    parts = ring(outs[:5], shift_y) + ring(outs[5:], shift_x)
+    one, two = kernel_call(
+        mirror_kernel,
+        (device, jnp.asarray(flags.reshape(-1))),
+        parts,
+        [(2, quarter, quarter)] * 2,
+    )
+    one = lax.ppermute(one, ("row", "col"), first)
+    two = lax.ppermute(two, ("row", "col"), second)
+    one_is_right = jnp.asarray(half)[device_index] == 1
+    left = jnp.where(one_is_right, two, one)
+    right = jnp.where(one_is_right, one, two)
+    real = jnp.concatenate([left[0], right[0]], axis=1)
+    imag = jnp.concatenate([left[1], right[1]], axis=1)
+    return real, imag, gain
+
+
+def starting_gains(initial_gains):
+    blocks = SIDE * SIDE // PLANES
+    pairs = [
+        (r * PLANES + c, (r % blocks * PLANES + c) * PLANES + r // blocks)
+        for r in range(SIDE * SIDE)
+        for c in range(PLANES)
+    ]
+    share = lax.ppermute(initial_gains, ("row", "col"), pairs)
+    return exchange(share, "row").transpose(1, 0, 2).reshape(2, -1)
+
+
 def body(samples, sky_model, initial_gains):
     row_count = lax.axis_size("row")
     column_count = lax.axis_size("col")
@@ -60,9 +361,8 @@
     block_row = sky_model.shape[0]
     share_size = initial_gains.shape[1]
     blocks = block_column // block_row
-    everything = lax.all_gather(initial_gains, ("row", "col"), axis=1, tiled=True)
-    gain = lax.dynamic_slice_in_dim(everything, column_index * block_column, block_column, 1)
-    vis_real, vis_imag = vis_tiles(samples)
+    gain = starting_gains(initial_gains)
+    vis_real, vis_imag, gain = vis_tiles(samples, gain)
     model_real = sky_model[:, 0, :].astype(jnp.float32)
     model_imag = sky_model[:, 1, :].astype(jnp.float32)
     global_rows = row_index * block_row + lax.broadcasted_iota(

time: 510 us -> 232 us (0.45)
  blocking collectives: 364 us -> 25.3 us
  starting transfers between devices: 3.55 us -> 70.3 us
  Pallas kernels: 0 us -> 26.4 us
  waiting for transfers between devices: 101 us -> 85.9 us
  matrix products: 14.5 us -> 0 us
  between operations: 13.7 us -> 1.2 us
  other arithmetic: 3.47 us -> 12.1 us
    all_gather x1 -> x0, blocking collectives: 339 us -> none  [body(): lax.all_gather(initial_gains, ('row', 'col'), axis=1, tiled=True)]
    all_gather x1 -> x0, waiting for transfers between devices: 93 us -> none  [vis_tiles(): all_antennas = lax.all_gather(flattened, 'col', axis=0, tiled=True)]
    ppermute x0 -> x31, waiting for transfers between devices: none -> 70.9 us  [the longest x12 24.6 us: shift_y(): return lax.ppermute(value, 'row', pairs)]
    ppermute x0 -> x31, starting transfers between devices: none -> 55.3 us  [the longest x12 19.2 us: shift_y(): return lax.ppermute(value, 'row', pairs)]
    pallas_call x0 -> x5, Pallas kernels: none -> 26.4 us  [kernel_call(): pl.pallas_call(kernel, out_shape=shapes, in_specs=[smem] * len(scalars) +...]
    dot_general x1 -> x0, matrix products: 14.5 us -> none  [vis_tiles(): lax.dot_general(all_antennas, right_side, (((1,), (1,)), ((), ())), prefe...]
    all_to_all x1 -> x2, starting transfers between devices: 3.51 us -> 14.9 us  [exchange(): return lax.all_to_all(copies, axis, 0, 0)]
    add x0 -> x12, other arithmetic: none -> 9.04 us  [ring_start(): return (own, right, left, up + right[0], down + left[0])]
  transfers between devices with their start and end apart: 3 -> 33, of which waited for: 2 -> 16; matrix products, arithmetic and copies ran while one was open for 1% -> 5% of each run, Pallas kernels for 0% -> 2%
where the time goes in v2:
time: 232 us; the launch traced here: 229 us
  waiting for transfers between devices  85.9 us (37%)
  starting transfers between devices  70.3 us (30%)
  Pallas kernels  26.4 us (11%)
  blocking collectives  25.3 us (11%)
  other arithmetic  12.1 us (5%)
  local copies, waits for them, and re-layouts  7.96 us (3%)
    pallas_call x5, Pallas kernels, kernel_call(): pl.pallas_call(kernel, out_shape=shapes, in_specs=[smem] * len(scalars) +...  26.4 us
    ppermute x12, waiting for transfers between devices, shift_y(): return lax.ppermute(value, 'row', pairs)  24.6 us
    ppermute x1, waiting for transfers between devices, starting_gains(): share = lax.ppermute(initial_gains, ('row', 'col'), pairs)  19.5 us
    ppermute x12, starting transfers between devices, shift_y(): return lax.ppermute(value, 'row', pairs)  19.2 us
    ppermute x12, waiting for transfers between devices, shift_x(): return lax.ppermute(value, 'row', pairs)  15.5 us
    all_to_all x1, blocking collectives, exchange(): return lax.all_to_all(copies, axis, 0, 0)  15 us
    all_to_all x2, waiting for transfers between devices, exchange(): return lax.all_to_all(copies, axis, 0, 0)  15 us
    all_to_all x2, starting transfers between devices, exchange(): return lax.all_to_all(copies, axis, 0, 0)  14.9 us
  transfers between devices with their start and end apart: 33, of which 16 were waited for; matrix products, arithmetic and copies ran while one was open for 5% of the time, Pallas kernels for 2%

profile of v2, /device:TPU:64, one launch (start us, length us, event | category | flops | bytes accessed | tf_op | source)
XLA Modules:
  0.0 229.1 jit_solution(7207204341434293852)
XLA Ops:
  1.7 1.9 collective-permute-start.1
  3.6 7.8 %collective-permute-start.2 = (f32[2,32]{1,0:T(2,128)S(1)}, f32[2,32]{1,0:T(2,128)S(1)}, u32[]{:S(2)}, u32[]{:S(2)}) collective-permute-start(f32[2,32]{1,0:T(2,128)S(1)} %copy-done.32), channel_id=1, source_target_pairs={{0,0},{2,16},{4,32},{6,48},{8,64},{10,80},{12,96},{14,112},{16,128... | collective-permute-start | bytes 776 | tf_op jit(solution)/shard_map/ppermute | solution.py:351
  11.5 19.5 %collective-permute-done.2 = f32[2,32]{1,0:T(2,128)S(1)} collective-permute-done((f32[2,32]{1,0:T(2,128)S(1)}, f32[2,32]{1,0:T(2,128)S(1)}, u32[]{:S(2)}, u32[]{:S(2)}) %collective-permute-start.2) | collective-permute-done | bytes 288 | tf_op jit(solution)/shard_map/ppermute | solution.py:351
  31.6 9.5 %all-to-all-start = ((f32[16,2,32]{2,1,0:T(2,128)}), f32[16,2,32]{2,1,0:T(2,128)S(1)}, u32[]{:S(2)}, u32[]{:S(2)}) async-start(f32[16,2,32]{2,1,0:T(2,128)} %broadcast_in_dim.8), calls=%async_computation | async-start | bytes 32768 | tf_op jit(solution)/shard_map/all_to_all | solution.py:257
  41.7 7.0 %all-to-all-done = f32[16,2,32]{2,1,0:T(2,128)S(1)} async-done(((f32[16,2,32]{2,1,0:T(2,128)}), f32[16,2,32]{2,1,0:T(2,128)S(1)}, u32[]{:S(2)}, u32[]{:S(2)}) %all-to-all-start) | async-done | bytes 4128 | tf_op jit(solution)/shard_map/all_to_all | solution.py:257
  48.8 3.8 %shard_map.82.diagonal = f32[6,256,256]{2,1,0:T(8,128)} custom-call(bf16[512,1024]{1,0:T(8,128)(2,1)} %bitcast.104), custom_call_target="tpu_custom_call" | custom-call | flops 805306368 | bytes 2621440 | tf_op jit(solution)/shard_map/pallas_call | solution.py:207
  53.6 5.8 %shard_map.83 = (f32[2,256,256]{2,1,0:T(8,128)}, f32[2,256,256]{2,1,0:T(8,128)}, f32[256,256]{1,0:T(8,128)}, f32[256,256]{1,0:T(8,128)}, f32[2,256,256]{2,1,0:T(...) custom-call(s32[2]{0:T(128)} %pad_add_fusion.device, ...), custom_call_target="tpu_custom_call" | custom-call | flops 2147483648 | bytes 7340032 | tf_op jit(solution)/shard_map/pallas_call | solution.py:207
  61.5 2.0 collective-permute-start.9
  64.7 5.7 %collective-permute-done.8.refs_12_ = f32[2,256,256]{2,1,0:T(8,128)S(1)} collective-permute-done((f32[2,256,256]{2,1,0:T(8,128)}, f32[2,256,256]{2,1,0:T(8,128)S(1)}, u32[]{:S(2)}, u32[]{:S(2)}) %collective-permute-start.8) | collective-permute-done | bytes 524320 | tf_op jit(solution)/shard_map/ppermute | solution.py:232
  71.0 1.7 fusion.7
  73.9 8.0 %collective-permute-done.3.refs_1_ = f32[2,256,256]{2,1,0:T(8,128)S(1)} collective-permute-done((f32[2,256,256]{2,1,0:T(8,128)}, f32[2,256,256]{2,1,0:T(8,128)S(1)}, u32[]{:S(2)}, u32[]{:S(2)}) %collective-permute-start.3) | collective-permute-done | bytes 524320 | tf_op jit(solution)/shard_map/ppermute | solution.py:225
  84.2 9.1 %shard_map.84 = (f32[2,256,256]{2,1,0:T(8,128)}, f32[2,256,256]{2,1,0:T(8,128)}, f32[256,256]{1,0:T(8,128)}, f32[256,256]{1,0:T(8,128)}, f32[2,256,256]{2,1,0:T(...) custom-call(s32[2]{0:T(128)} %pad_add_fusion.device, ...), custom_call_target="tpu_custom_call" | custom-call | flops 1610612736 | bytes 8912896 | tf_op jit(solution)/shard_map/pallas_call | solution.py:207
  93.3 2.5 %collective-permute-start.18 = (f32[2,256,256]{2,1,0:T(8,128)}, f32[2,256,256]{2,1,0:T(8,128)S(1)}, u32[]{:S(2)}, u32[]{:S(2)}) collective-permute-start(f32[2,256,256]{2,1,0:T(8,128)} %get-tuple-element.67), channel_id=1, source_target_pairs={{0,192},{16,208},{32,224},{48,240},{64,0},{80,16},{96,32},{112,48}... | collective-permute-start | bytes 1572872 | tf_op jit(solution)/shard_map/ppermute | solution.py:232
  97.0 3.2 %collective-permute-start.16 = (f32[256,256]{1,0:T(8,128)}, f32[256,256]{1,0:T(8,128)S(1)}, u32[]{:S(2)}, u32[]{:S(2)}) collective-permute-start(f32[256,256]{1,0:T(8,128)} %fusion.7), channel_id=1, source_target_pairs={{0,192},{16,208},{32,224},{48,240},{64,0},{80,16},{96,32},{112,48}... | collective-permute-start | bytes 786440 | tf_op jit(solution)/shard_map/ppermute | solution.py:232
  100.2 5.7 %collective-permute-done.18.refs_17_ = f32[2,256,256]{2,1,0:T(8,128)S(1)} collective-permute-done((f32[2,256,256]{2,1,0:T(8,128)}, f32[2,256,256]{2,1,0:T(8,128)S(1)}, u32[]{:S(2)}, u32[]{:S(2)}) %collective-permute-start.18) | collective-permute-done | bytes 524320 | tf_op jit(solution)/shard_map/ppermute | solution.py:232
  107.6 1.6 collective-permute-done.17.refs_16_
  112.4 5.5 %collective-permute-done.11.refs_6_ = f32[2,256,256]{2,1,0:T(8,128)S(1)} collective-permute-done((f32[2,256,256]{2,1,0:T(8,128)}, f32[2,256,256]{2,1,0:T(8,128)S(1)}, u32[]{:S(2)}, u32[]{:S(2)}) %collective-permute-start.11) | collective-permute-done | bytes 524320 | tf_op jit(solution)/shard_map/ppermute | solution.py:225
  117.9 4.3 %collective-permute-start.20 = (f32[256,256]{1,0:T(8,128)S(1)}, f32[256,256]{1,0:T(8,128)S(1)}, u32[]{:S(2)}, u32[]{:S(2)}) collective-permute-start(f32[256,256]{1,0:T(8,128)S(1)} %fusion.3), channel_id=1, source_target_pairs={{0,192},{16,208},{32,224},{48,240},{64,0},{80,16},{96,32},{112,48}... | collective-permute-start | bytes 786440 | tf_op jit(solution)/shard_map/ppermute | solution.py:232
  126.1 3.8 %collective-permute-done.19.refs_18_ = f32[256,256]{1,0:T(8,128)S(1)} collective-permute-done((f32[256,256]{1,0:T(8,128)S(1)}, f32[256,256]{1,0:T(8,128)S(1)}, u32[]{:S(2)}, u32[]{:S(2)}) %collective-permute-start.19) | collective-permute-done | bytes 262176 | tf_op jit(solution)/shard_map/ppermute | solution.py:232
  131.5 4.9 %shard_map.85 = (f32[2,128,256]{2,1,0:T(8,128)}, f32[2,128,256]{2,1,0:T(8,128)}, f32[128,256]{1,0:T(8,128)}, f32[128,256]{1,0:T(8,128)}, f32[256,256]{1,0:T(8,12...) custom-call(s32[2]{0:T(128)} %pad_add_fusion.device, ...), custom_call_target="tpu_custom_call" | custom-call | bytes 10485760 | tf_op jit(solution)/shard_map/pallas_call | solution.py:207
  136.5 2.0 collective-permute-start.25
  138.5 3.4 %collective-permute-start.22 = (f32[2,128,256]{2,1,0:T(8,128)}, f32[2,128,256]{2,1,0:T(8,128)S(1)}, u32[]{:S(2)}, u32[]{:S(2)}) collective-permute-start(f32[2,128,256]{2,1,0:T(8,128)} %get-tuple-element.72), channel_id=1, source_target_pairs={{0,192},{16,208},{32,224},{48,240},{64,0},{80,16},{96,32},{112,48}... | collective-permute-start | bytes 786440 | tf_op jit(solution)/shard_map/ppermute | solution.py:232
  148.6 3.5 %collective-permute-start.24 = (f32[128,256]{1,0:T(8,128)S(1)}, f32[128,256]{1,0:T(8,128)S(1)}, u32[]{:S(2)}, u32[]{:S(2)}) collective-permute-start(f32[128,256]{1,0:T(8,128)S(1)} %fusion.13), channel_id=1, source_target_pairs={{0,192},{16,208},{32,224},{48,240},{64,0},{80,16},{96,32},{112,48}... | collective-permute-start | bytes 393224 | tf_op jit(solution)/shard_map/ppermute | solution.py:232
  154.6 4.8 %collective-permute-done.23.refs_3_ = f32[128,256]{1,0:T(8,128)S(1)} collective-permute-done((f32[128,256]{1,0:T(8,128)S(1)}, f32[128,256]{1,0:T(8,128)S(1)}, u32[]{:S(2)}, u32[]{:S(2)}) %collective-permute-start.23) | collective-permute-done | bytes 131104 | tf_op jit(solution)/shard_map/ppermute | solution.py:232
  160.0 2.8 %shard_map.86 = (f32[2,256,256]{2,1,0:T(8,128)}, f32[2,256,256]{2,1,0:T(8,128)}) custom-call(s32[2]{0:T(128)} %pad_add_fusion.device, s32[256]{0:T(256)} %constant.48.clone.flags, f32[256,256]{1,0:T(8,128)} %get-tuple-element.70.refs_0_, f32[2,128,256]{2,1,0:T(8,128)} %copy-done.13, f32[2,128,256]{2,1,0:T(8,128)} %copy-done.12, f32[128,256]{1,0:T(8,128)} %copy-done.29, ...), custom_call_target="tpu_custom_call" | custom-call | bytes 3145728 | tf_op jit(solution)/shard_map/pallas_call | solution.py:207
  162.8 9.9 %collective-permute-start.29 = (f32[2,256,256]{2,1,0:T(8,128)}, f32[2,256,256]{2,1,0:T(8,128)S(1)}, u32[]{:S(2)}, u32[]{:S(2)}) collective-permute-start(f32[2,256,256]{2,1,0:T(8,128)} %get-tuple-element.80), channel_id=1, source_target_pairs={{112,32},{0,2},{32,18},{80,48},{208,46},{160,226},{128,242},{240,6... | collective-permute-start | bytes 1572872 | tf_op jit(solution)/shard_map/ppermute | solution.py:335
  172.7 1.9 collective-permute-start.30
  176.6 10.1 %collective-permute-done.29 = f32[2,256,256]{2,1,0:T(8,128)S(1)} collective-permute-done((f32[2,256,256]{2,1,0:T(8,128)}, f32[2,256,256]{2,1,0:T(8,128)S(1)}, u32[]{:S(2)}, u32[]{:S(2)}) %collective-permute-start.29) | collective-permute-done | bytes 524320 | tf_op jit(solution)/shard_map/ppermute | solution.py:335
  187.6 15.0 %all_to_all.20 = f32[8,3,256]{2,1,0:T(4,128)S(1)} all-to-all(f32[8,3,256]{2,1,0:T(4,128)S(1)} %broadcast_in_dim.9), channel_id=1, replica_groups=mesh['row'=16,'col'=8,'chan'=2] {'col'}, dimensions={0} | all-to-all | bytes 49152 | tf_op jit(solution)/shard_map/all_to_all | solution.py:257
  203.8 5.4 %all-to-all-start.2 = ((f32[16,16,128]{2,1,0:T(8,128)}), f32[16,16,128]{2,1,0:T(8,128)S(1)}, u32[]{:S(2)}, u32[]{:S(2)}) async-start(f32[16,16,128]{2,1,0:T(8,128)} %broadcast_in_dim.22), calls=%async_computation.2 | async-start | bytes 262144 | tf_op jit(solution)/shard_map/all_to_all | solution.py:257
  209.2 8.0 %all-to-all-done.2 = f32[16,16,128]{2,1,0:T(8,128)S(1)} async-done(((f32[16,16,128]{2,1,0:T(8,128)}), f32[16,16,128]{2,1,0:T(8,128)S(1)}, u32[]{:S(2)}, u32[]{:S(2)}) %all-to-all-start.2) | async-done | bytes 131104 | tf_op jit(solution)/shard_map/all_to_all | solution.py:257
  218.2 10.3 %all_to_all.21 = f32[8,3,32]{2,1,0:T(4,128)S(1)} all-to-all(f32[8,3,32]{2,1,0:T(4,128)S(1)} %maximum_bitcast_fusion), channel_id=1, replica_groups=mesh['row'=16,'col'=8,'chan'=2] {'col'}, dimensions={0} | all-to-all | bytes 6144 | tf_op jit(solution)/shard_map/all_to_all | solution.py:396
  (169 shorter events, 37.4 us)
Async XLA Ops:
  1.5 51.1 %collective-permute-start = (bf16[512,1024]{1,0:T(8,128)(2,1)S(1)}, bf16[512,1024]{1,0:T(8,128)(2,1)}, u32[]{:S(2)}, u32[]{:S(2)}) collective-permute-start(bf16[512,1024]{1,0:T(8,128)(2,1)S(1)} %bitcast.102), channel_id=1, source_target_pairs={{0,14},{2,0},{4,2},{6,4},{8,6},{10,8},{12,10},{14,12},{1,15},{3,1}... | collective-permute-start | bytes 3145736 | tf_op jit(solution)/shard_map/ppermute | solution.py:236
  1.7 50.9 %collective-permute-start.1 = (bf16[512,1024]{1,0:T(8,128)(2,1)S(1)}, bf16[512,1024]{1,0:T(8,128)(2,1)S(1)}, u32[]{:S(2)}, u32[]{:S(2)}) collective-permute-start(bf16[512,1024]{1,0:T(8,128)(2,1)S(1)} %bitcast.103), channel_id=1, source_target_pairs={{0,2},{2,4},{4,6},{6,8},{8,10},{10,12},{12,14},{14,0},{1,3},{3,5},... | collective-permute-start | bytes 3145736 | tf_op jit(solution)/shard_map/ppermute | solution.py:236
  3.6 27.4 %collective-permute-start.2 = (f32[2,32]{1,0:T(2,128)S(1)}, f32[2,32]{1,0:T(2,128)S(1)}, u32[]{:S(2)}, u32[]{:S(2)}) collective-permute-start(f32[2,32]{1,0:T(2,128)S(1)} %copy-done.32), channel_id=1, source_target_pairs={{0,0},{2,16},{4,32},{6,48},{8,64},{10,80},{12,96},{14,112},{16,128... | collective-permute-start | bytes 776 | tf_op jit(solution)/shard_map/ppermute | solution.py:351
  31.6 17.1 %all-to-all-start = ((f32[16,2,32]{2,1,0:T(2,128)}), f32[16,2,32]{2,1,0:T(2,128)S(1)}, u32[]{:S(2)}, u32[]{:S(2)}) async-start(f32[16,2,32]{2,1,0:T(2,128)} %broadcast_in_dim.8), calls=%async_computation | async-start | bytes 32768 | tf_op jit(solution)/shard_map/all_to_all | solution.py:257
  59.4 11.1 %collective-permute-start.8 = (f32[2,256,256]{2,1,0:T(8,128)}, f32[2,256,256]{2,1,0:T(8,128)S(1)}, u32[]{:S(2)}, u32[]{:S(2)}) collective-permute-start(f32[2,256,256]{2,1,0:T(8,128)} %get-tuple-element.56), channel_id=1, source_target_pairs={{0,192},{16,208},{32,224},{48,240},{64,0},{80,16},{96,32},{112,48}... | collective-permute-start | bytes 1572872 | tf_op jit(solution)/shard_map/ppermute | solution.py:232
  60.6 12.1 %collective-permute-start.7 = (f32[2,256,256]{2,1,0:T(8,128)}, f32[2,256,256]{2,1,0:T(8,128)S(1)}, u32[]{:S(2)}, u32[]{:S(2)}) collective-permute-start(f32[2,256,256]{2,1,0:T(8,128)} %get-tuple-element.54), channel_id=1, source_target_pairs={{0,64},{16,80},{32,96},{48,112},{64,128},{80,144},{96,160},{112,17... | collective-permute-start | bytes 1572872 | tf_op jit(solution)/shard_map/ppermute | solution.py:232
  61.5 21.7 %collective-permute-start.10 = (bf16[512,1024]{1,0:T(8,128)(2,1)}, bf16[512,1024]{1,0:T(8,128)(2,1)S(1)}, u32[]{:S(2)}, u32[]{:S(2)}) collective-permute-start(bf16[512,1024]{1,0:T(8,128)(2,1)} %copy-done.30), channel_id=1, source_target_pairs={{0,2},{2,4},{4,6},{6,8},{8,10},{10,12},{12,14},{14,0},{1,3},{3,5},... | collective-permute-start | bytes 3145736 | tf_op jit(solution)/shard_map/ppermute | solution.py:236
  61.5 22.7 %collective-permute-start.9 = (bf16[512,1024]{1,0:T(8,128)(2,1)}, bf16[512,1024]{1,0:T(8,128)(2,1)}, u32[]{:S(2)}, u32[]{:S(2)}) collective-permute-start(bf16[512,1024]{1,0:T(8,128)(2,1)} %collective-permute-done.above), channel_id=1, source_target_pairs={{0,14},{2,0},{4,2},{6,4},{8,6},{10,8},{12,10},{14,12},{1,15},{3,1}... | collective-permute-start | bytes 3145736 | tf_op jit(solution)/shard_map/ppermute | solution.py:236
  63.5 10.4 %collective-permute-start.4 = (f32[2,256,256]{2,1,0:T(8,128)}, f32[2,256,256]{2,1,0:T(8,128)S(1)}, u32[]{:S(2)}, u32[]{:S(2)}) collective-permute-start(f32[2,256,256]{2,1,0:T(8,128)} %get-tuple-element.49), channel_id=1, source_target_pairs={{0,48},{16,0},{32,16},{48,32},{64,112},{80,64},{96,80},{112,96},{1... | collective-permute-start | bytes 1572872 | tf_op jit(solution)/shard_map/ppermute | solution.py:225
  70.5 11.5 %collective-permute-start.3 = (f32[2,256,256]{2,1,0:T(8,128)}, f32[2,256,256]{2,1,0:T(8,128)S(1)}, u32[]{:S(2)}, u32[]{:S(2)}) collective-permute-start(f32[2,256,256]{2,1,0:T(8,128)} %get-tuple-element.48), channel_id=1, source_target_pairs={{0,16},{16,32},{32,48},{48,0},{64,80},{80,96},{96,112},{112,64},{1... | collective-permute-start | bytes 1572872 | tf_op jit(solution)/shard_map/ppermute | solution.py:225
  93.3 12.6 %collective-permute-start.18 = (f32[2,256,256]{2,1,0:T(8,128)}, f32[2,256,256]{2,1,0:T(8,128)S(1)}, u32[]{:S(2)}, u32[]{:S(2)}) collective-permute-start(f32[2,256,256]{2,1,0:T(8,128)} %get-tuple-element.67), channel_id=1, source_target_pairs={{0,192},{16,208},{32,224},{48,240},{64,0},{80,16},{96,32},{112,48}... | collective-permute-start | bytes 1572872 | tf_op jit(solution)/shard_map/ppermute | solution.py:232
  95.8 13.4 %collective-permute-start.17 = (f32[2,256,256]{2,1,0:T(8,128)}, f32[2,256,256]{2,1,0:T(8,128)S(1)}, u32[]{:S(2)}, u32[]{:S(2)}) collective-permute-start(f32[2,256,256]{2,1,0:T(8,128)} %get-tuple-element.66), channel_id=1, source_target_pairs={{0,64},{16,80},{32,96},{48,112},{64,128},{80,144},{96,160},{112,17... | collective-permute-start | bytes 1572872 | tf_op jit(solution)/shard_map/ppermute | solution.py:232
  95.8 15.6 %collective-permute-start.12 = (f32[2,256,256]{2,1,0:T(8,128)}, f32[2,256,256]{2,1,0:T(8,128)S(1)}, u32[]{:S(2)}, u32[]{:S(2)}) collective-permute-start(f32[2,256,256]{2,1,0:T(8,128)} %get-tuple-element.61), channel_id=1, source_target_pairs={{0,48},{16,0},{32,16},{48,32},{64,112},{80,64},{96,80},{112,96},{1... | collective-permute-start | bytes 1572872 | tf_op jit(solution)/shard_map/ppermute | solution.py:225
  97.0 25.3 %collective-permute-start.16 = (f32[256,256]{1,0:T(8,128)}, f32[256,256]{1,0:T(8,128)S(1)}, u32[]{:S(2)}, u32[]{:S(2)}) collective-permute-start(f32[256,256]{1,0:T(8,128)} %fusion.7), channel_id=1, source_target_pairs={{0,192},{16,208},{32,224},{48,240},{64,0},{80,16},{96,32},{112,48}... | collective-permute-start | bytes 786440 | tf_op jit(solution)/shard_map/ppermute | solution.py:232
  100.2 22.2 %collective-permute-start.15 = (f32[256,256]{1,0:T(8,128)S(1)}, f32[256,256]{1,0:T(8,128)S(1)}, u32[]{:S(2)}, u32[]{:S(2)}) collective-permute-start(f32[256,256]{1,0:T(8,128)S(1)} %fusion.8), channel_id=1, source_target_pairs={{0,64},{16,80},{32,96},{48,112},{64,128},{80,144},{96,160},{112,17... | collective-permute-start | bytes 786440 | tf_op jit(solution)/shard_map/ppermute | solution.py:232
  105.9 12.0 %collective-permute-start.11 = (f32[2,256,256]{2,1,0:T(8,128)}, f32[2,256,256]{2,1,0:T(8,128)S(1)}, u32[]{:S(2)}, u32[]{:S(2)}) collective-permute-start(f32[2,256,256]{2,1,0:T(8,128)} %get-tuple-element.60), channel_id=1, source_target_pairs={{0,16},{16,32},{32,48},{48,0},{64,80},{80,96},{96,112},{112,64},{1... | collective-permute-start | bytes 1572872 | tf_op jit(solution)/shard_map/ppermute | solution.py:225
  109.2 13.9 %collective-permute-start.6 = (f32[256,256]{1,0:T(8,128)S(1)}, f32[256,256]{1,0:T(8,128)S(1)}, u32[]{:S(2)}, u32[]{:S(2)}) collective-permute-start(f32[256,256]{1,0:T(8,128)S(1)} %fusion.9), channel_id=1, source_target_pairs={{0,48},{16,0},{32,16},{48,32},{64,112},{80,64},{96,80},{112,96},{1... | collective-permute-start | bytes 786440 | tf_op jit(solution)/shard_map/ppermute | solution.py:225
  111.4 13.1 %collective-permute-start.5 = (f32[256,256]{1,0:T(8,128)S(1)}, f32[256,256]{1,0:T(8,128)S(1)}, u32[]{:S(2)}, u32[]{:S(2)}) collective-permute-start(f32[256,256]{1,0:T(8,128)S(1)} %fusion.10), channel_id=1, source_target_pairs={{0,16},{16,32},{32,48},{48,0},{64,80},{80,96},{96,112},{112,64},{1... | collective-permute-start | bytes 786440 | tf_op jit(solution)/shard_map/ppermute | solution.py:225
  117.9 8.2 %collective-permute-start.20 = (f32[256,256]{1,0:T(8,128)S(1)}, f32[256,256]{1,0:T(8,128)S(1)}, u32[]{:S(2)}, u32[]{:S(2)}) collective-permute-start(f32[256,256]{1,0:T(8,128)S(1)} %fusion.3), channel_id=1, source_target_pairs={{0,192},{16,208},{32,224},{48,240},{64,0},{80,16},{96,32},{112,48}... | collective-permute-start | bytes 786440 | tf_op jit(solution)/shard_map/ppermute | solution.py:232
  122.3 7.7 %collective-permute-start.19 = (f32[256,256]{1,0:T(8,128)S(1)}, f32[256,256]{1,0:T(8,128)S(1)}, u32[]{:S(2)}, u32[]{:S(2)}) collective-permute-start(f32[256,256]{1,0:T(8,128)S(1)} %fusion.4), channel_id=1, source_target_pairs={{0,64},{16,80},{32,96},{48,112},{64,128},{80,144},{96,160},{112,17... | collective-permute-start | bytes 786440 | tf_op jit(solution)/shard_map/ppermute | solution.py:232
  122.4 7.6 %collective-permute-start.14 = (f32[256,256]{1,0:T(8,128)S(1)}, f32[256,256]{1,0:T(8,128)S(1)}, u32[]{:S(2)}, u32[]{:S(2)}) collective-permute-start(f32[256,256]{1,0:T(8,128)S(1)} %fusion.5), channel_id=1, source_target_pairs={{0,48},{16,0},{32,16},{48,32},{64,112},{80,64},{96,80},{112,96},{1... | collective-permute-start | bytes 786440 | tf_op jit(solution)/shard_map/ppermute | solution.py:225
  123.1 7.7 %collective-permute-start.13 = (f32[256,256]{1,0:T(8,128)S(1)}, f32[256,256]{1,0:T(8,128)S(1)}, u32[]{:S(2)}, u32[]{:S(2)}) collective-permute-start(f32[256,256]{1,0:T(8,128)S(1)} %fusion.6), channel_id=1, source_target_pairs={{0,16},{16,32},{32,48},{48,0},{64,80},{80,96},{96,112},{112,64},{1... | collective-permute-start | bytes 786440 | tf_op jit(solution)/shard_map/ppermute | solution.py:225
  136.4 6.7 %collective-permute-start.26 = (f32[2,128,256]{2,1,0:T(8,128)}, f32[2,128,256]{2,1,0:T(8,128)S(1)}, u32[]{:S(2)}, u32[]{:S(2)}) collective-permute-start(f32[2,128,256]{2,1,0:T(8,128)} %get-tuple-element.77), channel_id=1, source_target_pairs={{0,48},{16,0},{32,16},{48,32},{64,112},{80,64},{96,80},{112,96},{1... | collective-permute-start | bytes 786440 | tf_op jit(solution)/shard_map/ppermute | solution.py:225
  136.5 8.9 %collective-permute-start.25 = (f32[2,128,256]{2,1,0:T(8,128)}, f32[2,128,256]{2,1,0:T(8,128)S(1)}, u32[]{:S(2)}, u32[]{:S(2)}) collective-permute-start(f32[2,128,256]{2,1,0:T(8,128)} %get-tuple-element.76), channel_id=1, source_target_pairs={{0,16},{16,32},{32,48},{48,0},{64,80},{80,96},{96,112},{112,64},{1... | collective-permute-start | bytes 786440 | tf_op jit(solution)/shard_map/ppermute | solution.py:225
  138.5 9.0 %collective-permute-start.22 = (f32[2,128,256]{2,1,0:T(8,128)}, f32[2,128,256]{2,1,0:T(8,128)S(1)}, u32[]{:S(2)}, u32[]{:S(2)}) collective-permute-start(f32[2,128,256]{2,1,0:T(8,128)} %get-tuple-element.72), channel_id=1, source_target_pairs={{0,192},{16,208},{32,224},{48,240},{64,0},{80,16},{96,32},{112,48}... | collective-permute-start | bytes 786440 | tf_op jit(solution)/shard_map/ppermute | solution.py:232
  141.9 10.1 %collective-permute-start.21 = (f32[2,128,256]{2,1,0:T(8,128)}, f32[2,128,256]{2,1,0:T(8,128)S(1)}, u32[]{:S(2)}, u32[]{:S(2)}) collective-permute-start(f32[2,128,256]{2,1,0:T(8,128)} %get-tuple-element.71), channel_id=1, source_target_pairs={{0,64},{16,80},{32,96},{48,112},{64,128},{80,144},{96,160},{112,17... | collective-permute-start | bytes 786440 | tf_op jit(solution)/shard_map/ppermute | solution.py:232
  144.1 9.1 %collective-permute-start.28 = (f32[128,256]{1,0:T(8,128)S(1)}, f32[128,256]{1,0:T(8,128)S(1)}, u32[]{:S(2)}, u32[]{:S(2)}) collective-permute-start(f32[128,256]{1,0:T(8,128)S(1)} %fusion.11), channel_id=1, source_target_pairs={{0,48},{16,0},{32,16},{48,32},{64,112},{80,64},{96,80},{112,96},{1... | collective-permute-start | bytes 393224 | tf_op jit(solution)/shard_map/ppermute | solution.py:225
  146.5 6.8 %collective-permute-start.27 = (f32[128,256]{1,0:T(8,128)S(1)}, f32[128,256]{1,0:T(8,128)S(1)}, u32[]{:S(2)}, u32[]{:S(2)}) collective-permute-start(f32[128,256]{1,0:T(8,128)S(1)} %fusion.12), channel_id=1, source_target_pairs={{0,16},{16,32},{32,48},{48,0},{64,80},{80,96},{96,112},{112,64},{1... | collective-permute-start | bytes 393224 | tf_op jit(solution)/shard_map/ppermute | solution.py:225
  153.1 6.3 %collective-permute-start.23 = (f32[128,256]{1,0:T(8,128)S(1)}, f32[128,256]{1,0:T(8,128)S(1)}, u32[]{:S(2)}, u32[]{:S(2)}) collective-permute-start(f32[128,256]{1,0:T(8,128)S(1)} %fusion.14), channel_id=1, source_target_pairs={{0,64},{16,80},{32,96},{48,112},{64,128},{80,144},{96,160},{112,17... | collective-permute-start | bytes 393224 | tf_op jit(solution)/shard_map/ppermute | solution.py:232
  162.8 23.9 %collective-permute-start.29 = (f32[2,256,256]{2,1,0:T(8,128)}, f32[2,256,256]{2,1,0:T(8,128)S(1)}, u32[]{:S(2)}, u32[]{:S(2)}) collective-permute-start(f32[2,256,256]{2,1,0:T(8,128)} %get-tuple-element.80), channel_id=1, source_target_pairs={{112,32},{0,2},{32,18},{80,48},{208,46},{160,226},{128,242},{240,6... | collective-permute-start | bytes 1572872 | tf_op jit(solution)/shard_map/ppermute | solution.py:335
  172.7 14.0 %collective-permute-start.30 = (f32[2,256,256]{2,1,0:T(8,128)}, f32[2,256,256]{2,1,0:T(8,128)S(1)}, u32[]{:S(2)}, u32[]{:S(2)}) collective-permute-start(f32[2,256,256]{2,1,0:T(8,128)} %get-tuple-element.81), channel_id=1, source_target_pairs={{112,2},{0,48},{32,32},{80,18},{208,226},{160,62},{128,46},{240,24... | collective-permute-start | bytes 1572872 | tf_op jit(solution)/shard_map/ppermute | solution.py:334
  203.8 13.4 %all-to-all-start.2 = ((f32[16,16,128]{2,1,0:T(8,128)}), f32[16,16,128]{2,1,0:T(8,128)S(1)}, u32[]{:S(2)}, u32[]{:S(2)}) async-start(f32[16,16,128]{2,1,0:T(8,128)} %broadcast_in_dim.22), calls=%async_computation.2 | async-start | bytes 262144 | tf_op jit(solution)/shard_map/all_to_all | solution.py:257
  (35 other events, 430.0 us)

commit v3 on v2

--- a/solution.py
+++ b/solution.py
@@ -76,25 +76,36 @@
     return lax.dot_general(lhs, rhs, (((1,), (1,)), ((), ())), preferred_element_type=jnp.float32)
 
 
-def real_part(lhs, rhs):
-    return matmul(lhs, rhs)
-
-
-def imag_part(lhs, rhs):
-    times = lhs.shape[1] // 2
-    return matmul(lhs[:, times:], rhs[:, :times]) - matmul(lhs[:, :times], rhs[:, times:])
-
-
-def diagonal_kernel(here, out):
-    quarter = here.shape[0] // 2
-
-    @pl.loop(0, 3)
+def rows_of(ref, half):
+    quarter = ref.shape[0] // 2
+    return ref[pl.ds(pl.multiple_of(half * quarter, quarter), quarter), :]
+
+
+def side_by_side(out, real, imag):
+    times = real.shape[1]
+    out[:, :times] = real[...]
+    out[:, times:] = imag[...]
+
+
+def turned(out, real, imag):
+    times = real.shape[1]
+    out[:, :times] = -imag[...]
+    out[:, times:] = real[...]
+
+
+def diagonal_kernel(real, imag, out, block, found):
+    side_by_side(block.at[0], real, imag)
+    turned(block.at[1], real, imag)
+
+    @pl.loop(0, 6)
     def _(i):
-        low = pl.ds(pl.multiple_of(jnp.where(i == 1, quarter, 0), quarter), quarter)
-        other = pl.ds(pl.multiple_of(jnp.where(i == 0, 0, quarter), quarter), quarter)
-        lhs, rhs = here[low, :], here[other, :]
-        out[2 * i] = real_part(lhs, rhs)
-        out[2 * i + 1] = imag_part(lhs, rhs)
+        lhs = rows_of(block.at[0], jnp.where(i // 2 == 1, 1, 0))
+        rhs = rows_of(block.at[i % 2], jnp.where(i < 2, 0, 1))
+        found[i] = matmul(lhs, rhs)
+
+    out[0] = found[0] + found[1]
+    out[1] = found[2] + found[3]
+    out[2], out[3] = found[4], found[5]
 
 
 def stores(right, left, up, down, own):
@@ -113,83 +124,64 @@
 ORDER = ((2, 0), (1, 1), (2, 1), (3, 0), (1, 0), (3, 1), (0, 0), (0, 1))
 
 
-def early_kernel(device, table, here, above, below, *outs):
-    quarter = here.shape[0] // 2
+def stack(refs, lefts, rights):
+    side_by_side(lefts.at[0], refs[0], refs[1])
+    side_by_side(lefts.at[1], refs[4], refs[5])
+    side_by_side(rights.at[0], refs[2], refs[3])
+    turned(rights.at[1], refs[2], refs[3])
+
+
+def early_kernel(device, table, *refs):
+    outs, lefts, rights = refs[6:16], refs[16], refs[17]
+    stack(refs, lefts, rights)
     for t, j in ORDER:
-        for color, part in enumerate((real_part, imag_part)):
+        for color in range(2):
             index = table[device[0] * 16 + color * 8 + t * 2 + j]
-            low = pl.ds(pl.multiple_of((index // 2 % 2) * quarter, quarter), quarter)
-            other = pl.ds(pl.multiple_of((index % 2) * quarter, quarter), quarter)
-            lhs = jnp.where(index < 4, here[low, :], below[low, :])
-            stores(*outs[5 * color : 5 * color + 5])[t, j][...] = part(lhs, above[other, :])
-
-
-def late_kernel(device, table, diagonal, below, above2, below2, *refs):
-    outs, found = refs[:-1], refs[-1]
-    quarter = below.shape[0] // 2
+            lhs = rows_of(lefts.at[index // 4], index // 2 % 2)
+            rhs = rows_of(rights.at[color], index % 2)
+            stores(*outs[5 * color : 5 * color + 5])[t, j][...] = matmul(lhs, rhs)
+
+
+def late_kernel(device, table, diagonal, *refs):
+    outs, lefts, rights = refs[6:16], refs[16], refs[17]
+    stack(refs, lefts, rights)
     upper = (device[1] >= PLANES // 2).astype(jnp.int32)
-
-    @pl.loop(0, 2 * SIDE)
-    def _(place):
-        for color, part in enumerate((real_part, imag_part)):
-            index = table[device[0] * 16 + color * 8 + place]
-            out = found.at[color * 8 + place]
-
-            @pl.when(index < 6)
-            def _():
-                near = index < 4
-                h = jnp.where(near, index // 2, index - 4)
-                k = jnp.where(near, index % 2, (h + upper) % 2)
-                low = pl.ds(pl.multiple_of(h * quarter, quarter), quarter)
-                other = pl.ds(pl.multiple_of(k * quarter, quarter), quarter)
-                lhs = jnp.where(near, below[low, :], below2[low, :])
-                out[...] = part(lhs, above2[other, :])
-
-            @pl.when(index >= 6)
-            def _():
-                packed = diagonal[2 * color] + diagonal[2 * color + 1]
-                out[...] = jnp.where(index == 6, packed, diagonal[4 + color])
-
+    for t, j in ORDER:
+        for color in range(2):
+            index = table[device[0] * 16 + color * 8 + t * 2 + j]
+            near = index < 4
+            h = jnp.where(near, index // 2, index % 2)
+            k = jnp.where(near, index % 2, (h + upper) % 2)
+            lhs = rows_of(lefts.at[index // 4], h)
+            product = matmul(lhs, rows_of(rights.at[color], k))
+            ready = diagonal[jnp.maximum(index - 6, 0) * 2 + color]
+            out = stores(*outs[5 * color : 5 * color + 5])[t, j]
+            out[...] = jnp.where(index < 6, product, ready)
+
+
+def finish_kernel(device, ahead, *refs):
+    ins, outs, sums = refs[:20], refs[20:28], refs[28]
+    slab = sums.shape[1] // 4
     for color in range(2):
-        places = stores(*outs[5 * color : 5 * color + 5])
-        for t, j in ORDER:
-            places[t, j][...] = found[color * 8 + t * 2 + j]
-
-
-def finish_kernel(device, ahead, *refs):
-    ins, outs, sums = refs[:20], refs[20:30], refs[30]
-    quarter = sums.shape[-1]
-    half = quarter // 2
-    for color in range(2):
-        for group in range(2):
-            own, right, left, right2, left2 = ins[10 * color + 5 * group :][:5]
-            sums[2 * group] = own[0] + right2[...] + left[1]
-            sums[2 * group + 1] = own[1] + right[1] + left2[...]
-        right, left, up, down, own = outs[5 * color : 5 * color + 5]
-        entry = [sums.at[ahead[device[0] * 8 + color * 4 + t]] for t in range(SIDE)]
-        own[...] = entry[0][...]
-        up[...] = entry[1][:half, :]
-        right[1] = entry[1][half:, :]
-        right[0] = entry[2][:half, :]
-        left[0] = entry[2][half:, :]
-        left[1] = entry[3][:half, :]
-        down[...] = entry[3][half:, :]
+
+        @pl.loop(0, 4)
+        def _(i):
+            rows = pl.ds(pl.multiple_of(i * slab, slab), slab)
+            for group in range(2):
+                own, right, left, right2, left2 = ins[10 * color + 5 * group :][:5]
+                sums[2 * group, rows] = own[0, rows] + right2[rows] + left[1, rows]
+                sums[2 * group + 1, rows] = own[1, rows] + right[1, rows] + left2[rows]
+
+        @pl.loop(0, 4)
+        def _(i):
+            rows = pl.ds(pl.multiple_of(i * slab, slab), slab)
+            for t in range(SIDE):
+                outs[4 * color + t][rows] = sums[ahead[device[0] * 8 + color * 4 + t], rows]
 
 
 def mirror_kernel(device, flags, *refs):
-    total = []
-    for own, right, left, right2, left2 in (refs[:5], refs[5:10]):
-        half = right2.shape[0]
-        total.append(
-            jnp.concatenate(
-                [
-                    own[:half, :] + right2[...] + left[1],
-                    own[half:, :] + right[1] + left2[...],
-                ]
-            )
-        )
-    first, second = refs[10:]
-    p, q = total
+    p, q = [(refs[i][...] + refs[i + 2][...]) + (refs[i + 1][...] + refs[i + 3][...]) for i in (0, 4)]
+    first, second = refs[8:]
     pt, qt = p.T, q.T
     flip = flags[device[0] * 2] == 1
     diagonal = flags[device[0] * 2 + 1] == 1
@@ -214,10 +206,6 @@
     )(*scalars, *blocks)
 
 
-def message_shapes(rows, columns):
-    return [(2, rows, columns)] * 2 + [(rows, columns)] * 2
-
-
 def shift_x(value, step):
     pairs = [
         (y * SIDE + x, y * SIDE + (x + step) % SIDE) for y in range(SIDE) for x in range(SIDE)
@@ -247,8 +235,8 @@
     return own, right, left, shift(up, 1), shift(down, -1)
 
 
-def ring(outs, shift):
-    return ring_end(ring_start(outs, shift), shift)
+def direct(outs, shift):
+    return (outs[0],) + tuple(shift(outs[t], t) for t in range(1, SIDE))
 
 
 def exchange(parts, axis):
@@ -287,44 +275,52 @@
     first, second, early, late, ahead, flags, half = tables()
     device_index = row_index * PLANES + column_index
     device = jnp.stack([device_index, column_index]).astype(jnp.int32)
-    here = samples.reshape(samples.shape[0], -1)
-    antennas, times = here.shape
+    here = samples[:, 0, :], samples[:, 1, :]
+    antennas, times = here[0].shape
     quarter = antennas // 2
-    product = 2 * quarter * quarter * times
-    above, below = shift_z(here, -1), shift_z(here, 1)
-    gain, free = lax.optimization_barrier((gain, here))
-    (diagonal,) = kernel_call(diagonal_kernel, (), (free,), [(6, quarter, quarter)], 6 * product)
-    above, below, diagonal = lax.optimization_barrier((above, below, diagonal))
-    above2, below2 = shift_z(above, -1), shift_z(below, 1)
-    shapes = 2 * (message_shapes(quarter, quarter) + [(2, quarter, quarter)])
+    product = 4 * quarter * quarter * times
+    stacks = [pltpu.VMEM((2, antennas, 2 * times), here[0].dtype)] * 2
+    found = stacks[0], pltpu.VMEM((6, quarter, quarter), jnp.float32)
+    near = [(shift_z(part, -1), shift_z(part, 1)) for part in here]
+    far = [(shift_z(above, -1), shift_z(below, 1)) for above, below in near]
+    above, below = zip(*near)
+    above2, below2 = zip(*far)
+    gain, *free = lax.optimization_barrier((gain, *here))
+    (diagonal,) = kernel_call(diagonal_kernel, (), free, [(4, quarter, quarter)], 6 * product, found)
+    *below, diagonal = lax.optimization_barrier((*below, diagonal))
+    shapes = 2 * ([(2, quarter, quarter)] * 2 + [(quarter, quarter)] * 2 + [(2, quarter, quarter)])
     outs = kernel_call(
         early_kernel,
         (device, jnp.asarray(early.reshape(-1))),
-        (here, above, below),
+        (*here, *above, *below),
         shapes,
         16 * product,
+        stacks,
     )
     along_x, along_y = ring_start(outs[:5], shift_x), ring_start(outs[5:], shift_y)
     sums = along_x[3:] + along_y[3:]
-    *_, above2, below2 = lax.optimization_barrier((*sums, above2, below2))
+    *above2, first_below2, second_below2 = lax.optimization_barrier((*sums, *above2, *below2))[4:]
     early_parts = ring_end(along_x, shift_x), ring_end(along_y, shift_y)
     outs = kernel_call(
         late_kernel,
         (device, jnp.asarray(late.reshape(-1))),
-        (diagonal, below, above2, below2),
+        (diagonal, *below, *above2, first_below2, second_below2),
         shapes,
         12 * product,
-        scratch=(pltpu.VMEM((16, quarter, quarter), jnp.float32),),
-    )
-    late_parts = ring(outs[:5], shift_x), ring(outs[5:], shift_y)
+        stacks,
+    )
+    late_parts = [
+        ring_end(ring_start(part, shift), shift)
+        for part, shift in ((outs[:5], shift_x), (outs[5:], shift_y))
+    ]
     outs = kernel_call(
         finish_kernel,
         (device, jnp.asarray(ahead.reshape(-1))),
         early_parts[0] + late_parts[0] + early_parts[1] + late_parts[1],
-        2 * (message_shapes(quarter // 2, quarter) + [(quarter, quarter)]),
+        [(quarter, quarter)] * 8,
         scratch=(pltpu.VMEM((4, quarter, quarter), jnp.float32),),
     )
-    parts = ring(outs[:5], shift_y) + ring(outs[5:], shift_x)
+    parts = direct(outs[:4], shift_y) + direct(outs[4:], shift_x)
     one, two = kernel_call(
         mirror_kernel,
         (device, jnp.asarray(flags.reshape(-1))),

time: 232 us -> 244 us (1.052)
  starting transfers between devices: 70.3 us -> 78.1 us
  other arithmetic: 12.1 us -> 5.4 us
  local copies, waits for them, and re-layouts: 7.96 us -> 14.4 us
  blocking collectives: 25.3 us -> 28.8 us
    ppermute x4 -> x8, waiting for transfers between devices: 1.19 us -> 14 us  [shift_z(): lax.ppermute(value, 'col', [(c, (c + step) % PLANES) for c in range(PLANE...]
    ppermute x4 -> x8, starting transfers between devices: 4.13 us -> 12.8 us  [shift_z(): lax.ppermute(value, 'col', [(c, (c + step) % PLANES) for c in range(PLANE...]
    add x12 -> x8, other arithmetic: 9.04 us -> 2.27 us  [ring_start(): return (own, right, left, up + right[0], down + left[0])]
    ppermute x1, waiting for transfers between devices: 10.1 us -> 3.41 us  [vis_tiles(): two = lax.ppermute(two, ('row', 'col'), second)]
    ppermute x1, waiting for transfers between devices: 19.5 us -> 15.3 us  [starting_gains(): share = lax.ppermute(initial_gains, ('row', 'col'), pairs)]
    ppermute x1, waiting for transfers between devices: 0.01 us -> 4.25 us  [vis_tiles(): one = lax.ppermute(one, ('row', 'col'), first)]
    all_to_all x1, blocking collectives: 15 us -> 18.6 us  [exchange(): return lax.all_to_all(copies, axis, 0, 0)]
    ppermute x12 -> x11, starting transfers between devices: 12.4 us -> 9.16 us  [shift_x(): return lax.ppermute(value, 'row', pairs)]
  transfers between devices with their start and end apart: 33 -> 35, of which waited for: 16 -> 19; matrix products, arithmetic and copies ran while one was open for 5% -> 2% of each run, Pallas kernels for 2% -> 2%
where the time goes in v3:
time: 244 us; the launch traced here: 241 us
  waiting for transfers between devices  88.1 us (36%)
  starting transfers between devices  78.1 us (32%)
  blocking collectives  28.8 us (12%)
  Pallas kernels  25.1 us (10%)
  local copies, waits for them, and re-layouts  14.4 us (6%)
  other arithmetic  5.4 us (2%)
    pallas_call x5, Pallas kernels, kernel_call(): pl.pallas_call(kernel, out_shape=shapes, in_specs=[smem] * len(scalars) +...  25.1 us
    ppermute x11, waiting for transfers between devices, shift_y(): return lax.ppermute(value, 'row', pairs)  23.2 us
    all_to_all x1, blocking collectives, exchange(): return lax.all_to_all(copies, axis, 0, 0)  18.6 us
    all_to_all x2, starting transfers between devices, exchange(): return lax.all_to_all(copies, axis, 0, 0)  17.6 us
    ppermute x11, starting transfers between devices, shift_y(): return lax.ppermute(value, 'row', pairs)  17 us
    ppermute x1, waiting for transfers between devices, starting_gains(): share = lax.ppermute(initial_gains, ('row', 'col'), pairs)  15.3 us
    all_to_all x2, waiting for transfers between devices, exchange(): return lax.all_to_all(copies, axis, 0, 0)  14.9 us
    ppermute x8, waiting for transfers between devices, shift_z(): lax.ppermute(value, 'col', [(c, (c + step) % PLANES) for c in range(PLANE...  14 us
  transfers between devices with their start and end apart: 35, of which 19 were waited for; matrix products, arithmetic and copies ran while one was open for 2% of the time, Pallas kernels for 2%

profile of v3, /device:TPU:64, one launch (start us, length us, event | category | flops | bytes accessed | tf_op | source)
XLA Modules:
  0.0 241.4 jit_solution(5619247510569182290)
XLA Ops:
  0.0 3.2 %fusion.12 = (bf16[512,1,512]{2,1,0:T(2,128)(2,1)S(1)}, bf16[512,1,512]{2,1,0:T(2,128)(2,1)S(1)}) fusion(bf16[512,2,512]{2,1,0:T(2,128)(2,1)} %param.8), kind=kLoop, calls=%fused_computation.67 | loop fusion | bytes 2097152 | tf_op jit(solution)/shard_map/slice | solution.py:278
  5.5 3.2 %collective-permute-start.3 = (bf16[512,512]{1,0:T(8,128)(2,1)S(1)}, bf16[512,512]{1,0:T(8,128)(2,1)S(1)}, u32[]{:S(2)}, u32[]{:S(2)}) collective-permute-start(bf16[512,512]{1,0:T(8,128)(2,1)S(1)} %bitcast.93), channel_id=1, source_target_pairs={{0,2},{2,4},{4,6},{6,8},{8,10},{10,12},{12,14},{14,0},{1,3},{3,5},... | collective-permute-start | bytes 1572872 | tf_op jit(solution)/shard_map/ppermute | solution.py:224
  8.7 6.9 %collective-permute-start.4 = (f32[2,32]{1,0:T(2,128)S(1)}, f32[2,32]{1,0:T(2,128)S(1)}, u32[]{:S(2)}, u32[]{:S(2)}) collective-permute-start(f32[2,32]{1,0:T(2,128)S(1)} %copy-done.39), channel_id=1, source_target_pairs={{0,0},{2,16},{4,32},{6,48},{8,64},{10,80},{12,96},{14,112},{16,128... | collective-permute-start | bytes 776 | tf_op jit(solution)/shard_map/ppermute | solution.py:347
  15.7 15.3 %collective-permute-done.4 = f32[2,32]{1,0:T(2,128)S(1)} collective-permute-done((f32[2,32]{1,0:T(2,128)S(1)}, f32[2,32]{1,0:T(2,128)S(1)}, u32[]{:S(2)}, u32[]{:S(2)}) %collective-permute-start.4) | collective-permute-done | bytes 288 | tf_op jit(solution)/shard_map/ppermute | solution.py:347
  31.5 9.8 %all-to-all-start = ((f32[16,2,32]{2,1,0:T(2,128)}), f32[16,2,32]{2,1,0:T(2,128)S(1)}, u32[]{:S(2)}, u32[]{:S(2)}) async-start(f32[16,2,32]{2,1,0:T(2,128)} %broadcast_in_dim.8), calls=%async_computation | async-start | bytes 32768 | tf_op jit(solution)/shard_map/all_to_all | solution.py:245
  42.0 6.9 %all-to-all-done = f32[16,2,32]{2,1,0:T(2,128)S(1)} async-done(((f32[16,2,32]{2,1,0:T(2,128)}), f32[16,2,32]{2,1,0:T(2,128)S(1)}, u32[]{:S(2)}, u32[]{:S(2)}) %all-to-all-start) | async-done | bytes 4128 | tf_op jit(solution)/shard_map/all_to_all | solution.py:245
  49.0 4.5 %shard_map.82.diagonal = f32[4,256,256]{2,1,0:T(8,128)} custom-call(bf16[512,512]{1,0:T(8,128)(2,1)} %bitcast.91, bf16[512,512]{1,0:T(8,128)(2,1)} %bitcast.95), custom_call_target="tpu_custom_call" | custom-call | flops 805306368 | bytes 2097152 | tf_op jit(solution)/shard_map/pallas_call | solution.py:199
  54.7 6.0 %shard_map.83 = (f32[2,256,256]{2,1,0:T(8,128)}, f32[2,256,256]{2,1,0:T(8,128)}, f32[256,256]{1,0:T(8,128)}, f32[256,256]{1,0:T(8,128)}, f32[2,256,256]{2,1,0:T(...) custom-call(s32[2]{0:T(128)} %pad_add_fusion.device, ...), custom_call_target="tpu_custom_call" | custom-call | flops 2147483648 | bytes 7340032 | tf_op jit(solution)/shard_map/pallas_call | solution.py:199
  66.5 5.0 %collective-permute-done.10.refs_12_ = f32[2,256,256]{2,1,0:T(8,128)S(1)} collective-permute-done((f32[2,256,256]{2,1,0:T(8,128)}, f32[2,256,256]{2,1,0:T(8,128)S(1)}, u32[]{:S(2)}, u32[]{:S(2)}) %collective-permute-start.10) | collective-permute-done | bytes 524320 | tf_op jit(solution)/shard_map/ppermute | solution.py:220
  80.5 5.9 %collective-permute-done.12.refs_3_ = bf16[512,512]{1,0:T(8,128)(2,1)S(1)} collective-permute-done((bf16[512,512]{1,0:T(8,128)(2,1)}, bf16[512,512]{1,0:T(8,128)(2,1)S(1)}, u32[]{:S(2)}, u32[]{:S(2)}) %collective-permute-start.12) | collective-permute-done | bytes 524320 | tf_op jit(solution)/shard_map/ppermute | solution.py:224
  86.4 3.0 %collective-permute-done.13.refs_4_ = bf16[512,512]{1,0:T(8,128)(2,1)S(1)} collective-permute-done((bf16[512,512]{1,0:T(8,128)(2,1)S(1)}, bf16[512,512]{1,0:T(8,128)(2,1)S(1)}, u32[]{:S(2)}, u32[]{:S(2)}) %collective-permute-start.13) | collective-permute-done | bytes 524320 | tf_op jit(solution)/shard_map/ppermute | solution.py:224
  90.2 5.1 %collective-permute-done.14.refs_5_ = bf16[512,512]{1,0:T(8,128)(2,1)} collective-permute-done((bf16[512,512]{1,0:T(8,128)(2,1)}, bf16[512,512]{1,0:T(8,128)(2,1)}, u32[]{:S(2)}, u32[]{:S(2)}) %collective-permute-start.14) | collective-permute-done | bytes 524320 | tf_op jit(solution)/shard_map/ppermute | solution.py:224
  95.3 6.5 %shard_map.84 = (f32[2,256,256]{2,1,0:T(8,128)}, f32[2,256,256]{2,1,0:T(8,128)}, f32[256,256]{1,0:T(8,128)}, f32[256,256]{1,0:T(8,128)}, f32[2,256,256]{2,1,0:T(...) custom-call(s32[2]{0:T(128)} %pad_add_fusion.device, ...), custom_call_target="tpu_custom_call" | custom-call | flops 1610612736 | bytes 8388608 | tf_op jit(solution)/shard_map/pallas_call | solution.py:199
  101.8 2.6 %collective-permute-start.22 = (f32[2,256,256]{2,1,0:T(8,128)}, f32[2,256,256]{2,1,0:T(8,128)S(1)}, u32[]{:S(2)}, u32[]{:S(2)}) collective-permute-start(f32[2,256,256]{2,1,0:T(8,128)} %get-tuple-element.71), channel_id=1, source_target_pairs={{0,192},{16,208},{32,224},{48,240},{64,0},{80,16},{96,32},{112,48}... | collective-permute-start | bytes 1572872 | tf_op jit(solution)/shard_map/ppermute | solution.py:220
  105.4 3.2 %collective-permute-start.20 = (f32[256,256]{1,0:T(8,128)S(1)}, f32[256,256]{1,0:T(8,128)S(1)}, u32[]{:S(2)}, u32[]{:S(2)}) collective-permute-start(f32[256,256]{1,0:T(8,128)S(1)} %fusion.7), channel_id=1, source_target_pairs={{0,192},{16,208},{32,224},{48,240},{64,0},{80,16},{96,32},{112,48}... | collective-permute-start | bytes 786440 | tf_op jit(solution)/shard_map/ppermute | solution.py:220
  108.7 5.0 %collective-permute-done.22.refs_17_ = f32[2,256,256]{2,1,0:T(8,128)S(1)} collective-permute-done((f32[2,256,256]{2,1,0:T(8,128)}, f32[2,256,256]{2,1,0:T(8,128)S(1)}, u32[]{:S(2)}, u32[]{:S(2)}) %collective-permute-start.22) | collective-permute-done | bytes 524320 | tf_op jit(solution)/shard_map/ppermute | solution.py:220
  119.2 6.8 %collective-permute-done.15.refs_6_ = f32[2,256,256]{2,1,0:T(8,128)S(1)} collective-permute-done((f32[2,256,256]{2,1,0:T(8,128)}, f32[2,256,256]{2,1,0:T(8,128)S(1)}, u32[]{:S(2)}, u32[]{:S(2)}) %collective-permute-start.15) | collective-permute-done | bytes 524320 | tf_op jit(solution)/shard_map/ppermute | solution.py:213
  126.0 4.3 %collective-permute-start.24 = (f32[256,256]{1,0:T(8,128)S(1)}, f32[256,256]{1,0:T(8,128)S(1)}, u32[]{:S(2)}, u32[]{:S(2)}) collective-permute-start(f32[256,256]{1,0:T(8,128)S(1)} %fusion.3), channel_id=1, source_target_pairs={{0,192},{16,208},{32,224},{48,240},{64,0},{80,16},{96,32},{112,48}... | collective-permute-start | bytes 786440 | tf_op jit(solution)/shard_map/ppermute | solution.py:220
  134.3 3.8 %collective-permute-done.23.refs_18_ = f32[256,256]{1,0:T(8,128)S(1)} collective-permute-done((f32[256,256]{1,0:T(8,128)S(1)}, f32[256,256]{1,0:T(8,128)S(1)}, u32[]{:S(2)}, u32[]{:S(2)}) %collective-permute-start.23) | collective-permute-done | bytes 262176 | tf_op jit(solution)/shard_map/ppermute | solution.py:220
  139.2 5.3 %shard_map.85 = (f32[256,256]{1,0:T(8,128)}, f32[256,256]{1,0:T(8,128)}, f32[256,256]{1,0:T(8,128)}, f32[256,256]{1,0:T(8,128)}, f32[256,256]{1,0:T(8,128)}, /*i...) custom-call(s32[2]{0:T(128)} %pad_add_fusion.device, s32[1024]{0:T(1024)} %constant.47.clone.ahead, ...), custom_call_target="tpu_custom_call" | custom-call | bytes 10485760 | tf_op jit(solution)/shard_map/pallas_call | solution.py:199
  144.7 4.6 %collective-permute-start.26 = (f32[256,256]{1,0:T(8,128)}, f32[256,256]{1,0:T(8,128)S(1)}, u32[]{:S(2)}, u32[]{:S(2)}) collective-permute-start(f32[256,256]{1,0:T(8,128)} %get-tuple-element.76), channel_id=1, source_target_pairs={{0,128},{16,144},{32,160},{48,176},{64,192},{80,208},{96,224},{112... | collective-permute-start | bytes 786440 | tf_op jit(solution)/shard_map/ppermute | solution.py:220
  152.8 3.8 %collective-permute-done.26.refs_2_ = f32[256,256]{1,0:T(8,128)S(1)} collective-permute-done((f32[256,256]{1,0:T(8,128)}, f32[256,256]{1,0:T(8,128)S(1)}, u32[]{:S(2)}, u32[]{:S(2)}) %collective-permute-start.26) | collective-permute-done | bytes 262176 | tf_op jit(solution)/shard_map/ppermute | solution.py:220
  156.6 3.2 %collective-permute-done.28.refs_5_ = f32[256,256]{1,0:T(8,128)S(1)} collective-permute-done((f32[256,256]{1,0:T(8,128)}, f32[256,256]{1,0:T(8,128)S(1)}, u32[]{:S(2)}, u32[]{:S(2)}) %collective-permute-start.28) | collective-permute-done | bytes 262176 | tf_op jit(solution)/shard_map/ppermute | solution.py:213
  159.9 2.6 %collective-permute-done.30.refs_7_ = f32[256,256]{1,0:T(8,128)S(1)} collective-permute-done((f32[256,256]{1,0:T(8,128)}, f32[256,256]{1,0:T(8,128)S(1)}, u32[]{:S(2)}, u32[]{:S(2)}) %collective-permute-start.30) | collective-permute-done | bytes 262176 | tf_op jit(solution)/shard_map/ppermute | solution.py:213
  163.2 2.8 %shard_map.86 = (f32[2,256,256]{2,1,0:T(8,128)}, f32[2,256,256]{2,1,0:T(8,128)}) custom-call(s32[2]{0:T(128)} %pad_add_fusion.device, s32[256]{0:T(256)} %constant.48.clone.flags, f32[256,256]{1,0:T(8,128)} %get-tuple-element.74.refs_0_, f32[256,256]{1,0:T(8,128)} %copy-done.20, f32[256,256]{1,0:T(8,128)} %copy-done.24, f32[256,256]{1,0:T(8,128)} %copy-done.26, ...), custom_call_target="tpu_custom_call" | custom-call | bytes 3145728 | tf_op jit(solution)/shard_map/pallas_call | solution.py:199
  166.0 12.7 %collective-permute-start.31 = (f32[2,256,256]{2,1,0:T(8,128)}, f32[2,256,256]{2,1,0:T(8,128)S(1)}, u32[]{:S(2)}, u32[]{:S(2)}) collective-permute-start(f32[2,256,256]{2,1,0:T(8,128)} %get-tuple-element.82), channel_id=1, source_target_pairs={{112,32},{0,2},{32,18},{80,48},{208,46},{160,226},{128,242},{240,6... | collective-permute-start | bytes 1572872 | tf_op jit(solution)/shard_map/ppermute | solution.py:331
  183.4 3.4 %collective-permute-done.31 = f32[2,256,256]{2,1,0:T(8,128)S(1)} collective-permute-done((f32[2,256,256]{2,1,0:T(8,128)}, f32[2,256,256]{2,1,0:T(8,128)S(1)}, u32[]{:S(2)}, u32[]{:S(2)}) %collective-permute-start.31) | collective-permute-done | bytes 524320 | tf_op jit(solution)/shard_map/ppermute | solution.py:331
  186.8 4.2 %collective-permute-done.32 = f32[2,256,256]{2,1,0:T(8,128)S(1)} collective-permute-done((f32[2,256,256]{2,1,0:T(8,128)}, f32[2,256,256]{2,1,0:T(8,128)S(1)}, u32[]{:S(2)}, u32[]{:S(2)}) %collective-permute-start.32) | collective-permute-done | bytes 524320 | tf_op jit(solution)/shard_map/ppermute | solution.py:330
  192.0 18.6 %all_to_all.20 = f32[8,3,256]{2,1,0:T(4,128)S(1)} all-to-all(f32[8,3,256]{2,1,0:T(4,128)S(1)} %broadcast_in_dim.9), channel_id=1, replica_groups=mesh['row'=16,'col'=8,'chan'=2] {'col'}, dimensions={0} | all-to-all | bytes 49152 | tf_op jit(solution)/shard_map/all_to_all | solution.py:245
  211.8 7.8 %all-to-all-start.2 = ((f32[16,16,128]{2,1,0:T(8,128)}), f32[16,16,128]{2,1,0:T(8,128)S(1)}, u32[]{:S(2)}, u32[]{:S(2)}) async-start(f32[16,16,128]{2,1,0:T(8,128)} %broadcast_in_dim.22), calls=%async_computation.2 | async-start | bytes 262144 | tf_op jit(solution)/shard_map/all_to_all | solution.py:245
  219.6 8.0 %all-to-all-done.2 = f32[16,16,128]{2,1,0:T(8,128)S(1)} async-done(((f32[16,16,128]{2,1,0:T(8,128)}), f32[16,16,128]{2,1,0:T(8,128)S(1)}, u32[]{:S(2)}, u32[]{:S(2)}) %all-to-all-start.2) | async-done | bytes 131104 | tf_op jit(solution)/shard_map/all_to_all | solution.py:245
  230.5 10.3 %all_to_all.21 = f32[8,3,32]{2,1,0:T(4,128)S(1)} all-to-all(f32[8,3,32]{2,1,0:T(4,128)S(1)} %maximum_bitcast_fusion), channel_id=1, replica_groups=mesh['row'=16,'col'=8,'chan'=2] {'col'}, dimensions={0} | all-to-all | bytes 6144 | tf_op jit(solution)/shard_map/all_to_all | solution.py:392
  (187 shorter events, 45.6 us)
Async XLA Ops:
  3.3 50.2 %collective-permute-start.2 = (bf16[512,512]{1,0:T(8,128)(2,1)S(1)}, bf16[512,512]{1,0:T(8,128)(2,1)S(1)}, u32[]{:S(2)}, u32[]{:S(2)}) collective-permute-start(bf16[512,512]{1,0:T(8,128)(2,1)S(1)} %bitcast.89), channel_id=1, source_target_pairs={{0,2},{2,4},{4,6},{6,8},{8,10},{10,12},{12,14},{14,0},{1,3},{3,5},... | collective-permute-start | bytes 1572872 | tf_op jit(solution)/shard_map/ppermute | solution.py:224
  5.5 48.1 %collective-permute-start.3 = (bf16[512,512]{1,0:T(8,128)(2,1)S(1)}, bf16[512,512]{1,0:T(8,128)(2,1)S(1)}, u32[]{:S(2)}, u32[]{:S(2)}) collective-permute-start(bf16[512,512]{1,0:T(8,128)(2,1)S(1)} %bitcast.93), channel_id=1, source_target_pairs={{0,2},{2,4},{4,6},{6,8},{8,10},{10,12},{12,14},{14,0},{1,3},{3,5},... | collective-permute-start | bytes 1572872 | tf_op jit(solution)/shard_map/ppermute | solution.py:224
  8.7 44.9 %collective-permute-start = (bf16[512,512]{1,0:T(8,128)(2,1)S(1)}, bf16[512,512]{1,0:T(8,128)(2,1)S(1)}, u32[]{:S(2)}, u32[]{:S(2)}) collective-permute-start(bf16[512,512]{1,0:T(8,128)(2,1)S(1)} %bitcast.90), channel_id=1, source_target_pairs={{0,14},{2,0},{4,2},{6,4},{8,6},{10,8},{12,10},{14,12},{1,15},{3,1}... | collective-permute-start | bytes 1572872 | tf_op jit(solution)/shard_map/ppermute | solution.py:224
  8.7 44.9 %collective-permute-start.1 = (bf16[512,512]{1,0:T(8,128)(2,1)S(1)}, bf16[512,512]{1,0:T(8,128)(2,1)}, u32[]{:S(2)}, u32[]{:S(2)}) collective-permute-start(bf16[512,512]{1,0:T(8,128)(2,1)S(1)} %bitcast.94), channel_id=1, source_target_pairs={{0,14},{2,0},{4,2},{6,4},{8,6},{10,8},{12,10},{14,12},{1,15},{3,1}... | collective-permute-start | bytes 1572872 | tf_op jit(solution)/shard_map/ppermute | solution.py:224
  8.7 22.2 %collective-permute-start.4 = (f32[2,32]{1,0:T(2,128)S(1)}, f32[2,32]{1,0:T(2,128)S(1)}, u32[]{:S(2)}, u32[]{:S(2)}) collective-permute-start(f32[2,32]{1,0:T(2,128)S(1)} %copy-done.39), channel_id=1, source_target_pairs={{0,0},{2,16},{4,32},{6,48},{8,64},{10,80},{12,96},{14,112},{16,128... | collective-permute-start | bytes 776 | tf_op jit(solution)/shard_map/ppermute | solution.py:347
  31.5 17.4 %all-to-all-start = ((f32[16,2,32]{2,1,0:T(2,128)}), f32[16,2,32]{2,1,0:T(2,128)S(1)}, u32[]{:S(2)}, u32[]{:S(2)}) async-start(f32[16,2,32]{2,1,0:T(2,128)} %broadcast_in_dim.8), calls=%async_computation | async-start | bytes 32768 | tf_op jit(solution)/shard_map/all_to_all | solution.py:245
  60.7 10.9 %collective-permute-start.10 = (f32[2,256,256]{2,1,0:T(8,128)}, f32[2,256,256]{2,1,0:T(8,128)S(1)}, u32[]{:S(2)}, u32[]{:S(2)}) collective-permute-start(f32[2,256,256]{2,1,0:T(8,128)} %get-tuple-element.58), channel_id=1, source_target_pairs={{0,192},{16,208},{32,224},{48,240},{64,0},{80,16},{96,32},{112,48}... | collective-permute-start | bytes 1572872 | tf_op jit(solution)/shard_map/ppermute | solution.py:220
  61.8 12.5 %collective-permute-start.9 = (f32[2,256,256]{2,1,0:T(8,128)}, f32[2,256,256]{2,1,0:T(8,128)S(1)}, u32[]{:S(2)}, u32[]{:S(2)}) collective-permute-start(f32[2,256,256]{2,1,0:T(8,128)} %get-tuple-element.56), channel_id=1, source_target_pairs={{0,64},{16,80},{32,96},{48,112},{64,128},{80,144},{96,160},{112,17... | collective-permute-start | bytes 1572872 | tf_op jit(solution)/shard_map/ppermute | solution.py:220
  62.8 13.2 %collective-permute-start.6 = (f32[2,256,256]{2,1,0:T(8,128)}, f32[2,256,256]{2,1,0:T(8,128)S(1)}, u32[]{:S(2)}, u32[]{:S(2)}) collective-permute-start(f32[2,256,256]{2,1,0:T(8,128)} %get-tuple-element.51), channel_id=1, source_target_pairs={{0,48},{16,0},{32,16},{48,32},{64,112},{80,64},{96,80},{112,96},{1... | collective-permute-start | bytes 1572872 | tf_op jit(solution)/shard_map/ppermute | solution.py:213
  64.0 15.5 %collective-permute-start.5 = (f32[2,256,256]{2,1,0:T(8,128)}, f32[2,256,256]{2,1,0:T(8,128)S(1)}, u32[]{:S(2)}, u32[]{:S(2)}) collective-permute-start(f32[2,256,256]{2,1,0:T(8,128)} %get-tuple-element.50), channel_id=1, source_target_pairs={{0,16},{16,32},{32,48},{48,0},{64,80},{80,96},{96,112},{112,64},{1... | collective-permute-start | bytes 1572872 | tf_op jit(solution)/shard_map/ppermute | solution.py:213
  64.8 15.6 %collective-permute-start.11 = (bf16[512,512]{1,0:T(8,128)(2,1)}, bf16[512,512]{1,0:T(8,128)(2,1)S(1)}, u32[]{:S(2)}, u32[]{:S(2)}) collective-permute-start(bf16[512,512]{1,0:T(8,128)(2,1)} %copy-done.35), channel_id=1, source_target_pairs={{0,14},{2,0},{4,2},{6,4},{8,6},{10,8},{12,10},{14,12},{1,15},{3,1}... | collective-permute-start | bytes 1572872 | tf_op jit(solution)/shard_map/ppermute | solution.py:224
  71.6 14.8 %collective-permute-start.12 = (bf16[512,512]{1,0:T(8,128)(2,1)}, bf16[512,512]{1,0:T(8,128)(2,1)S(1)}, u32[]{:S(2)}, u32[]{:S(2)}) collective-permute-start(bf16[512,512]{1,0:T(8,128)(2,1)} %collective-permute-done.1.refs_3_), channel_id=1, source_target_pairs={{0,14},{2,0},{4,2},{6,4},{8,6},{10,8},{12,10},{14,12},{1,15},{3,1}... | collective-permute-start | bytes 1572872 | tf_op jit(solution)/shard_map/ppermute | solution.py:224
  74.3 15.1 %collective-permute-start.13 = (bf16[512,512]{1,0:T(8,128)(2,1)S(1)}, bf16[512,512]{1,0:T(8,128)(2,1)S(1)}, u32[]{:S(2)}, u32[]{:S(2)}) collective-permute-start(bf16[512,512]{1,0:T(8,128)(2,1)S(1)} %copy-done.33), channel_id=1, source_target_pairs={{0,2},{2,4},{4,6},{6,8},{8,10},{10,12},{12,14},{14,0},{1,3},{3,5},... | collective-permute-start | bytes 1572872 | tf_op jit(solution)/shard_map/ppermute | solution.py:224
  76.0 19.3 %collective-permute-start.14 = (bf16[512,512]{1,0:T(8,128)(2,1)}, bf16[512,512]{1,0:T(8,128)(2,1)}, u32[]{:S(2)}, u32[]{:S(2)}) collective-permute-start(bf16[512,512]{1,0:T(8,128)(2,1)} %copy-done.34), channel_id=1, source_target_pairs={{0,2},{2,4},{4,6},{6,8},{8,10},{10,12},{12,14},{14,0},{1,3},{3,5},... | collective-permute-start | bytes 1572872 | tf_op jit(solution)/shard_map/ppermute | solution.py:224
  101.8 11.9 %collective-permute-start.22 = (f32[2,256,256]{2,1,0:T(8,128)}, f32[2,256,256]{2,1,0:T(8,128)S(1)}, u32[]{:S(2)}, u32[]{:S(2)}) collective-permute-start(f32[2,256,256]{2,1,0:T(8,128)} %get-tuple-element.71), channel_id=1, source_target_pairs={{0,192},{16,208},{32,224},{48,240},{64,0},{80,16},{96,32},{112,48}... | collective-permute-start | bytes 1572872 | tf_op jit(solution)/shard_map/ppermute | solution.py:220
  104.4 12.6 %collective-permute-start.21 = (f32[2,256,256]{2,1,0:T(8,128)}, f32[2,256,256]{2,1,0:T(8,128)S(1)}, u32[]{:S(2)}, u32[]{:S(2)}) collective-permute-start(f32[2,256,256]{2,1,0:T(8,128)} %get-tuple-element.70), channel_id=1, source_target_pairs={{0,64},{16,80},{32,96},{48,112},{64,128},{80,144},{96,160},{112,17... | collective-permute-start | bytes 1572872 | tf_op jit(solution)/shard_map/ppermute | solution.py:220
  104.4 13.7 %collective-permute-start.16 = (f32[2,256,256]{2,1,0:T(8,128)}, f32[2,256,256]{2,1,0:T(8,128)S(1)}, u32[]{:S(2)}, u32[]{:S(2)}) collective-permute-start(f32[2,256,256]{2,1,0:T(8,128)} %get-tuple-element.65), channel_id=1, source_target_pairs={{0,48},{16,0},{32,16},{48,32},{64,112},{80,64},{96,80},{112,96},{1... | collective-permute-start | bytes 1572872 | tf_op jit(solution)/shard_map/ppermute | solution.py:213
  105.4 25.0 %collective-permute-start.20 = (f32[256,256]{1,0:T(8,128)S(1)}, f32[256,256]{1,0:T(8,128)S(1)}, u32[]{:S(2)}, u32[]{:S(2)}) collective-permute-start(f32[256,256]{1,0:T(8,128)S(1)} %fusion.7), channel_id=1, source_target_pairs={{0,192},{16,208},{32,224},{48,240},{64,0},{80,16},{96,32},{112,48}... | collective-permute-start | bytes 786440 | tf_op jit(solution)/shard_map/ppermute | solution.py:220
  108.7 21.9 %collective-permute-start.19 = (f32[256,256]{1,0:T(8,128)S(1)}, f32[256,256]{1,0:T(8,128)S(1)}, u32[]{:S(2)}, u32[]{:S(2)}) collective-permute-start(f32[256,256]{1,0:T(8,128)S(1)} %fusion.8), channel_id=1, source_target_pairs={{0,64},{16,80},{32,96},{48,112},{64,128},{80,144},{96,160},{112,17... | collective-permute-start | bytes 786440 | tf_op jit(solution)/shard_map/ppermute | solution.py:220
  113.7 12.4 %collective-permute-start.15 = (f32[2,256,256]{2,1,0:T(8,128)}, f32[2,256,256]{2,1,0:T(8,128)S(1)}, u32[]{:S(2)}, u32[]{:S(2)}) collective-permute-start(f32[2,256,256]{2,1,0:T(8,128)} %get-tuple-element.64), channel_id=1, source_target_pairs={{0,16},{16,32},{32,48},{48,0},{64,80},{80,96},{96,112},{112,64},{1... | collective-permute-start | bytes 1572872 | tf_op jit(solution)/shard_map/ppermute | solution.py:213
  117.0 13.7 %collective-permute-start.8 = (f32[256,256]{1,0:T(8,128)S(1)}, f32[256,256]{1,0:T(8,128)S(1)}, u32[]{:S(2)}, u32[]{:S(2)}) collective-permute-start(f32[256,256]{1,0:T(8,128)S(1)} %fusion.9), channel_id=1, source_target_pairs={{0,48},{16,0},{32,16},{48,32},{64,112},{80,64},{96,80},{112,96},{1... | collective-permute-start | bytes 786440 | tf_op jit(solution)/shard_map/ppermute | solution.py:213
  118.1 14.5 %collective-permute-start.7 = (f32[256,256]{1,0:T(8,128)S(1)}, f32[256,256]{1,0:T(8,128)S(1)}, u32[]{:S(2)}, u32[]{:S(2)}) collective-permute-start(f32[256,256]{1,0:T(8,128)S(1)} %fusion.10), channel_id=1, source_target_pairs={{0,16},{16,32},{32,48},{48,0},{64,80},{80,96},{96,112},{112,64},{1... | collective-permute-start | bytes 786440 | tf_op jit(solution)/shard_map/ppermute | solution.py:213
  126.0 8.2 %collective-permute-start.24 = (f32[256,256]{1,0:T(8,128)S(1)}, f32[256,256]{1,0:T(8,128)S(1)}, u32[]{:S(2)}, u32[]{:S(2)}) collective-permute-start(f32[256,256]{1,0:T(8,128)S(1)} %fusion.3), channel_id=1, source_target_pairs={{0,192},{16,208},{32,224},{48,240},{64,0},{80,16},{96,32},{112,48}... | collective-permute-start | bytes 786440 | tf_op jit(solution)/shard_map/ppermute | solution.py:220
  130.7 7.9 %collective-permute-start.17 = (f32[256,256]{1,0:T(8,128)S(1)}, f32[256,256]{1,0:T(8,128)S(1)}, u32[]{:S(2)}, u32[]{:S(2)}) collective-permute-start(f32[256,256]{1,0:T(8,128)S(1)} %fusion.6), channel_id=1, source_target_pairs={{0,16},{16,32},{32,48},{48,0},{64,80},{80,96},{96,112},{112,64},{1... | collective-permute-start | bytes 786440 | tf_op jit(solution)/shard_map/ppermute | solution.py:213
  144.6 7.9 %collective-permute-start.25 = (f32[256,256]{1,0:T(8,128)}, f32[256,256]{1,0:T(8,128)S(1)}, u32[]{:S(2)}, u32[]{:S(2)}) collective-permute-start(f32[256,256]{1,0:T(8,128)} %get-tuple-element.75), channel_id=1, source_target_pairs={{0,64},{16,80},{32,96},{48,112},{64,128},{80,144},{96,160},{112,17... | collective-permute-start | bytes 786440 | tf_op jit(solution)/shard_map/ppermute | solution.py:220
  144.7 11.9 %collective-permute-start.26 = (f32[256,256]{1,0:T(8,128)}, f32[256,256]{1,0:T(8,128)S(1)}, u32[]{:S(2)}, u32[]{:S(2)}) collective-permute-start(f32[256,256]{1,0:T(8,128)} %get-tuple-element.76), channel_id=1, source_target_pairs={{0,128},{16,144},{32,160},{48,176},{64,192},{80,208},{96,224},{112... | collective-permute-start | bytes 786440 | tf_op jit(solution)/shard_map/ppermute | solution.py:220
  149.3 10.6 %collective-permute-start.28 = (f32[256,256]{1,0:T(8,128)}, f32[256,256]{1,0:T(8,128)S(1)}, u32[]{:S(2)}, u32[]{:S(2)}) collective-permute-start(f32[256,256]{1,0:T(8,128)} %get-tuple-element.79), channel_id=1, source_target_pairs={{0,16},{16,32},{32,48},{48,0},{64,80},{80,96},{96,112},{112,64},{1... | collective-permute-start | bytes 786440 | tf_op jit(solution)/shard_map/ppermute | solution.py:213
  150.1 9.7 %collective-permute-start.29 = (f32[256,256]{1,0:T(8,128)}, f32[256,256]{1,0:T(8,128)S(1)}, u32[]{:S(2)}, u32[]{:S(2)}) collective-permute-start(f32[256,256]{1,0:T(8,128)} %get-tuple-element.80), channel_id=1, source_target_pairs={{0,32},{16,48},{32,0},{48,16},{64,96},{80,112},{96,64},{112,80},{1... | collective-permute-start | bytes 786440 | tf_op jit(solution)/shard_map/ppermute | solution.py:213
  152.5 10.0 %collective-permute-start.30 = (f32[256,256]{1,0:T(8,128)}, f32[256,256]{1,0:T(8,128)S(1)}, u32[]{:S(2)}, u32[]{:S(2)}) collective-permute-start(f32[256,256]{1,0:T(8,128)} %get-tuple-element.81), channel_id=1, source_target_pairs={{0,48},{16,0},{32,16},{48,32},{64,112},{80,64},{96,80},{112,96},{1... | collective-permute-start | bytes 786440 | tf_op jit(solution)/shard_map/ppermute | solution.py:213
  166.0 20.8 %collective-permute-start.31 = (f32[2,256,256]{2,1,0:T(8,128)}, f32[2,256,256]{2,1,0:T(8,128)S(1)}, u32[]{:S(2)}, u32[]{:S(2)}) collective-permute-start(f32[2,256,256]{2,1,0:T(8,128)} %get-tuple-element.82), channel_id=1, source_target_pairs={{112,32},{0,2},{32,18},{80,48},{208,46},{160,226},{128,242},{240,6... | collective-permute-start | bytes 1572872 | tf_op jit(solution)/shard_map/ppermute | solution.py:331
  178.7 12.4 %collective-permute-start.32 = (f32[2,256,256]{2,1,0:T(8,128)}, f32[2,256,256]{2,1,0:T(8,128)S(1)}, u32[]{:S(2)}, u32[]{:S(2)}) collective-permute-start(f32[2,256,256]{2,1,0:T(8,128)} %get-tuple-element.83), channel_id=1, source_target_pairs={{112,2},{0,48},{32,32},{80,18},{208,226},{160,62},{128,46},{240,24... | collective-permute-start | bytes 1572872 | tf_op jit(solution)/shard_map/ppermute | solution.py:330
  211.8 15.8 %all-to-all-start.2 = ((f32[16,16,128]{2,1,0:T(8,128)}), f32[16,16,128]{2,1,0:T(8,128)S(1)}, u32[]{:S(2)}, u32[]{:S(2)}) async-start(f32[16,16,128]{2,1,0:T(8,128)} %broadcast_in_dim.22), calls=%async_computation.2 | async-start | bytes 262144 | tf_op jit(solution)/shard_map/all_to_all | solution.py:245
  (46 other events, 284.9 us)

commit v4 on v3

--- a/solution.py
+++ b/solution.py
@@ -1,3 +1,7 @@
+import functools
+
+import functools
+
 import jax
 import jax.numpy as jnp
 import numpy as np
@@ -81,21 +85,20 @@
     return ref[pl.ds(pl.multiple_of(half * quarter, quarter), quarter), :]
 
 
-def side_by_side(out, real, imag):
-    times = real.shape[1]
-    out[:, :times] = real[...]
-    out[:, times:] = imag[...]
-
-
-def turned(out, real, imag):
-    times = real.shape[1]
-    out[:, :times] = -imag[...]
-    out[:, times:] = real[...]
+def side_by_side(out, real, imag, turned=False):
+    antennas, times = real.shape
+    slab = antennas // 4
+
+    @pl.loop(0, 4)
+    def _(i):
+        rows = pl.ds(pl.multiple_of(i * slab, slab), slab)
+        out[rows, :times] = -imag[rows, :] if turned else real[rows, :]
+        out[rows, times:] = real[rows, :] if turned else imag[rows, :]
 
 
 def diagonal_kernel(real, imag, out, block, found):
     side_by_side(block.at[0], real, imag)
-    turned(block.at[1], real, imag)
+    side_by_side(block.at[1], real, imag, turned=True)
 
     @pl.loop(0, 6)
     def _(i):
@@ -108,75 +111,76 @@
     out[2], out[3] = found[4], found[5]
 
 
-def stores(right, left, up, down, own):
-    return {
-        (0, 0): own.at[0],
-        (0, 1): own.at[1],
-        (1, 0): up,
-        (1, 1): right.at[1],
-        (2, 0): right.at[0],
-        (2, 1): left.at[0],
-        (3, 0): left.at[1],
-        (3, 1): down,
-    }
-
-
-ORDER = ((2, 0), (1, 1), (2, 1), (3, 0), (1, 0), (3, 1), (0, 0), (0, 1))
+FIRST = (((2, 0), (1, 1)), ((2, 1), (3, 0)))
+REST = (((1, 0), (3, 1)), ((0, 0), (0, 1)))
 
 
 def stack(refs, lefts, rights):
     side_by_side(lefts.at[0], refs[0], refs[1])
     side_by_side(lefts.at[1], refs[4], refs[5])
     side_by_side(rights.at[0], refs[2], refs[3])
-    turned(rights.at[1], refs[2], refs[3])
-
-
-def early_kernel(device, table, *refs):
-    outs, lefts, rights = refs[6:16], refs[16], refs[17]
+    side_by_side(rights.at[1], refs[2], refs[3], turned=True)
+
+
+def early_kernel(entries, device, table, *refs):
+    outs, lefts, rights = refs[6:10], refs[10], refs[11]
     stack(refs, lefts, rights)
-    for t, j in ORDER:
-        for color in range(2):
-            index = table[device[0] * 16 + color * 8 + t * 2 + j]
-            lhs = rows_of(lefts.at[index // 4], index // 2 % 2)
-            rhs = rows_of(rights.at[color], index % 2)
-            stores(*outs[5 * color : 5 * color + 5])[t, j][...] = matmul(lhs, rhs)
-
-
-def late_kernel(device, table, diagonal, *refs):
-    outs, lefts, rights = refs[6:16], refs[16], refs[17]
+    for out in range(2):
+        for place, (t, j) in enumerate(entries[out]):
+            for color in range(2):
+                index = table[device[0] * 16 + color * 8 + t * 2 + j]
+                lhs = rows_of(lefts.at[index // 4], index // 2 % 2)
+                rhs = rows_of(rights.at[color], index % 2)
+                outs[2 * color + out][place] = matmul(lhs, rhs)
+
+
+def late_kernel(entries, device, table, *refs):
+    diagonal, outs, lefts, rights = refs[6], refs[7:11], refs[11], refs[12]
     stack(refs, lefts, rights)
     upper = (device[1] >= PLANES // 2).astype(jnp.int32)
-    for t, j in ORDER:
-        for color in range(2):
-            index = table[device[0] * 16 + color * 8 + t * 2 + j]
-            near = index < 4
-            h = jnp.where(near, index // 2, index % 2)
-            k = jnp.where(near, index % 2, (h + upper) % 2)
-            lhs = rows_of(lefts.at[index // 4], h)
-            product = matmul(lhs, rows_of(rights.at[color], k))
-            ready = diagonal[jnp.maximum(index - 6, 0) * 2 + color]
-            out = stores(*outs[5 * color : 5 * color + 5])[t, j]
-            out[...] = jnp.where(index < 6, product, ready)
+    for out in range(2):
+        for place, (t, j) in enumerate(entries[out]):
+            for color in range(2):
+                index = table[device[0] * 16 + color * 8 + t * 2 + j]
+                near = index < 4
+                h = jnp.where(near, index // 2, index % 2)
+                k = jnp.where(near, index % 2, (h + upper) % 2)
+                lhs = rows_of(lefts.at[index // 4], h)
+                product = matmul(lhs, rows_of(rights.at[color], k))
+                ready = diagonal[jnp.maximum(index - 6, 0) * 2 + color]
+                outs[2 * color + out][place] = jnp.where(index < 6, product, ready)
 
 
 def finish_kernel(device, ahead, *refs):
     ins, outs, sums = refs[:20], refs[20:28], refs[28]
-    slab = sums.shape[1] // 4
     for color in range(2):
-
-        @pl.loop(0, 4)
-        def _(i):
-            rows = pl.ds(pl.multiple_of(i * slab, slab), slab)
-            for group in range(2):
-                own, right, left, right2, left2 = ins[10 * color + 5 * group :][:5]
-                sums[2 * group, rows] = own[0, rows] + right2[rows] + left[1, rows]
-                sums[2 * group + 1, rows] = own[1, rows] + right[1, rows] + left2[rows]
-
-        @pl.loop(0, 4)
-        def _(i):
-            rows = pl.ds(pl.multiple_of(i * slab, slab), slab)
-            for t in range(SIDE):
-                outs[4 * color + t][rows] = sums[ahead[device[0] * 8 + color * 4 + t], rows]
+        for group in range(2):
+            own, right, left, right2, left2 = ins[10 * color + 5 * group :][:5]
+            sums[2 * group] = own[0] + right2[...] + left[0]
+            sums[2 * group + 1] = own[1] + right[0] + left2[...]
+        for t in range(SIDE):
+            outs[4 * color + t][...] = sums[ahead[device[0] * 8 + color * 4 + t]]
+
+
+def finish(device, ahead, parts):
+    slabs = 4
+    quarter = parts[0].shape[-1]
+    slab = quarter // slabs
+    smem = pl.BlockSpec(memory_space=pltpu.SMEM)
+    one = pl.BlockSpec((slab, quarter), lambda i: (i, 0))
+    second = pl.BlockSpec((1, slab, quarter), lambda i: (1, i, 0))
+    both = pl.BlockSpec((2, slab, quarter), lambda i: (0, i, 0))
+    return pl.pallas_call(
+        finish_kernel,
+        grid=(slabs,),
+        out_shape=[jax.ShapeDtypeStruct((quarter, quarter), jnp.float32)] * 8,
+        in_specs=[smem, smem] + 4 * [both, second, second, one, one],
+        out_specs=[one] * 8,
+        scratch_shapes=[pltpu.VMEM((4, slab, quarter), jnp.float32)],
+        cost_estimate=pl.CostEstimate(
+            flops=16 * quarter * quarter, bytes_accessed=128 * quarter * quarter, transcendentals=0
+        ),
+    )(device, ahead, *parts)
 
 
 def mirror_kernel(device, flags, *refs):
@@ -224,15 +228,17 @@
     return lax.ppermute(value, "col", [(c, (c + step) % PLANES) for c in range(PLANES)])
 
 
-def ring_start(outs, shift):
-    right, left, up, down, own = outs
-    right, left = shift(right, 1), shift(left, -1)
-    return own, right, left, up + right[0], down + left[0]
-
-
-def ring_end(parts, shift):
-    own, right, left, up, down = parts
-    return own, right, left, shift(up, 1), shift(down, -1)
+def ring_start(right, left, shift):
+    return shift(right, 1), shift(left, -1)
+
+
+def ring_sums(received, rest):
+    right, left = received
+    return rest[0] + right[0], rest[1] + left[0]
+
+
+def ring_end(own, received, sums, shift):
+    return own, *received, shift(sums[0], 1), shift(sums[1], -1)
 
 
 def direct(outs, shift):
@@ -275,50 +281,48 @@
     first, second, early, late, ahead, flags, half = tables()
     device_index = row_index * PLANES + column_index
     device = jnp.stack([device_index, column_index]).astype(jnp.int32)
-    here = samples[:, 0, :], samples[:, 1, :]
-    antennas, times = here[0].shape
+    real, later = lax.optimization_barrier((samples[:, 0, :], samples))
+    here = real, later[:, 1, :]
+    antennas, times = real.shape
     quarter = antennas // 2
     product = 4 * quarter * quarter * times
-    stacks = [pltpu.VMEM((2, antennas, 2 * times), here[0].dtype)] * 2
+    stacks = [pltpu.VMEM((2, antennas, 2 * times), real.dtype)] * 2
     found = stacks[0], pltpu.VMEM((6, quarter, quarter), jnp.float32)
     near = [(shift_z(part, -1), shift_z(part, 1)) for part in here]
+    gain, near[0] = lax.optimization_barrier((gain, near[0]))
     far = [(shift_z(above, -1), shift_z(below, 1)) for above, below in near]
     above, below = zip(*near)
     above2, below2 = zip(*far)
-    gain, *free = lax.optimization_barrier((gain, *here))
-    (diagonal,) = kernel_call(diagonal_kernel, (), free, [(4, quarter, quarter)], 6 * product, found)
-    *below, diagonal = lax.optimization_barrier((*below, diagonal))
-    shapes = 2 * ([(2, quarter, quarter)] * 2 + [(quarter, quarter)] * 2 + [(2, quarter, quarter)])
-    outs = kernel_call(
-        early_kernel,
-        (device, jnp.asarray(early.reshape(-1))),
-        (*here, *above, *below),
-        shapes,
-        16 * product,
-        stacks,
-    )
-    along_x, along_y = ring_start(outs[:5], shift_x), ring_start(outs[5:], shift_y)
-    sums = along_x[3:] + along_y[3:]
-    *above2, first_below2, second_below2 = lax.optimization_barrier((*sums, *above2, *below2))[4:]
-    early_parts = ring_end(along_x, shift_x), ring_end(along_y, shift_y)
-    outs = kernel_call(
-        late_kernel,
-        (device, jnp.asarray(late.reshape(-1))),
-        (diagonal, *below, *above2, first_below2, second_below2),
-        shapes,
-        12 * product,
-        stacks,
-    )
-    late_parts = [
-        ring_end(ring_start(part, shift), shift)
-        for part, shift in ((outs[:5], shift_x), (outs[5:], shift_y))
-    ]
-    outs = kernel_call(
-        finish_kernel,
-        (device, jnp.asarray(ahead.reshape(-1))),
+    shapes = [(2, quarter, quarter)] * 4
+    axes = (shift_x, shift_y)
+
+    def chunks(kernel, entries, table, blocks, products):
+        return kernel_call(
+            functools.partial(kernel, entries),
+            (device, jnp.asarray(table.reshape(-1))),
+            blocks,
+            shapes,
+            products * product,
+            stacks,
+        )
+
+    blocks = *here, *above, *below
+    first_outs = chunks(early_kernel, FIRST, early, blocks, 8)
+    received = [ring_start(*first_outs[2 * i : 2 * i + 2], axes[i]) for i in range(2)]
+    outs = chunks(early_kernel, REST, early, blocks, 8)
+    (diagonal,) = kernel_call(diagonal_kernel, (), here, [(4, quarter, quarter)], 6 * product, found)
+    sums = [ring_sums(received[i], outs[2 * i]) for i in range(2)]
+    early_parts = [ring_end(outs[2 * i + 1], received[i], sums[i], axes[i]) for i in range(2)]
+    _, blocks = lax.optimization_barrier((sums, (*below, *above2, *below2, diagonal)))
+    first_outs = chunks(late_kernel, FIRST, late, blocks, 8)
+    received = [ring_start(*first_outs[2 * i : 2 * i + 2], axes[i]) for i in range(2)]
+    outs = chunks(late_kernel, REST, late, blocks, 8)
+    sums = [ring_sums(received[i], outs[2 * i]) for i in range(2)]
+    late_parts = [ring_end(outs[2 * i + 1], received[i], sums[i], axes[i]) for i in range(2)]
+    outs = finish(
+        device,
+        jnp.asarray(ahead.reshape(-1)),
         early_parts[0] + late_parts[0] + early_parts[1] + late_parts[1],
-        [(quarter, quarter)] * 8,
-        scratch=(pltpu.VMEM((4, quarter, quarter), jnp.float32),),
     )
     parts = direct(outs[:4], shift_y) + direct(outs[4:], shift_x)
     one, two = kernel_call(

time: 244 us -> 224 us (0.918)
  blocking collectives: 28.8 us -> 19.8 us
  starting transfers between devices: 78.1 us -> 69.6 us
  waiting for transfers between devices: 88.1 us -> 80.3 us
  Pallas kernels: 25.1 us -> 31.4 us
  other arithmetic: 5.4 us -> 8.32 us
  local copies, waits for them, and re-layouts: 14.4 us -> 11.5 us
    ppermute x1, waiting for transfers between devices: 3.41 us -> 19.5 us  [vis_tiles(): two = lax.ppermute(two, ('row', 'col'), second)]
    ppermute x11, waiting for transfers between devices: 23.2 us -> 9.26 us  [shift_y(): return lax.ppermute(value, 'row', pairs)]
    ppermute x1, starting transfers between devices: 12.7 us -> 1.91 us  [vis_tiles(): two = lax.ppermute(two, ('row', 'col'), second)]
    all_to_all x1, blocking collectives: 18.6 us -> 9.53 us  [exchange(): return lax.all_to_all(copies, axis, 0, 0)]
    ppermute x11, starting transfers between devices: 9.16 us -> 15.4 us  [shift_x(): return lax.ppermute(value, 'row', pairs)]
    ppermute x8, waiting for transfers between devices: 14 us -> 8.58 us  [shift_z(): lax.ppermute(value, 'col', [(c, (c + step) % PLANES) for c in range(PLANE...]
    ppermute x8, starting transfers between devices: 12.8 us -> 7.47 us  [shift_z(): lax.ppermute(value, 'col', [(c, (c + step) % PLANES) for c in range(PLANE...]
    ppermute x1, starting transfers between devices: 1.92 us -> 6.93 us  [vis_tiles(): one = lax.ppermute(one, ('row', 'col'), first)]
  transfers between devices with their start and end apart: 35 -> 35, of which waited for: 19 -> 20; matrix products, arithmetic and copies ran while one was open for 2% -> 4% of each run, Pallas kernels for 2% -> 6%
where the time goes in v4:
time: 224 us; the launch traced here: 222 us
  waiting for transfers between devices  80.3 us (36%)
  starting transfers between devices  69.6 us (31%)
  Pallas kernels  31.4 us (14%)
  blocking collectives  19.8 us (9%)
  local copies, waits for them, and re-layouts  11.5 us (5%)
  other arithmetic  8.32 us (4%)
    pallas_call x6, Pallas kernels, kernel_call(): pl.pallas_call(kernel, out_shape=shapes, in_specs=[smem] * len(scalars) +...  26.8 us
    ppermute x1, waiting for transfers between devices, vis_tiles(): two = lax.ppermute(two, ('row', 'col'), second)  19.5 us
    all_to_all x2, starting transfers between devices, exchange(): return lax.all_to_all(copies, axis, 0, 0)  16.4 us
    ppermute x1, waiting for transfers between devices, starting_gains(): share = lax.ppermute(initial_gains, ('row', 'col'), pairs)  15.9 us
    ppermute x11, starting transfers between devices, shift_x(): return lax.ppermute(value, 'row', pairs)  15.4 us
    all_to_all x2, waiting for transfers between devices, exchange(): return lax.all_to_all(copies, axis, 0, 0)  14.9 us
    ppermute x11, starting transfers between devices, shift_y(): return lax.ppermute(value, 'row', pairs)  13.5 us
    ppermute x11, waiting for transfers between devices, shift_x(): return lax.ppermute(value, 'row', pairs)  12.2 us
  transfers between devices with their start and end apart: 35, of which 20 were waited for; matrix products, arithmetic and copies ran while one was open for 4% of the time, Pallas kernels for 6%

profile of v4, /device:TPU:64, one launch (start us, length us, event | category | flops | bytes accessed | tf_op | source)
XLA Modules:
  0.0 222.0 jit_solution(10221336853136198824)
XLA Ops:
  1.6 1.9 collective-permute-start.2
  3.8 3.2 %collective-permute-start.4 = (bf16[512,512]{1,0:T(8,128)(2,1)S(1)}, bf16[512,512]{1,0:T(8,128)(2,1)S(1)}, u32[]{:S(2)}, u32[]{:S(2)}) collective-permute-start(bf16[512,512]{1,0:T(8,128)(2,1)S(1)} %slice_bitcast_fusion.refs_1_.imag), channel_id=1, source_target_pairs={{0,2},{2,4},{4,6},{6,8},{8,10},{10,12},{12,14},{14,0},{1,3},{3,5},... | collective-permute-start | bytes 1572872 | tf_op jit(solution)/shard_map/ppermute | solution.py:228
  7.0 8.0 %collective-permute-start = (f32[2,32]{1,0:T(2,128)S(1)}, f32[2,32]{1,0:T(2,128)S(1)}, u32[]{:S(2)}, u32[]{:S(2)}) collective-permute-start(f32[2,32]{1,0:T(2,128)S(1)} %copy-done.35), channel_id=1, source_target_pairs={{0,0},{2,16},{4,32},{6,48},{8,64},{10,80},{12,96},{14,112},{16,128... | collective-permute-start | bytes 776 | tf_op jit(solution)/shard_map/ppermute | solution.py:351
  15.1 15.9 %collective-permute-done = f32[2,32]{1,0:T(2,128)S(1)} collective-permute-done((f32[2,32]{1,0:T(2,128)S(1)}, f32[2,32]{1,0:T(2,128)S(1)}, u32[]{:S(2)}, u32[]{:S(2)}) %collective-permute-start) | collective-permute-done | bytes 288 | tf_op jit(solution)/shard_map/ppermute | solution.py:351
  31.6 9.5 %all-to-all-start = ((f32[16,2,32]{2,1,0:T(2,128)}), f32[16,2,32]{2,1,0:T(2,128)S(1)}, u32[]{:S(2)}, u32[]{:S(2)}) async-start(f32[16,2,32]{2,1,0:T(2,128)} %broadcast_in_dim.8), calls=%async_computation | async-start | bytes 32768 | tf_op jit(solution)/shard_map/all_to_all | solution.py:251
  41.7 6.9 %all-to-all-done = f32[16,2,32]{2,1,0:T(2,128)S(1)} async-done(((f32[16,2,32]{2,1,0:T(2,128)}), f32[16,2,32]{2,1,0:T(2,128)S(1)}, u32[]{:S(2)}, u32[]{:S(2)}) %all-to-all-start) | async-done | bytes 4128 | tf_op jit(solution)/shard_map/all_to_all | solution.py:251
  50.5 4.7 %shard_map.101 = (f32[2,256,256]{2,1,0:T(8,128)}, f32[2,256,256]{2,1,0:T(8,128)}, f32[2,256,256]{2,1,0:T(8,128)}, f32[2,256,256]{2,1,0:T(8,128)}) custom-call(s32[2]{0:T(128)} %pad_add_fusion.device, s32[2048]{0:T(1024)} %constant.45.clone.table, bf16[512,512]{1,0:T(8,128)(2,1)} %bitcast.76, bf16[512,512]{1,0:T(8,128)(2,1)} %copy-done.17, ...), custom_call_target="tpu_custom_call" | custom-call | flops 1073741824 | bytes 5242880 | tf_op jit(solution)/shard_map/pallas_call | solution.py:203
  57.9 2.7 %collective-permute-start.6 = (f32[2,256,256]{2,1,0:T(8,128)}, f32[2,256,256]{2,1,0:T(8,128)}, u32[]{:S(2)}, u32[]{:S(2)}) collective-permute-start(f32[2,256,256]{2,1,0:T(8,128)} %get-tuple-element.49), channel_id=1, source_target_pairs={{0,48},{16,0},{32,16},{48,32},{64,112},{80,64},{96,80},{112,96},{1... | collective-permute-start | bytes 1572872 | tf_op jit(solution)/shard_map/ppermute | solution.py:217
  60.5 4.5 %shard_map.102.refs_6_ = f32[4,256,256]{2,1,0:T(8,128)} custom-call(bf16[512,512]{1,0:T(8,128)(2,1)} %bitcast.77, bf16[512,512]{1,0:T(8,128)(2,1)} %copy-done.17), custom_call_target="tpu_custom_call" | custom-call | flops 805306368 | bytes 2097152 | tf_op jit(solution)/shard_map/pallas_call | solution.py:203
  70.5 4.7 %shard_map.100 = (f32[2,256,256]{2,1,0:T(8,128)}, f32[2,256,256]{2,1,0:T(8,128)}, f32[2,256,256]{2,1,0:T(8,128)}, f32[2,256,256]{2,1,0:T(8,128)}) custom-call(s32[2]{0:T(128)} %pad_add_fusion.device, s32[2048]{0:T(1024)} %constant.45.clone.table, bf16[512,512]{1,0:T(8,128)(2,1)} %bitcast.78, bf16[512,512]{1,0:T(8,128)(2,1)} %copy-done.17, ...), custom_call_target="tpu_custom_call" | custom-call | flops 1073741824 | bytes 5242880 | tf_op jit(solution)/shard_map/pallas_call | solution.py:203
  75.2 2.1 fusion.7
  81.4 4.6 %collective-permute-done.14.refs_5_ = bf16[512,512]{1,0:T(8,128)(2,1)S(1)} collective-permute-done((bf16[512,512]{1,0:T(8,128)(2,1)S(1)}, bf16[512,512]{1,0:T(8,128)(2,1)S(1)}, u32[]{:S(2)}, u32[]{:S(2)}) %collective-permute-start.14) | collective-permute-done | bytes 524320 | tf_op jit(solution)/shard_map/ppermute | solution.py:228
  88.6 5.0 %shard_map.104 = (f32[2,256,256]{2,1,0:T(8,128)}, f32[2,256,256]{2,1,0:T(8,128)}, f32[2,256,256]{2,1,0:T(8,128)}, f32[2,256,256]{2,1,0:T(8,128)}) custom-call(s32[2]{0:T(128)} %pad_add_fusion.device, s32[2048]{0:T(1024)} %constant.46.clone.table, bf16[512,512]{1,0:T(8,128)(2,1)} %copy-done.1, bf16[512,512]{1,0:T(8,128)(2,1)} %copy-done.3, ...), custom_call_target="tpu_custom_call" | custom-call | flops 1073741824 | bytes 6291456 | tf_op jit(solution)/shard_map/pallas_call | solution.py:203
  94.1 2.7 %collective-permute-start.22 = (f32[2,256,256]{2,1,0:T(8,128)}, f32[2,256,256]{2,1,0:T(8,128)S(1)}, u32[]{:S(2)}, u32[]{:S(2)}) collective-permute-start(f32[2,256,256]{2,1,0:T(8,128)} %get-tuple-element.68), channel_id=1, source_target_pairs={{0,192},{16,208},{32,224},{48,240},{64,0},{80,16},{96,32},{112,48}... | collective-permute-start | bytes 1572872 | tf_op jit(solution)/shard_map/ppermute | solution.py:224
  97.3 2.7 %collective-permute-start.16 = (f32[2,256,256]{2,1,0:T(8,128)}, f32[2,256,256]{2,1,0:T(8,128)S(1)}, u32[]{:S(2)}, u32[]{:S(2)}) collective-permute-start(f32[2,256,256]{2,1,0:T(8,128)} %get-tuple-element.63), channel_id=1, source_target_pairs={{0,48},{16,0},{32,16},{48,32},{64,112},{80,64},{96,80},{112,96},{1... | collective-permute-start | bytes 1572872 | tf_op jit(solution)/shard_map/ppermute | solution.py:217
  100.0 5.0 %shard_map.103 = (f32[2,256,256]{2,1,0:T(8,128)}, f32[2,256,256]{2,1,0:T(8,128)}, f32[2,256,256]{2,1,0:T(8,128)}, f32[2,256,256]{2,1,0:T(8,128)}) custom-call(s32[2]{0:T(128)} %pad_add_fusion.device, s32[2048]{0:T(1024)} %constant.46.clone.table, bf16[512,512]{1,0:T(8,128)(2,1)} %copy-done.1, bf16[512,512]{1,0:T(8,128)(2,1)} %copy-done.3, ...), custom_call_target="tpu_custom_call" | custom-call | flops 1073741824 | bytes 6291456 | tf_op jit(solution)/shard_map/pallas_call | solution.py:203
  110.3 2.6 %collective-permute-start.8 = (f32[256,256]{1,0:T(8,128)S(1)}, f32[256,256]{1,0:T(8,128)S(1)}, u32[]{:S(2)}, u32[]{:S(2)}) collective-permute-start(f32[256,256]{1,0:T(8,128)S(1)} %get-tuple-element.105), channel_id=1, source_target_pairs={{0,48},{16,0},{32,16},{48,32},{64,112},{80,64},{96,80},{112,96},{1... | collective-permute-start | bytes 786440 | tf_op jit(solution)/shard_map/ppermute | solution.py:217
  113.7 2.6 %collective-permute-start.24 = (f32[256,256]{1,0:T(8,128)S(1)}, f32[256,256]{1,0:T(8,128)S(1)}, u32[]{:S(2)}, u32[]{:S(2)}) collective-permute-start(f32[256,256]{1,0:T(8,128)S(1)} %get-tuple-element.99), channel_id=1, source_target_pairs={{0,192},{16,208},{32,224},{48,240},{64,0},{80,16},{96,32},{112,48}... | collective-permute-start | bytes 786440 | tf_op jit(solution)/shard_map/ppermute | solution.py:224
  120.5 3.4 %collective-permute-done.17.refs_8_ = f32[256,256]{1,0:T(8,128)S(1)} collective-permute-done((f32[256,256]{1,0:T(8,128)S(1)}, f32[256,256]{1,0:T(8,128)S(1)}, u32[]{:S(2)}, u32[]{:S(2)}) %collective-permute-start.17) | collective-permute-done | bytes 262176 | tf_op jit(solution)/shard_map/ppermute | solution.py:217
  125.3 4.6 %shard_map.105 = (f32[256,256]{1,0:T(8,128)}, f32[256,256]{1,0:T(8,128)}, f32[256,256]{1,0:T(8,128)}, f32[256,256]{1,0:T(8,128)}, f32[256,256]{1,0:T(8,128)}, /*...) custom-call(s32[2]{0:T(128)} %pad_add_fusion.device, s32[1024]{0:T(1024)} %constant.47.clone.ahead, ...), custom_call_target="tpu_custom_call" | custom-call | flops 1048576 | bytes 8388608 | tf_op jit(solution)/shard_map/pallas_call | solution.py:173
  130.0 3.0 %collective-permute-start.26 = (f32[256,256]{1,0:T(8,128)}, f32[256,256]{1,0:T(8,128)S(1)}, u32[]{:S(2)}, u32[]{:S(2)}) collective-permute-start(f32[256,256]{1,0:T(8,128)} %get-tuple-element.72), channel_id=1, source_target_pairs={{0,128},{16,144},{32,160},{48,176},{64,192},{80,208},{96,224},{112... | collective-permute-start | bytes 786440 | tf_op jit(solution)/shard_map/ppermute | solution.py:224
  133.5 4.2 %collective-permute-start.29 = (f32[256,256]{1,0:T(8,128)}, f32[256,256]{1,0:T(8,128)S(1)}, u32[]{:S(2)}, u32[]{:S(2)}) collective-permute-start(f32[256,256]{1,0:T(8,128)} %get-tuple-element.76), channel_id=1, source_target_pairs={{0,32},{16,48},{32,0},{48,16},{64,96},{80,112},{96,64},{112,80},{1... | collective-permute-start | bytes 786440 | tf_op jit(solution)/shard_map/ppermute | solution.py:217
  137.7 2.9 %collective-permute-done.25.refs_1_ = f32[256,256]{1,0:T(8,128)S(1)} collective-permute-done((f32[256,256]{1,0:T(8,128)}, f32[256,256]{1,0:T(8,128)S(1)}, u32[]{:S(2)}, u32[]{:S(2)}) %collective-permute-start.25) | collective-permute-done | bytes 262176 | tf_op jit(solution)/shard_map/ppermute | solution.py:224
  141.5 3.5 %collective-permute-done.29.refs_6_ = f32[256,256]{1,0:T(8,128)S(1)} collective-permute-done((f32[256,256]{1,0:T(8,128)}, f32[256,256]{1,0:T(8,128)S(1)}, u32[]{:S(2)}, u32[]{:S(2)}) %collective-permute-start.29) | collective-permute-done | bytes 262176 | tf_op jit(solution)/shard_map/ppermute | solution.py:217
  145.0 2.2 collective-permute-done.30.refs_7_
  147.9 2.8 %shard_map.106 = (f32[2,256,256]{2,1,0:T(8,128)}, f32[2,256,256]{2,1,0:T(8,128)}) custom-call(s32[2]{0:T(128)} %pad_add_fusion.device, s32[256]{0:T(256)} %constant.48.clone.flags, f32[256,256]{1,0:T(8,128)} %get-tuple-element.70.refs_0_, f32[256,256]{1,0:T(8,128)} %copy-done.25, f32[256,256]{1,0:T(8,128)} %copy-done.26, f32[256,256]{1,0:T(8,128)} %copy-done.27, ...), custom_call_target="tpu_custom_call" | custom-call | bytes 3145728 | tf_op jit(solution)/shard_map/pallas_call | solution.py:203
  152.6 6.9 %collective-permute-start.32 = (f32[2,256,256]{2,1,0:T(8,128)}, f32[2,256,256]{2,1,0:T(8,128)S(1)}, u32[]{:S(2)}, u32[]{:S(2)}) collective-permute-start(f32[2,256,256]{2,1,0:T(8,128)} %get-tuple-element.79), channel_id=1, source_target_pairs={{112,2},{0,48},{32,32},{80,18},{208,226},{160,62},{128,46},{240,24... | collective-permute-start | bytes 1572872 | tf_op jit(solution)/shard_map/ppermute | solution.py:334
  162.2 19.5 %collective-permute-done.31 = f32[2,256,256]{2,1,0:T(8,128)S(1)} collective-permute-done((f32[2,256,256]{2,1,0:T(8,128)}, f32[2,256,256]{2,1,0:T(8,128)S(1)}, u32[]{:S(2)}, u32[]{:S(2)}) %collective-permute-start.31) | collective-permute-done | bytes 524320 | tf_op jit(solution)/shard_map/ppermute | solution.py:335
  182.6 9.5 %all_to_all.20 = f32[8,3,256]{2,1,0:T(4,128)S(1)} all-to-all(f32[8,3,256]{2,1,0:T(4,128)S(1)} %broadcast_in_dim.9), channel_id=1, replica_groups=mesh['row'=16,'col'=8,'chan'=2] {'col'}, dimensions={0} | all-to-all | bytes 49152 | tf_op jit(solution)/shard_map/all_to_all | solution.py:251
  193.4 6.9 %all-to-all-start.2 = ((f32[16,16,128]{2,1,0:T(8,128)}), f32[16,16,128]{2,1,0:T(8,128)S(1)}, u32[]{:S(2)}, u32[]{:S(2)}) async-start(f32[16,16,128]{2,1,0:T(8,128)} %broadcast_in_dim.22), calls=%async_computation.2 | async-start | bytes 262144 | tf_op jit(solution)/shard_map/all_to_all | solution.py:251
  200.2 8.0 %all-to-all-done.2 = f32[16,16,128]{2,1,0:T(8,128)S(1)} async-done(((f32[16,16,128]{2,1,0:T(8,128)}), f32[16,16,128]{2,1,0:T(8,128)S(1)}, u32[]{:S(2)}, u32[]{:S(2)}) %all-to-all-start.2) | async-done | bytes 131104 | tf_op jit(solution)/shard_map/all_to_all | solution.py:251
  211.1 10.3 %all_to_all.21 = f32[8,3,32]{2,1,0:T(4,128)S(1)} all-to-all(f32[8,3,32]{2,1,0:T(4,128)S(1)} %maximum_bitcast_fusion), channel_id=1, replica_groups=mesh['row'=16,'col'=8,'chan'=2] {'col'}, dimensions={0} | all-to-all | bytes 6144 | tf_op jit(solution)/shard_map/all_to_all | solution.py:396
  (177 shorter events, 43.8 us)
Async XLA Ops:
  1.4 47.3 %collective-permute-start.1 = (bf16[512,512]{1,0:T(8,128)(2,1)S(1)}, bf16[512,512]{1,0:T(8,128)(2,1)}, u32[]{:S(2)}, u32[]{:S(2)}) collective-permute-start(bf16[512,512]{1,0:T(8,128)(2,1)S(1)} %bitcast.74), channel_id=1, source_target_pairs={{0,14},{2,0},{4,2},{6,4},{8,6},{10,8},{12,10},{14,12},{1,15},{3,1}... | collective-permute-start | bytes 1572872 | tf_op jit(solution)/shard_map/ppermute | solution.py:228
  1.6 47.1 %collective-permute-start.2 = (bf16[512,512]{1,0:T(8,128)(2,1)S(1)}, bf16[512,512]{1,0:T(8,128)(2,1)S(1)}, u32[]{:S(2)}, u32[]{:S(2)}) collective-permute-start(bf16[512,512]{1,0:T(8,128)(2,1)S(1)} %bitcast.75), channel_id=1, source_target_pairs={{0,2},{2,4},{4,6},{6,8},{8,10},{10,12},{12,14},{14,0},{1,3},{3,5},... | collective-permute-start | bytes 1572872 | tf_op jit(solution)/shard_map/ppermute | solution.py:228
  3.8 45.0 %collective-permute-start.4 = (bf16[512,512]{1,0:T(8,128)(2,1)S(1)}, bf16[512,512]{1,0:T(8,128)(2,1)S(1)}, u32[]{:S(2)}, u32[]{:S(2)}) collective-permute-start(bf16[512,512]{1,0:T(8,128)(2,1)S(1)} %slice_bitcast_fusion.refs_1_.imag), channel_id=1, source_target_pairs={{0,2},{2,4},{4,6},{6,8},{8,10},{10,12},{12,14},{14,0},{1,3},{3,5},... | collective-permute-start | bytes 1572872 | tf_op jit(solution)/shard_map/ppermute | solution.py:228
  7.0 41.8 %collective-permute-start.3 = (bf16[512,512]{1,0:T(8,128)(2,1)S(1)}, bf16[512,512]{1,0:T(8,128)(2,1)S(1)}, u32[]{:S(2)}, u32[]{:S(2)}) collective-permute-start(bf16[512,512]{1,0:T(8,128)(2,1)S(1)} %slice_bitcast_fusion.refs_1_.imag), channel_id=1, source_target_pairs={{0,14},{2,0},{4,2},{6,4},{8,6},{10,8},{12,10},{14,12},{1,15},{3,1}... | collective-permute-start | bytes 1572872 | tf_op jit(solution)/shard_map/ppermute | solution.py:228
  7.0 23.9 %collective-permute-start = (f32[2,32]{1,0:T(2,128)S(1)}, f32[2,32]{1,0:T(2,128)S(1)}, u32[]{:S(2)}, u32[]{:S(2)}) collective-permute-start(f32[2,32]{1,0:T(2,128)S(1)} %copy-done.35), channel_id=1, source_target_pairs={{0,0},{2,16},{4,32},{6,48},{8,64},{10,80},{12,96},{14,112},{16,128... | collective-permute-start | bytes 776 | tf_op jit(solution)/shard_map/ppermute | solution.py:351
  31.6 17.1 %all-to-all-start = ((f32[16,2,32]{2,1,0:T(2,128)}), f32[16,2,32]{2,1,0:T(2,128)S(1)}, u32[]{:S(2)}, u32[]{:S(2)}) async-start(f32[16,2,32]{2,1,0:T(2,128)} %broadcast_in_dim.8), calls=%async_computation | async-start | bytes 32768 | tf_op jit(solution)/shard_map/all_to_all | solution.py:251
  55.3 11.1 %collective-permute-start.10 = (f32[2,256,256]{2,1,0:T(8,128)}, f32[2,256,256]{2,1,0:T(8,128)}, u32[]{:S(2)}, u32[]{:S(2)}) collective-permute-start(f32[2,256,256]{2,1,0:T(8,128)} %get-tuple-element.53), channel_id=1, source_target_pairs={{0,192},{16,208},{32,224},{48,240},{64,0},{80,16},{96,32},{112,48}... | collective-permute-start | bytes 1572872 | tf_op jit(solution)/shard_map/ppermute | solution.py:224
  56.4 12.0 %collective-permute-start.9 = (f32[2,256,256]{2,1,0:T(8,128)}, f32[2,256,256]{2,1,0:T(8,128)}, u32[]{:S(2)}, u32[]{:S(2)}) collective-permute-start(f32[2,256,256]{2,1,0:T(8,128)} %get-tuple-element.52), channel_id=1, source_target_pairs={{0,64},{16,80},{32,96},{48,112},{64,128},{80,144},{96,160},{112,17... | collective-permute-start | bytes 1572872 | tf_op jit(solution)/shard_map/ppermute | solution.py:224
  57.3 11.8 %collective-permute-start.5 = (f32[2,256,256]{2,1,0:T(8,128)}, f32[2,256,256]{2,1,0:T(8,128)}, u32[]{:S(2)}, u32[]{:S(2)}) collective-permute-start(f32[2,256,256]{2,1,0:T(8,128)} %get-tuple-element.48), channel_id=1, source_target_pairs={{0,16},{16,32},{32,48},{48,0},{64,80},{80,96},{96,112},{112,64},{1... | collective-permute-start | bytes 1572872 | tf_op jit(solution)/shard_map/ppermute | solution.py:217
  57.9 19.5 %collective-permute-start.6 = (f32[2,256,256]{2,1,0:T(8,128)}, f32[2,256,256]{2,1,0:T(8,128)}, u32[]{:S(2)}, u32[]{:S(2)}) collective-permute-start(f32[2,256,256]{2,1,0:T(8,128)} %get-tuple-element.49), channel_id=1, source_target_pairs={{0,48},{16,0},{32,16},{48,32},{64,112},{80,64},{96,80},{112,96},{1... | collective-permute-start | bytes 1572872 | tf_op jit(solution)/shard_map/ppermute | solution.py:217
  65.1 14.8 %collective-permute-start.13 = (bf16[512,512]{1,0:T(8,128)(2,1)S(1)}, bf16[512,512]{1,0:T(8,128)(2,1)S(1)}, u32[]{:S(2)}, u32[]{:S(2)}) collective-permute-start(bf16[512,512]{1,0:T(8,128)(2,1)S(1)} %copy-done.2), channel_id=1, source_target_pairs={{0,2},{2,4},{4,6},{6,8},{8,10},{10,12},{12,14},{14,0},{1,3},{3,5},... | collective-permute-start | bytes 1572872 | tf_op jit(solution)/shard_map/ppermute | solution.py:228
  66.4 15.0 %collective-permute-start.11 = (bf16[512,512]{1,0:T(8,128)(2,1)}, bf16[512,512]{1,0:T(8,128)(2,1)S(1)}, u32[]{:S(2)}, u32[]{:S(2)}) collective-permute-start(bf16[512,512]{1,0:T(8,128)(2,1)} %collective-permute-done.1.refs_2_), channel_id=1, source_target_pairs={{0,14},{2,0},{4,2},{6,4},{8,6},{10,8},{12,10},{14,12},{1,15},{3,1}... | collective-permute-start | bytes 1572872 | tf_op jit(solution)/shard_map/ppermute | solution.py:228
  68.5 17.5 %collective-permute-start.14 = (bf16[512,512]{1,0:T(8,128)(2,1)S(1)}, bf16[512,512]{1,0:T(8,128)(2,1)S(1)}, u32[]{:S(2)}, u32[]{:S(2)}) collective-permute-start(bf16[512,512]{1,0:T(8,128)(2,1)S(1)} %copy-done.4), channel_id=1, source_target_pairs={{0,2},{2,4},{4,6},{6,8},{8,10},{10,12},{12,14},{14,0},{1,3},{3,5},... | collective-permute-start | bytes 1572872 | tf_op jit(solution)/shard_map/ppermute | solution.py:228
  69.1 18.7 %collective-permute-start.12 = (bf16[512,512]{1,0:T(8,128)(2,1)}, bf16[512,512]{1,0:T(8,128)(2,1)S(1)}, u32[]{:S(2)}, u32[]{:S(2)}) collective-permute-start(bf16[512,512]{1,0:T(8,128)(2,1)} %copy-done.34), channel_id=1, source_target_pairs={{0,14},{2,0},{4,2},{6,4},{8,6},{10,8},{12,10},{14,12},{1,15},{3,1}... | collective-permute-start | bytes 1572872 | tf_op jit(solution)/shard_map/ppermute | solution.py:228
  93.5 13.3 %collective-permute-start.21 = (f32[2,256,256]{2,1,0:T(8,128)}, f32[2,256,256]{2,1,0:T(8,128)S(1)}, u32[]{:S(2)}, u32[]{:S(2)}) collective-permute-start(f32[2,256,256]{2,1,0:T(8,128)} %get-tuple-element.67), channel_id=1, source_target_pairs={{0,64},{16,80},{32,96},{48,112},{64,128},{80,144},{96,160},{112,17... | collective-permute-start | bytes 1572872 | tf_op jit(solution)/shard_map/ppermute | solution.py:224
  94.1 14.3 %collective-permute-start.22 = (f32[2,256,256]{2,1,0:T(8,128)}, f32[2,256,256]{2,1,0:T(8,128)S(1)}, u32[]{:S(2)}, u32[]{:S(2)}) collective-permute-start(f32[2,256,256]{2,1,0:T(8,128)} %get-tuple-element.68), channel_id=1, source_target_pairs={{0,192},{16,208},{32,224},{48,240},{64,0},{80,16},{96,32},{112,48}... | collective-permute-start | bytes 1572872 | tf_op jit(solution)/shard_map/ppermute | solution.py:224
  96.8 13.6 %collective-permute-start.15 = (f32[2,256,256]{2,1,0:T(8,128)}, f32[2,256,256]{2,1,0:T(8,128)S(1)}, u32[]{:S(2)}, u32[]{:S(2)}) collective-permute-start(f32[2,256,256]{2,1,0:T(8,128)} %get-tuple-element.62), channel_id=1, source_target_pairs={{0,16},{16,32},{32,48},{48,0},{64,80},{80,96},{96,112},{112,64},{1... | collective-permute-start | bytes 1572872 | tf_op jit(solution)/shard_map/ppermute | solution.py:217
  97.3 15.6 %collective-permute-start.16 = (f32[2,256,256]{2,1,0:T(8,128)}, f32[2,256,256]{2,1,0:T(8,128)S(1)}, u32[]{:S(2)}, u32[]{:S(2)}) collective-permute-start(f32[2,256,256]{2,1,0:T(8,128)} %get-tuple-element.63), channel_id=1, source_target_pairs={{0,48},{16,0},{32,16},{48,32},{64,112},{80,64},{96,80},{112,96},{1... | collective-permute-start | bytes 1572872 | tf_op jit(solution)/shard_map/ppermute | solution.py:217
  100.0 13.7 %collective-permute-start.19 = (f32[256,256]{1,0:T(8,128)}, f32[256,256]{1,0:T(8,128)S(1)}, u32[]{:S(2)}, u32[]{:S(2)}) collective-permute-start(f32[256,256]{1,0:T(8,128)} %get-tuple-element.104), channel_id=1, source_target_pairs={{0,64},{16,80},{32,96},{48,112},{64,128},{80,144},{96,160},{112,17... | collective-permute-start | bytes 786440 | tf_op jit(solution)/shard_map/ppermute | solution.py:224
  106.8 9.5 %collective-permute-start.20 = (f32[256,256]{1,0:T(8,128)}, f32[256,256]{1,0:T(8,128)S(1)}, u32[]{:S(2)}, u32[]{:S(2)}) collective-permute-start(f32[256,256]{1,0:T(8,128)} %get-tuple-element.103), channel_id=1, source_target_pairs={{0,192},{16,208},{32,224},{48,240},{64,0},{80,16},{96,32},{112,48}... | collective-permute-start | bytes 786440 | tf_op jit(solution)/shard_map/ppermute | solution.py:224
  108.3 9.9 %collective-permute-start.7 = (f32[256,256]{1,0:T(8,128)S(1)}, f32[256,256]{1,0:T(8,128)S(1)}, u32[]{:S(2)}, u32[]{:S(2)}) collective-permute-start(f32[256,256]{1,0:T(8,128)S(1)} %copy-done.32), channel_id=1, source_target_pairs={{0,16},{16,32},{32,48},{48,0},{64,80},{80,96},{96,112},{112,64},{1... | collective-permute-start | bytes 786440 | tf_op jit(solution)/shard_map/ppermute | solution.py:217
  110.3 9.3 %collective-permute-start.8 = (f32[256,256]{1,0:T(8,128)S(1)}, f32[256,256]{1,0:T(8,128)S(1)}, u32[]{:S(2)}, u32[]{:S(2)}) collective-permute-start(f32[256,256]{1,0:T(8,128)S(1)} %get-tuple-element.105), channel_id=1, source_target_pairs={{0,48},{16,0},{32,16},{48,32},{64,112},{80,64},{96,80},{112,96},{1... | collective-permute-start | bytes 786440 | tf_op jit(solution)/shard_map/ppermute | solution.py:217
  112.9 7.6 %collective-permute-start.23 = (f32[256,256]{1,0:T(8,128)S(1)}, f32[256,256]{1,0:T(8,128)S(1)}, u32[]{:S(2)}, u32[]{:S(2)}) collective-permute-start(f32[256,256]{1,0:T(8,128)S(1)} %get-tuple-element.100), channel_id=1, source_target_pairs={{0,64},{16,80},{32,96},{48,112},{64,128},{80,144},{96,160},{112,17... | collective-permute-start | bytes 786440 | tf_op jit(solution)/shard_map/ppermute | solution.py:224
  116.4 7.6 %collective-permute-start.17 = (f32[256,256]{1,0:T(8,128)S(1)}, f32[256,256]{1,0:T(8,128)S(1)}, u32[]{:S(2)}, u32[]{:S(2)}) collective-permute-start(f32[256,256]{1,0:T(8,128)S(1)} %get-tuple-element.102), channel_id=1, source_target_pairs={{0,16},{16,32},{32,48},{48,0},{64,80},{80,96},{96,112},{112,64},{1... | collective-permute-start | bytes 786440 | tf_op jit(solution)/shard_map/ppermute | solution.py:217
  129.9 10.7 %collective-permute-start.25 = (f32[256,256]{1,0:T(8,128)}, f32[256,256]{1,0:T(8,128)S(1)}, u32[]{:S(2)}, u32[]{:S(2)}) collective-permute-start(f32[256,256]{1,0:T(8,128)} %get-tuple-element.71), channel_id=1, source_target_pairs={{0,64},{16,80},{32,96},{48,112},{64,128},{80,144},{96,160},{112,17... | collective-permute-start | bytes 786440 | tf_op jit(solution)/shard_map/ppermute | solution.py:224
  130.0 10.6 %collective-permute-start.26 = (f32[256,256]{1,0:T(8,128)}, f32[256,256]{1,0:T(8,128)S(1)}, u32[]{:S(2)}, u32[]{:S(2)}) collective-permute-start(f32[256,256]{1,0:T(8,128)} %get-tuple-element.72), channel_id=1, source_target_pairs={{0,128},{16,144},{32,160},{48,176},{64,192},{80,208},{96,224},{112... | collective-permute-start | bytes 786440 | tf_op jit(solution)/shard_map/ppermute | solution.py:224
  133.0 8.5 %collective-permute-start.27 = (f32[256,256]{1,0:T(8,128)}, f32[256,256]{1,0:T(8,128)S(1)}, u32[]{:S(2)}, u32[]{:S(2)}) collective-permute-start(f32[256,256]{1,0:T(8,128)} %get-tuple-element.73), channel_id=1, source_target_pairs={{0,192},{16,208},{32,224},{48,240},{64,0},{80,16},{96,32},{112,48}... | collective-permute-start | bytes 786440 | tf_op jit(solution)/shard_map/ppermute | solution.py:224
  133.5 8.0 %collective-permute-start.28 = (f32[256,256]{1,0:T(8,128)}, f32[256,256]{1,0:T(8,128)S(1)}, u32[]{:S(2)}, u32[]{:S(2)}) collective-permute-start(f32[256,256]{1,0:T(8,128)} %get-tuple-element.75), channel_id=1, source_target_pairs={{0,16},{16,32},{32,48},{48,0},{64,80},{80,96},{96,112},{112,64},{1... | collective-permute-start | bytes 786440 | tf_op jit(solution)/shard_map/ppermute | solution.py:217
  133.5 11.5 %collective-permute-start.29 = (f32[256,256]{1,0:T(8,128)}, f32[256,256]{1,0:T(8,128)S(1)}, u32[]{:S(2)}, u32[]{:S(2)}) collective-permute-start(f32[256,256]{1,0:T(8,128)} %get-tuple-element.76), channel_id=1, source_target_pairs={{0,32},{16,48},{32,0},{48,16},{64,96},{80,112},{96,64},{112,80},{1... | collective-permute-start | bytes 786440 | tf_op jit(solution)/shard_map/ppermute | solution.py:217
  150.7 30.9 %collective-permute-start.31 = (f32[2,256,256]{2,1,0:T(8,128)}, f32[2,256,256]{2,1,0:T(8,128)S(1)}, u32[]{:S(2)}, u32[]{:S(2)}) collective-permute-start(f32[2,256,256]{2,1,0:T(8,128)} %get-tuple-element.78), channel_id=1, source_target_pairs={{112,32},{0,2},{32,18},{80,48},{208,46},{160,226},{128,242},{240,6... | collective-permute-start | bytes 1572872 | tf_op jit(solution)/shard_map/ppermute | solution.py:335
  152.6 29.0 %collective-permute-start.32 = (f32[2,256,256]{2,1,0:T(8,128)}, f32[2,256,256]{2,1,0:T(8,128)S(1)}, u32[]{:S(2)}, u32[]{:S(2)}) collective-permute-start(f32[2,256,256]{2,1,0:T(8,128)} %get-tuple-element.79), channel_id=1, source_target_pairs={{112,2},{0,48},{32,32},{80,18},{208,226},{160,62},{128,46},{240,24... | collective-permute-start | bytes 1572872 | tf_op jit(solution)/shard_map/ppermute | solution.py:334
  193.4 14.9 %all-to-all-start.2 = ((f32[16,16,128]{2,1,0:T(8,128)}), f32[16,16,128]{2,1,0:T(8,128)S(1)}, u32[]{:S(2)}, u32[]{:S(2)}) async-start(f32[16,16,128]{2,1,0:T(8,128)} %broadcast_in_dim.22), calls=%async_computation.2 | async-start | bytes 262144 | tf_op jit(solution)/shard_map/all_to_all | solution.py:251
  (42 other events, 221.8 us)

commit v5 on v4

--- a/solution.py
+++ b/solution.py
@@ -1,7 +1,3 @@
-import functools
-
-import functools
-
 import jax
 import jax.numpy as jnp
 import numpy as np
@@ -85,70 +81,87 @@
     return ref[pl.ds(pl.multiple_of(half * quarter, quarter), quarter), :]
 
 
-def side_by_side(out, real, imag, turned=False):
-    antennas, times = real.shape
-    slab = antennas // 4
-
-    @pl.loop(0, 4)
-    def _(i):
-        rows = pl.ds(pl.multiple_of(i * slab, slab), slab)
-        out[rows, :times] = -imag[rows, :] if turned else real[rows, :]
-        out[rows, times:] = real[rows, :] if turned else imag[rows, :]
-
-
-def diagonal_kernel(real, imag, out, block, found):
-    side_by_side(block.at[0], real, imag)
-    side_by_side(block.at[1], real, imag, turned=True)
-
-    @pl.loop(0, 6)
-    def _(i):
-        lhs = rows_of(block.at[0], jnp.where(i // 2 == 1, 1, 0))
-        rhs = rows_of(block.at[i % 2], jnp.where(i < 2, 0, 1))
-        found[i] = matmul(lhs, rhs)
+def slabs(rows, count=4):
+    def run(function):
+        @pl.loop(0, count)
+        def _(i):
+            function(pl.ds(pl.multiple_of(i * (rows // count), rows // count), rows // count))
+
+    return run
+
+
+def turn(out, block):
+    times = block.shape[1] // 2
+
+    @slabs(block.shape[0])
+    def _(rows):
+        out[rows, :times] = -block[rows, times:]
+        out[rows, times:] = block[rows, :times]
+
+
+def diagonal_kernel(block, out, turned, found):
+    turn(turned, block)
+    for part, rhs in enumerate((block, turned)):
+
+        @pl.loop(0, 3)
+        def _(i):
+            lhs = rows_of(block, jnp.where(i == 1, 1, 0))
+            found[2 * i + part] = matmul(lhs, rows_of(rhs, jnp.where(i == 0, 0, 1)))
 
     out[0] = found[0] + found[1]
     out[1] = found[2] + found[3]
     out[2], out[3] = found[4], found[5]
 
 
-FIRST = (((2, 0), (1, 1)), ((2, 1), (3, 0)))
-REST = (((1, 0), (3, 1)), ((0, 0), (0, 1)))
-
-
-def stack(refs, lefts, rights):
-    side_by_side(lefts.at[0], refs[0], refs[1])
-    side_by_side(lefts.at[1], refs[4], refs[5])
-    side_by_side(rights.at[0], refs[2], refs[3])
-    side_by_side(rights.at[1], refs[2], refs[3], turned=True)
-
-
-def early_kernel(entries, device, table, *refs):
-    outs, lefts, rights = refs[6:10], refs[10], refs[11]
-    stack(refs, lefts, rights)
-    for out in range(2):
-        for place, (t, j) in enumerate(entries[out]):
-            for color in range(2):
-                index = table[device[0] * 16 + color * 8 + t * 2 + j]
-                lhs = rows_of(lefts.at[index // 4], index // 2 % 2)
-                rhs = rows_of(rights.at[color], index % 2)
-                outs[2 * color + out][place] = matmul(lhs, rhs)
-
-
-def late_kernel(entries, device, table, *refs):
-    diagonal, outs, lefts, rights = refs[6], refs[7:11], refs[11], refs[12]
-    stack(refs, lefts, rights)
+ORDER = ((2, 0), (1, 1), (2, 1), (3, 0), (1, 0), (3, 1), (0, 0), (0, 1))
+
+
+def stores(right, left, up, down, own):
+    return {
+        (0, 0): own.at[0],
+        (0, 1): own.at[1],
+        (1, 0): up,
+        (1, 1): right.at[1],
+        (2, 0): right.at[0],
+        (2, 1): left.at[0],
+        (3, 0): left.at[1],
+        (3, 1): down,
+    }
+
+
+def stack(lefts, one, two):
+    @slabs(one.shape[0])
+    def _(rows):
+        lefts[0, rows], lefts[1, rows] = one[rows], two[rows]
+
+
+def early_kernel(device, table, one, two, block, *refs):
+    outs, lefts, turned = refs[:10], refs[10], refs[11]
+    stack(lefts, one, two)
+    turn(turned, block)
+    for t, j in ORDER:
+        for color, rhs in enumerate((block, turned)):
+            index = table[device[0] * 16 + color * 8 + t * 2 + j]
+            lhs = rows_of(lefts.at[index // 4], index // 2 % 2)
+            out = stores(*outs[5 * color : 5 * color + 5])[t, j]
+            out[...] = matmul(lhs, rows_of(rhs, index % 2))
+
+
+def late_kernel(device, table, one, two, block, diagonal, *refs):
+    outs, lefts, turned = refs[:10], refs[10], refs[11]
+    stack(lefts, one, two)
+    turn(turned, block)
     upper = (device[1] >= PLANES // 2).astype(jnp.int32)
-    for out in range(2):
-        for place, (t, j) in enumerate(entries[out]):
-            for color in range(2):
-                index = table[device[0] * 16 + color * 8 + t * 2 + j]
-                near = index < 4
-                h = jnp.where(near, index // 2, index % 2)
-                k = jnp.where(near, index % 2, (h + upper) % 2)
-                lhs = rows_of(lefts.at[index // 4], h)
-                product = matmul(lhs, rows_of(rights.at[color], k))
-                ready = diagonal[jnp.maximum(index - 6, 0) * 2 + color]
-                outs[2 * color + out][place] = jnp.where(index < 6, product, ready)
+    for t, j in ORDER:
+        for color, rhs in enumerate((block, turned)):
+            index = table[device[0] * 16 + color * 8 + t * 2 + j]
+            near = index < 4
+            h = jnp.where(near, index // 2, index % 2)
+            k = jnp.where(near, index % 2, (h + upper) % 2)
+            product = matmul(rows_of(lefts.at[index // 4], h), rows_of(rhs, k))
+            ready = diagonal[jnp.maximum(index - 6, 0) * 2 + color]
+            out = stores(*outs[5 * color : 5 * color + 5])[t, j]
+            out[...] = jnp.where(index < 6, product, ready)
 
 
 def finish_kernel(device, ahead, *refs):
@@ -163,16 +176,16 @@
 
 
 def finish(device, ahead, parts):
-    slabs = 4
+    steps = 4
     quarter = parts[0].shape[-1]
-    slab = quarter // slabs
+    slab = quarter // steps
     smem = pl.BlockSpec(memory_space=pltpu.SMEM)
     one = pl.BlockSpec((slab, quarter), lambda i: (i, 0))
     second = pl.BlockSpec((1, slab, quarter), lambda i: (1, i, 0))
     both = pl.BlockSpec((2, slab, quarter), lambda i: (0, i, 0))
     return pl.pallas_call(
         finish_kernel,
-        grid=(slabs,),
+        grid=(steps,),
         out_shape=[jax.ShapeDtypeStruct((quarter, quarter), jnp.float32)] * 8,
         in_specs=[smem, smem] + 4 * [both, second, second, one, one],
         out_specs=[one] * 8,
@@ -281,44 +294,35 @@
     first, second, early, late, ahead, flags, half = tables()
     device_index = row_index * PLANES + column_index
     device = jnp.stack([device_index, column_index]).astype(jnp.int32)
-    real, later = lax.optimization_barrier((samples[:, 0, :], samples))
-    here = real, later[:, 1, :]
-    antennas, times = real.shape
+    here = samples.reshape(samples.shape[0], -1)
+    antennas, times = here.shape
     quarter = antennas // 2
-    product = 4 * quarter * quarter * times
-    stacks = [pltpu.VMEM((2, antennas, 2 * times), real.dtype)] * 2
-    found = stacks[0], pltpu.VMEM((6, quarter, quarter), jnp.float32)
-    near = [(shift_z(part, -1), shift_z(part, 1)) for part in here]
-    gain, near[0] = lax.optimization_barrier((gain, near[0]))
-    far = [(shift_z(above, -1), shift_z(below, 1)) for above, below in near]
-    above, below = zip(*near)
-    above2, below2 = zip(*far)
-    shapes = [(2, quarter, quarter)] * 4
+    product = 2 * quarter * quarter * times
+    turned = pltpu.VMEM(here.shape, here.dtype)
+    stacks = pltpu.VMEM((2,) + here.shape, here.dtype), turned
+    found = turned, pltpu.VMEM((6, quarter, quarter), jnp.float32)
+    above, below = shift_z(here, -1), shift_z(here, 1)
+    gain, above, below = lax.optimization_barrier((gain, above, below))
+    above2, below2 = shift_z(above, -1), shift_z(below, 1)
+    shapes = 2 * ([(2, quarter, quarter)] * 2 + [(quarter, quarter)] * 2 + [(2, quarter, quarter)])
     axes = (shift_x, shift_y)
 
-    def chunks(kernel, entries, table, blocks, products):
-        return kernel_call(
-            functools.partial(kernel, entries),
-            (device, jnp.asarray(table.reshape(-1))),
-            blocks,
-            shapes,
-            products * product,
-            stacks,
-        )
-
-    blocks = *here, *above, *below
-    first_outs = chunks(early_kernel, FIRST, early, blocks, 8)
-    received = [ring_start(*first_outs[2 * i : 2 * i + 2], axes[i]) for i in range(2)]
-    outs = chunks(early_kernel, REST, early, blocks, 8)
-    (diagonal,) = kernel_call(diagonal_kernel, (), here, [(4, quarter, quarter)], 6 * product, found)
-    sums = [ring_sums(received[i], outs[2 * i]) for i in range(2)]
-    early_parts = [ring_end(outs[2 * i + 1], received[i], sums[i], axes[i]) for i in range(2)]
-    _, blocks = lax.optimization_barrier((sums, (*below, *above2, *below2, diagonal)))
-    first_outs = chunks(late_kernel, FIRST, late, blocks, 8)
-    received = [ring_start(*first_outs[2 * i : 2 * i + 2], axes[i]) for i in range(2)]
-    outs = chunks(late_kernel, REST, late, blocks, 8)
-    sums = [ring_sums(received[i], outs[2 * i]) for i in range(2)]
-    late_parts = [ring_end(outs[2 * i + 1], received[i], sums[i], axes[i]) for i in range(2)]
+    def chunks(kernel, table, blocks):
+        scalars = device, jnp.asarray(table.reshape(-1))
+        return kernel_call(kernel, scalars, blocks, shapes, 16 * product, stacks)
+
+    outs = chunks(early_kernel, early, (here, below, above))
+    received = [ring_start(*outs[5 * i : 5 * i + 2], axes[i]) for i in range(2)]
+    (diagonal,) = kernel_call(
+        diagonal_kernel, (), (here,), [(4, quarter, quarter)], 6 * product, found
+    )
+    sums = [ring_sums(received[i], outs[5 * i + 2 : 5 * i + 4]) for i in range(2)]
+    early_parts = [ring_end(outs[5 * i + 4], received[i], sums[i], axes[i]) for i in range(2)]
+    _, blocks = lax.optimization_barrier((sums, (below, below2, above2, diagonal)))
+    outs = chunks(late_kernel, late, blocks)
+    received = [ring_start(*outs[5 * i : 5 * i + 2], axes[i]) for i in range(2)]
+    sums = [ring_sums(received[i], outs[5 * i + 2 : 5 * i + 4]) for i in range(2)]
+    late_parts = [ring_end(outs[5 * i + 4], received[i], sums[i], axes[i]) for i in range(2)]
     outs = finish(
         device,
         jnp.asarray(ahead.reshape(-1)),
@@ -377,7 +381,7 @@
     power = (model_real * model_real + model_imag * model_imag) * cross_mask
 
     parts = columns_to_rows(weight_real, weight_imag, power, gain)
-    sums = jnp.sum(exchange(parts, "col"), axis=0)
+    sums = jnp.sum(exchange(parts.reshape(-1, 128), "col"), axis=0).reshape(parts.shape)
     gain = sums[:2] / sums[2:]
 
     parts = rows_to_columns(weight_real, weight_imag, power, gain)

time: 224 us -> 226 us (level)
  blocking collectives: 19.8 us -> 28 us
  Pallas kernels: 31.4 us -> 24.1 us
  other arithmetic: 8.32 us -> 5.02 us
  waiting for transfers between devices: 80.3 us -> 83.3 us
  starting transfers between devices: 69.6 us -> 72.5 us
    ppermute x1, waiting for transfers between devices: 19.5 us -> 3.82 us  [vis_tiles(): two = lax.ppermute(two, ('row', 'col'), second)]
    ppermute x1, starting transfers between devices: 1.91 us -> 13.9 us  [vis_tiles(): two = lax.ppermute(two, ('row', 'col'), second)]
    ppermute x11, waiting for transfers between devices: 9.26 us -> 20.2 us  [shift_y(): return lax.ppermute(value, 'row', pairs)]
    all_to_all x1, blocking collectives: 9.53 us -> 17.7 us  [exchange(): return lax.all_to_all(copies, axis, 0, 0)]
    ppermute x11, waiting for transfers between devices: 12.2 us -> 20.2 us  [shift_x(): return lax.ppermute(value, 'row', pairs)]
    pallas_call x6 -> x4, Pallas kernels: 26.8 us -> 19.5 us  [kernel_call(): pl.pallas_call(kernel, out_shape=shapes, in_specs=[smem] * len(scalars) +...]
    ppermute x8 -> x4, waiting for transfers between devices: 8.58 us -> 1.51 us  [shift_z(): lax.ppermute(value, 'col', [(c, (c + step) % PLANES) for c in range(PLANE...]
    ppermute x11, starting transfers between devices: 15.4 us -> 9.74 us  [shift_x(): return lax.ppermute(value, 'row', pairs)]
  transfers between devices with their start and end apart: 35 -> 31, of which waited for: 20 -> 20; matrix products, arithmetic and copies ran while one was open for 4% -> 2% of each run, Pallas kernels for 6% -> 2%
where the time goes in v5:
time: 226 us; the launch traced here: 224 us
  waiting for transfers between devices  83.3 us (37%)
  starting transfers between devices  72.5 us (32%)
  blocking collectives  28 us (12%)
  Pallas kernels  24.1 us (11%)
  local copies, waits for them, and re-layouts  9.78 us (4%)
  other arithmetic  5.02 us (2%)
    ppermute x11, waiting for transfers between devices, shift_x(): return lax.ppermute(value, 'row', pairs)  20.2 us
    ppermute x11, waiting for transfers between devices, shift_y(): return lax.ppermute(value, 'row', pairs)  20.2 us
    ppermute x1, waiting for transfers between devices, starting_gains(): share = lax.ppermute(initial_gains, ('row', 'col'), pairs)  19.5 us
    pallas_call x4, Pallas kernels, kernel_call(): pl.pallas_call(kernel, out_shape=shapes, in_specs=[smem] * len(scalars) +...  19.5 us
    all_to_all x2, starting transfers between devices, exchange(): return lax.all_to_all(copies, axis, 0, 0)  18 us
    all_to_all x1, blocking collectives, exchange(): return lax.all_to_all(copies, axis, 0, 0)  17.7 us
    ppermute x11, starting transfers between devices, shift_y(): return lax.ppermute(value, 'row', pairs)  17 us
    all_to_all x2, waiting for transfers between devices, exchange(): return lax.all_to_all(copies, axis, 0, 0)  15 us
  transfers between devices with their start and end apart: 31, of which 20 were waited for; matrix products, arithmetic and copies ran while one was open for 2% of the time, Pallas kernels for 2%

profile of v5, /device:TPU:64, one launch (start us, length us, event | category | flops | bytes accessed | tf_op | source)
XLA Modules:
  0.0 223.8 jit_solution(7531069331754191731)
XLA Ops:
  1.7 1.9 collective-permute-start.2
  3.6 7.8 %collective-permute-start = (f32[2,32]{1,0:T(2,128)S(1)}, f32[2,32]{1,0:T(2,128)S(1)}, u32[]{:S(2)}, u32[]{:S(2)}) collective-permute-start(f32[2,32]{1,0:T(2,128)S(1)} %copy-done.34), channel_id=1, source_target_pairs={{0,0},{2,16},{4,32},{6,48},{8,64},{10,80},{12,96},{14,112},{16,128... | collective-permute-start | bytes 776 | tf_op jit(solution)/shard_map/ppermute | solution.py:355
  11.5 19.5 %collective-permute-done = f32[2,32]{1,0:T(2,128)S(1)} collective-permute-done((f32[2,32]{1,0:T(2,128)S(1)}, f32[2,32]{1,0:T(2,128)S(1)}, u32[]{:S(2)}, u32[]{:S(2)}) %collective-permute-start) | collective-permute-done | bytes 288 | tf_op jit(solution)/shard_map/ppermute | solution.py:355
  31.6 9.5 %all-to-all-start = ((f32[16,2,32]{2,1,0:T(2,128)}), f32[16,2,32]{2,1,0:T(2,128)S(1)}, u32[]{:S(2)}, u32[]{:S(2)}) async-start(f32[16,2,32]{2,1,0:T(2,128)} %broadcast_in_dim.20), calls=%async_computation | async-start | bytes 32768 | tf_op jit(solution)/shard_map/all_to_all | solution.py:264
  41.7 7.0 %all-to-all-done = f32[16,2,32]{2,1,0:T(2,128)S(1)} async-done(((f32[16,2,32]{2,1,0:T(2,128)}), f32[16,2,32]{2,1,0:T(2,128)S(1)}, u32[]{:S(2)}, u32[]{:S(2)}) %all-to-all-start) | async-done | bytes 4128 | tf_op jit(solution)/shard_map/all_to_all | solution.py:264
  49.8 6.0 %shard_map.82 = (f32[2,256,256]{2,1,0:T(8,128)}, f32[2,256,256]{2,1,0:T(8,128)}, f32[256,256]{1,0:T(8,128)}, f32[256,256]{1,0:T(8,128)}, f32[2,256,256]{2,1,0:T(...) custom-call(s32[2]{0:T(128)} %pad_add_fusion.device, ...), custom_call_target="tpu_custom_call" | custom-call | flops 2147483648 | bytes 7340032 | tf_op jit(solution)/shard_map/pallas_call | solution.py:216
  57.8 2.0 collective-permute-start.10
  61.0 4.4 %shard_map.83.diagonal = f32[4,256,256]{2,1,0:T(8,128)} custom-call(bf16[512,1024]{1,0:T(8,128)(2,1)} %bitcast.92), custom_call_target="tpu_custom_call" | custom-call | flops 805306368 | bytes 2097152 | tf_op jit(solution)/shard_map/pallas_call | solution.py:216
  70.0 8.0 %collective-permute-done.3.refs_1_ = f32[2,256,256]{2,1,0:T(8,128)S(1)} collective-permute-done((f32[2,256,256]{2,1,0:T(8,128)S(1)}, f32[2,256,256]{2,1,0:T(8,128)S(1)}, u32[]{:S(2)}, u32[]{:S(2)}) %collective-permute-start.3) | collective-permute-done | bytes 524320 | tf_op jit(solution)/shard_map/ppermute | solution.py:230
  79.6 6.3 %shard_map.84 = (f32[2,256,256]{2,1,0:T(8,128)}, f32[2,256,256]{2,1,0:T(8,128)}, f32[256,256]{1,0:T(8,128)}, f32[256,256]{1,0:T(8,128)}, f32[2,256,256]{2,1,0:T(...) custom-call(s32[2]{0:T(128)} %pad_add_fusion.device, ...), custom_call_target="tpu_custom_call" | custom-call | flops 2147483648 | bytes 8388608 | tf_op jit(solution)/shard_map/pallas_call | solution.py:216
  85.9 2.6 %collective-permute-start.18 = (f32[2,256,256]{2,1,0:T(8,128)}, f32[2,256,256]{2,1,0:T(8,128)S(1)}, u32[]{:S(2)}, u32[]{:S(2)}) collective-permute-start(f32[2,256,256]{2,1,0:T(8,128)} %get-tuple-element.65), channel_id=1, source_target_pairs={{0,192},{16,208},{32,224},{48,240},{64,0},{80,16},{96,32},{112,48}... | collective-permute-start | bytes 1572872 | tf_op jit(solution)/shard_map/ppermute | solution.py:237
  89.7 3.2 %collective-permute-start.16 = (f32[256,256]{1,0:T(8,128)}, f32[256,256]{1,0:T(8,128)S(1)}, u32[]{:S(2)}, u32[]{:S(2)}) collective-permute-start(f32[256,256]{1,0:T(8,128)} %fusion.7), channel_id=1, source_target_pairs={{0,192},{16,208},{32,224},{48,240},{64,0},{80,16},{96,32},{112,48}... | collective-permute-start | bytes 786440 | tf_op jit(solution)/shard_map/ppermute | solution.py:237
  93.0 5.6 %collective-permute-done.18.refs_17_ = f32[2,256,256]{2,1,0:T(8,128)S(1)} collective-permute-done((f32[2,256,256]{2,1,0:T(8,128)}, f32[2,256,256]{2,1,0:T(8,128)S(1)}, u32[]{:S(2)}, u32[]{:S(2)}) %collective-permute-start.18) | collective-permute-done | bytes 524320 | tf_op jit(solution)/shard_map/ppermute | solution.py:237
  100.3 1.5 collective-permute-done.17.refs_16_
  104.1 6.6 %collective-permute-done.11.refs_6_ = f32[2,256,256]{2,1,0:T(8,128)S(1)} collective-permute-done((f32[2,256,256]{2,1,0:T(8,128)}, f32[2,256,256]{2,1,0:T(8,128)S(1)}, u32[]{:S(2)}, u32[]{:S(2)}) %collective-permute-start.11) | collective-permute-done | bytes 524320 | tf_op jit(solution)/shard_map/ppermute | solution.py:230
  110.7 4.3 %collective-permute-start.20 = (f32[256,256]{1,0:T(8,128)S(1)}, f32[256,256]{1,0:T(8,128)S(1)}, u32[]{:S(2)}, u32[]{:S(2)}) collective-permute-start(f32[256,256]{1,0:T(8,128)S(1)} %fusion.3), channel_id=1, source_target_pairs={{0,192},{16,208},{32,224},{48,240},{64,0},{80,16},{96,32},{112,48}... | collective-permute-start | bytes 786440 | tf_op jit(solution)/shard_map/ppermute | solution.py:237
  117.3 1.6 collective-permute-done.20.refs_19_
  118.9 3.8 %collective-permute-done.19.refs_18_ = f32[256,256]{1,0:T(8,128)S(1)} collective-permute-done((f32[256,256]{1,0:T(8,128)S(1)}, f32[256,256]{1,0:T(8,128)S(1)}, u32[]{:S(2)}, u32[]{:S(2)}) %collective-permute-start.19) | collective-permute-done | bytes 262176 | tf_op jit(solution)/shard_map/ppermute | solution.py:237
  124.1 4.6 %shard_map.85 = (f32[256,256]{1,0:T(8,128)}, f32[256,256]{1,0:T(8,128)}, f32[256,256]{1,0:T(8,128)}, f32[256,256]{1,0:T(8,128)}, f32[256,256]{1,0:T(8,128)}, /*i...) custom-call(s32[2]{0:T(128)} %pad_add_fusion.device, s32[1024]{0:T(1024)} %constant.47.clone.ahead, ...), custom_call_target="tpu_custom_call" | custom-call | flops 1048576 | bytes 8388608 | tf_op jit(solution)/shard_map/pallas_call | solution.py:186
  128.8 4.6 %collective-permute-start.22 = (f32[256,256]{1,0:T(8,128)}, f32[256,256]{1,0:T(8,128)S(1)}, u32[]{:S(2)}, u32[]{:S(2)}) collective-permute-start(f32[256,256]{1,0:T(8,128)} %get-tuple-element.70), channel_id=1, source_target_pairs={{0,128},{16,144},{32,160},{48,176},{64,192},{80,208},{96,224},{112... | collective-permute-start | bytes 786440 | tf_op jit(solution)/shard_map/ppermute | solution.py:237
  134.9 1.7 collective-permute-done.21.refs_1_
  136.9 3.8 %collective-permute-done.22.refs_2_ = f32[256,256]{1,0:T(8,128)S(1)} collective-permute-done((f32[256,256]{1,0:T(8,128)}, f32[256,256]{1,0:T(8,128)S(1)}, u32[]{:S(2)}, u32[]{:S(2)}) %collective-permute-start.22) | collective-permute-done | bytes 262176 | tf_op jit(solution)/shard_map/ppermute | solution.py:237
  140.7 3.2 %collective-permute-done.24.refs_5_ = f32[256,256]{1,0:T(8,128)S(1)} collective-permute-done((f32[256,256]{1,0:T(8,128)}, f32[256,256]{1,0:T(8,128)S(1)}, u32[]{:S(2)}, u32[]{:S(2)}) %collective-permute-start.24) | collective-permute-done | bytes 262176 | tf_op jit(solution)/shard_map/ppermute | solution.py:230
  145.6 2.8 %shard_map.86 = (f32[2,256,256]{2,1,0:T(8,128)}, f32[2,256,256]{2,1,0:T(8,128)}) custom-call(s32[2]{0:T(128)} %pad_add_fusion.device, s32[256]{0:T(256)} %constant.48.clone.flags, f32[256,256]{1,0:T(8,128)} %get-tuple-element.68.refs_0_, f32[256,256]{1,0:T(8,128)} %copy-done.18, f32[256,256]{1,0:T(8,128)} %copy-done.20, f32[256,256]{1,0:T(8,128)} %copy-done.22, ...), custom_call_target="tpu_custom_call" | custom-call | bytes 3145728 | tf_op jit(solution)/shard_map/pallas_call | solution.py:216
  148.4 13.9 %collective-permute-start.27 = (f32[2,256,256]{2,1,0:T(8,128)}, f32[2,256,256]{2,1,0:T(8,128)S(1)}, u32[]{:S(2)}, u32[]{:S(2)}) collective-permute-start(f32[2,256,256]{2,1,0:T(8,128)} %get-tuple-element.76), channel_id=1, source_target_pairs={{112,32},{0,2},{32,18},{80,48},{208,46},{160,226},{128,242},{240,6... | collective-permute-start | bytes 1572872 | tf_op jit(solution)/shard_map/ppermute | solution.py:339
  162.4 1.9 collective-permute-start.28
  166.8 3.8 %collective-permute-done.27 = f32[2,256,256]{2,1,0:T(8,128)S(1)} collective-permute-done((f32[2,256,256]{2,1,0:T(8,128)}, f32[2,256,256]{2,1,0:T(8,128)S(1)}, u32[]{:S(2)}, u32[]{:S(2)}) %collective-permute-start.27) | collective-permute-done | bytes 524320 | tf_op jit(solution)/shard_map/ppermute | solution.py:339
  170.6 3.1 %collective-permute-done.28 = f32[2,256,256]{2,1,0:T(8,128)S(1)} collective-permute-done((f32[2,256,256]{2,1,0:T(8,128)}, f32[2,256,256]{2,1,0:T(8,128)S(1)}, u32[]{:S(2)}, u32[]{:S(2)}) %collective-permute-start.28) | collective-permute-done | bytes 524320 | tf_op jit(solution)/shard_map/ppermute | solution.py:338
  174.7 17.7 %all_to_all.20 = f32[8,6,128]{2,1,0:T(8,128)S(1)} all-to-all(f32[8,6,128]{2,1,0:T(8,128)S(1)} %broadcast_in_dim.22), channel_id=1, replica_groups=mesh['row'=16,'col'=8,'chan'=2] {'col'}, dimensions={0} | all-to-all | bytes 49152 | tf_op jit(solution)/shard_map/all_to_all | solution.py:264
  193.6 8.5 %all-to-all-start.2 = ((f32[16,16,128]{2,1,0:T(8,128)}), f32[16,16,128]{2,1,0:T(8,128)S(1)}, u32[]{:S(2)}, u32[]{:S(2)}) async-start(f32[16,16,128]{2,1,0:T(8,128)} %broadcast_in_dim.24), calls=%async_computation.2 | async-start | bytes 262144 | tf_op jit(solution)/shard_map/all_to_all | solution.py:264
  202.1 8.0 %all-to-all-done.2 = f32[16,16,128]{2,1,0:T(8,128)S(1)} async-done(((f32[16,16,128]{2,1,0:T(8,128)}), f32[16,16,128]{2,1,0:T(8,128)S(1)}, u32[]{:S(2)}, u32[]{:S(2)}) %all-to-all-start.2) | async-done | bytes 131104 | tf_op jit(solution)/shard_map/all_to_all | solution.py:264
  212.9 10.3 %all_to_all.21 = f32[8,3,32]{2,1,0:T(4,128)S(1)} all-to-all(f32[8,3,32]{2,1,0:T(4,128)S(1)} %maximum_bitcast_fusion), channel_id=1, replica_groups=mesh['row'=16,'col'=8,'chan'=2] {'col'}, dimensions={0} | all-to-all | bytes 6144 | tf_op jit(solution)/shard_map/all_to_all | solution.py:400
  (170 shorter events, 33.0 us)
Async XLA Ops:
  1.5 47.3 %copy-start.9 = (bf16[64,8,2,512]{3,1,2,0:T(8,128)(2,1)}, bf16[64,8,2,512]{3,1,2,0:T(8,128)(2,1)S(1)}, u32[]{:S(2)}) copy-start(bf16[64,8,2,512]{3,1,2,0:T(8,128)(2,1)S(1)} %copy.28) | copy-start | bytes 3145732
  1.5 47.3 %collective-permute-start.1 = (bf16[512,1024]{1,0:T(8,128)(2,1)S(1)}, bf16[512,1024]{1,0:T(8,128)(2,1)}, u32[]{:S(2)}, u32[]{:S(2)}) collective-permute-start(bf16[512,1024]{1,0:T(8,128)(2,1)S(1)} %bitcast.89), channel_id=1, source_target_pairs={{0,14},{2,0},{4,2},{6,4},{8,6},{10,8},{12,10},{14,12},{1,15},{3,1}... | collective-permute-start | bytes 3145736 | tf_op jit(solution)/shard_map/ppermute | solution.py:241
  1.7 47.1 %collective-permute-start.2 = (bf16[512,1024]{1,0:T(8,128)(2,1)S(1)}, bf16[512,1024]{1,0:T(8,128)(2,1)S(1)}, u32[]{:S(2)}, u32[]{:S(2)}) collective-permute-start(bf16[512,1024]{1,0:T(8,128)(2,1)S(1)} %bitcast.90), channel_id=1, source_target_pairs={{0,2},{2,4},{4,6},{6,8},{8,10},{10,12},{12,14},{14,0},{1,3},{3,5},... | collective-permute-start | bytes 3145736 | tf_op jit(solution)/shard_map/ppermute | solution.py:241
  3.6 27.4 %collective-permute-start = (f32[2,32]{1,0:T(2,128)S(1)}, f32[2,32]{1,0:T(2,128)S(1)}, u32[]{:S(2)}, u32[]{:S(2)}) collective-permute-start(f32[2,32]{1,0:T(2,128)S(1)} %copy-done.34), channel_id=1, source_target_pairs={{0,0},{2,16},{4,32},{6,48},{8,64},{10,80},{12,96},{14,112},{16,128... | collective-permute-start | bytes 776 | tf_op jit(solution)/shard_map/ppermute | solution.py:355
  31.6 17.1 %all-to-all-start = ((f32[16,2,32]{2,1,0:T(2,128)}), f32[16,2,32]{2,1,0:T(2,128)S(1)}, u32[]{:S(2)}, u32[]{:S(2)}) async-start(f32[16,2,32]{2,1,0:T(2,128)} %broadcast_in_dim.20), calls=%async_computation | async-start | bytes 32768 | tf_op jit(solution)/shard_map/all_to_all | solution.py:264
  55.8 11.0 %collective-permute-start.8 = (f32[2,256,256]{2,1,0:T(8,128)}, f32[2,256,256]{2,1,0:T(8,128)S(1)}, u32[]{:S(2)}, u32[]{:S(2)}) collective-permute-start(f32[2,256,256]{2,1,0:T(8,128)} %get-tuple-element.52), channel_id=1, source_target_pairs={{0,192},{16,208},{32,224},{48,240},{64,0},{80,16},{96,32},{112,48}... | collective-permute-start | bytes 1572872 | tf_op jit(solution)/shard_map/ppermute | solution.py:237
  56.9 11.9 %collective-permute-start.7 = (f32[2,256,256]{2,1,0:T(8,128)}, f32[2,256,256]{2,1,0:T(8,128)S(1)}, u32[]{:S(2)}, u32[]{:S(2)}) collective-permute-start(f32[2,256,256]{2,1,0:T(8,128)} %get-tuple-element.50), channel_id=1, source_target_pairs={{0,64},{16,80},{32,96},{48,112},{64,128},{80,144},{96,160},{112,17... | collective-permute-start | bytes 1572872 | tf_op jit(solution)/shard_map/ppermute | solution.py:237
  57.8 21.8 %collective-permute-start.9 = (bf16[512,1024]{1,0:T(8,128)(2,1)}, bf16[512,1024]{1,0:T(8,128)(2,1)}, u32[]{:S(2)}, u32[]{:S(2)}) collective-permute-start(bf16[512,1024]{1,0:T(8,128)(2,1)} %copy-done.32), channel_id=1, source_target_pairs={{0,2},{2,4},{4,6},{6,8},{8,10},{10,12},{12,14},{14,0},{1,3},{3,5},... | collective-permute-start | bytes 3145736 | tf_op jit(solution)/shard_map/ppermute | solution.py:241
  57.8 21.8 %collective-permute-start.10 = (bf16[512,1024]{1,0:T(8,128)(2,1)}, bf16[512,1024]{1,0:T(8,128)(2,1)}, u32[]{:S(2)}, u32[]{:S(2)}) collective-permute-start(bf16[512,1024]{1,0:T(8,128)(2,1)} %collective-permute-done.1.block), channel_id=1, source_target_pairs={{0,14},{2,0},{4,2},{6,4},{8,6},{10,8},{12,10},{14,12},{1,15},{3,1}... | collective-permute-start | bytes 3145736 | tf_op jit(solution)/shard_map/ppermute | solution.py:241
  59.8 9.9 %collective-permute-start.4 = (f32[2,256,256]{2,1,0:T(8,128)}, f32[2,256,256]{2,1,0:T(8,128)S(1)}, u32[]{:S(2)}, u32[]{:S(2)}) collective-permute-start(f32[2,256,256]{2,1,0:T(8,128)} %get-tuple-element.46), channel_id=1, source_target_pairs={{0,48},{16,0},{32,16},{48,32},{64,112},{80,64},{96,80},{112,96},{1... | collective-permute-start | bytes 1572872 | tf_op jit(solution)/shard_map/ppermute | solution.py:230
  66.8 11.2 %collective-permute-start.3 = (f32[2,256,256]{2,1,0:T(8,128)S(1)}, f32[2,256,256]{2,1,0:T(8,128)S(1)}, u32[]{:S(2)}, u32[]{:S(2)}) collective-permute-start(f32[2,256,256]{2,1,0:T(8,128)S(1)} %copy-done.33), channel_id=1, source_target_pairs={{0,16},{16,32},{32,48},{48,0},{64,80},{80,96},{96,112},{112,64},{1... | collective-permute-start | bytes 1572872 | tf_op jit(solution)/shard_map/ppermute | solution.py:230
  85.9 12.6 %collective-permute-start.18 = (f32[2,256,256]{2,1,0:T(8,128)}, f32[2,256,256]{2,1,0:T(8,128)S(1)}, u32[]{:S(2)}, u32[]{:S(2)}) collective-permute-start(f32[2,256,256]{2,1,0:T(8,128)} %get-tuple-element.65), channel_id=1, source_target_pairs={{0,192},{16,208},{32,224},{48,240},{64,0},{80,16},{96,32},{112,48}... | collective-permute-start | bytes 1572872 | tf_op jit(solution)/shard_map/ppermute | solution.py:237
  88.5 13.3 %collective-permute-start.17 = (f32[2,256,256]{2,1,0:T(8,128)}, f32[2,256,256]{2,1,0:T(8,128)S(1)}, u32[]{:S(2)}, u32[]{:S(2)}) collective-permute-start(f32[2,256,256]{2,1,0:T(8,128)} %get-tuple-element.64), channel_id=1, source_target_pairs={{0,64},{16,80},{32,96},{48,112},{64,128},{80,144},{96,160},{112,17... | collective-permute-start | bytes 1572872 | tf_op jit(solution)/shard_map/ppermute | solution.py:237
  88.5 14.6 %collective-permute-start.12 = (f32[2,256,256]{2,1,0:T(8,128)}, f32[2,256,256]{2,1,0:T(8,128)S(1)}, u32[]{:S(2)}, u32[]{:S(2)}) collective-permute-start(f32[2,256,256]{2,1,0:T(8,128)} %get-tuple-element.59), channel_id=1, source_target_pairs={{0,48},{16,0},{32,16},{48,32},{64,112},{80,64},{96,80},{112,96},{1... | collective-permute-start | bytes 1572872 | tf_op jit(solution)/shard_map/ppermute | solution.py:230
  89.7 25.3 %collective-permute-start.16 = (f32[256,256]{1,0:T(8,128)}, f32[256,256]{1,0:T(8,128)S(1)}, u32[]{:S(2)}, u32[]{:S(2)}) collective-permute-start(f32[256,256]{1,0:T(8,128)} %fusion.7), channel_id=1, source_target_pairs={{0,192},{16,208},{32,224},{48,240},{64,0},{80,16},{96,32},{112,48}... | collective-permute-start | bytes 786440 | tf_op jit(solution)/shard_map/ppermute | solution.py:237
  93.0 22.2 %collective-permute-start.15 = (f32[256,256]{1,0:T(8,128)S(1)}, f32[256,256]{1,0:T(8,128)S(1)}, u32[]{:S(2)}, u32[]{:S(2)}) collective-permute-start(f32[256,256]{1,0:T(8,128)S(1)} %fusion.8), channel_id=1, source_target_pairs={{0,64},{16,80},{32,96},{48,112},{64,128},{80,144},{96,160},{112,17... | collective-permute-start | bytes 786440 | tf_op jit(solution)/shard_map/ppermute | solution.py:237
  98.6 12.1 %collective-permute-start.11 = (f32[2,256,256]{2,1,0:T(8,128)}, f32[2,256,256]{2,1,0:T(8,128)S(1)}, u32[]{:S(2)}, u32[]{:S(2)}) collective-permute-start(f32[2,256,256]{2,1,0:T(8,128)} %get-tuple-element.58), channel_id=1, source_target_pairs={{0,16},{16,32},{32,48},{48,0},{64,80},{80,96},{96,112},{112,64},{1... | collective-permute-start | bytes 1572872 | tf_op jit(solution)/shard_map/ppermute | solution.py:230
  101.9 13.9 %collective-permute-start.6 = (f32[256,256]{1,0:T(8,128)S(1)}, f32[256,256]{1,0:T(8,128)S(1)}, u32[]{:S(2)}, u32[]{:S(2)}) collective-permute-start(f32[256,256]{1,0:T(8,128)S(1)} %fusion.9), channel_id=1, source_target_pairs={{0,48},{16,0},{32,16},{48,32},{64,112},{80,64},{96,80},{112,96},{1... | collective-permute-start | bytes 786440 | tf_op jit(solution)/shard_map/ppermute | solution.py:230
  103.1 14.2 %collective-permute-start.5 = (f32[256,256]{1,0:T(8,128)S(1)}, f32[256,256]{1,0:T(8,128)S(1)}, u32[]{:S(2)}, u32[]{:S(2)}) collective-permute-start(f32[256,256]{1,0:T(8,128)S(1)} %fusion.10), channel_id=1, source_target_pairs={{0,16},{16,32},{32,48},{48,0},{64,80},{80,96},{96,112},{112,64},{1... | collective-permute-start | bytes 786440 | tf_op jit(solution)/shard_map/ppermute | solution.py:230
  110.7 8.2 %collective-permute-start.20 = (f32[256,256]{1,0:T(8,128)S(1)}, f32[256,256]{1,0:T(8,128)S(1)}, u32[]{:S(2)}, u32[]{:S(2)}) collective-permute-start(f32[256,256]{1,0:T(8,128)S(1)} %fusion.3), channel_id=1, source_target_pairs={{0,192},{16,208},{32,224},{48,240},{64,0},{80,16},{96,32},{112,48}... | collective-permute-start | bytes 786440 | tf_op jit(solution)/shard_map/ppermute | solution.py:237
  115.1 7.7 %collective-permute-start.19 = (f32[256,256]{1,0:T(8,128)S(1)}, f32[256,256]{1,0:T(8,128)S(1)}, u32[]{:S(2)}, u32[]{:S(2)}) collective-permute-start(f32[256,256]{1,0:T(8,128)S(1)} %fusion.4), channel_id=1, source_target_pairs={{0,64},{16,80},{32,96},{48,112},{64,128},{80,144},{96,160},{112,17... | collective-permute-start | bytes 786440 | tf_op jit(solution)/shard_map/ppermute | solution.py:237
  115.2 7.6 %collective-permute-start.14 = (f32[256,256]{1,0:T(8,128)S(1)}, f32[256,256]{1,0:T(8,128)S(1)}, u32[]{:S(2)}, u32[]{:S(2)}) collective-permute-start(f32[256,256]{1,0:T(8,128)S(1)} %fusion.5), channel_id=1, source_target_pairs={{0,48},{16,0},{32,16},{48,32},{64,112},{80,64},{96,80},{112,96},{1... | collective-permute-start | bytes 786440 | tf_op jit(solution)/shard_map/ppermute | solution.py:230
  115.8 7.6 %collective-permute-start.13 = (f32[256,256]{1,0:T(8,128)S(1)}, f32[256,256]{1,0:T(8,128)S(1)}, u32[]{:S(2)}, u32[]{:S(2)}) collective-permute-start(f32[256,256]{1,0:T(8,128)S(1)} %fusion.6), channel_id=1, source_target_pairs={{0,16},{16,32},{32,48},{48,0},{64,80},{80,96},{96,112},{112,64},{1... | collective-permute-start | bytes 786440 | tf_op jit(solution)/shard_map/ppermute | solution.py:230
  128.7 7.9 %collective-permute-start.21 = (f32[256,256]{1,0:T(8,128)}, f32[256,256]{1,0:T(8,128)S(1)}, u32[]{:S(2)}, u32[]{:S(2)}) collective-permute-start(f32[256,256]{1,0:T(8,128)} %get-tuple-element.69), channel_id=1, source_target_pairs={{0,64},{16,80},{32,96},{48,112},{64,128},{80,144},{96,160},{112,17... | collective-permute-start | bytes 786440 | tf_op jit(solution)/shard_map/ppermute | solution.py:237
  128.8 11.9 %collective-permute-start.22 = (f32[256,256]{1,0:T(8,128)}, f32[256,256]{1,0:T(8,128)S(1)}, u32[]{:S(2)}, u32[]{:S(2)}) collective-permute-start(f32[256,256]{1,0:T(8,128)} %get-tuple-element.70), channel_id=1, source_target_pairs={{0,128},{16,144},{32,160},{48,176},{64,192},{80,208},{96,224},{112... | collective-permute-start | bytes 786440 | tf_op jit(solution)/shard_map/ppermute | solution.py:237
  133.3 7.4 %collective-permute-start.23 = (f32[256,256]{1,0:T(8,128)}, f32[256,256]{1,0:T(8,128)S(1)}, u32[]{:S(2)}, u32[]{:S(2)}) collective-permute-start(f32[256,256]{1,0:T(8,128)} %get-tuple-element.71), channel_id=1, source_target_pairs={{0,192},{16,208},{32,224},{48,240},{64,0},{80,16},{96,32},{112,48}... | collective-permute-start | bytes 786440 | tf_op jit(solution)/shard_map/ppermute | solution.py:237
  133.3 10.6 %collective-permute-start.24 = (f32[256,256]{1,0:T(8,128)}, f32[256,256]{1,0:T(8,128)S(1)}, u32[]{:S(2)}, u32[]{:S(2)}) collective-permute-start(f32[256,256]{1,0:T(8,128)} %get-tuple-element.73), channel_id=1, source_target_pairs={{0,16},{16,32},{32,48},{48,0},{64,80},{80,96},{96,112},{112,64},{1... | collective-permute-start | bytes 786440 | tf_op jit(solution)/shard_map/ppermute | solution.py:230
  134.1 9.9 %collective-permute-start.25 = (f32[256,256]{1,0:T(8,128)}, f32[256,256]{1,0:T(8,128)S(1)}, u32[]{:S(2)}, u32[]{:S(2)}) collective-permute-start(f32[256,256]{1,0:T(8,128)} %get-tuple-element.74), channel_id=1, source_target_pairs={{0,32},{16,48},{32,0},{48,16},{64,96},{80,112},{96,64},{112,80},{1... | collective-permute-start | bytes 786440 | tf_op jit(solution)/shard_map/ppermute | solution.py:230
  136.5 8.4 %collective-permute-start.26 = (f32[256,256]{1,0:T(8,128)}, f32[256,256]{1,0:T(8,128)S(1)}, u32[]{:S(2)}, u32[]{:S(2)}) collective-permute-start(f32[256,256]{1,0:T(8,128)} %get-tuple-element.75), channel_id=1, source_target_pairs={{0,48},{16,0},{32,16},{48,32},{64,112},{80,64},{96,80},{112,96},{1... | collective-permute-start | bytes 786440 | tf_op jit(solution)/shard_map/ppermute | solution.py:230
  148.4 22.2 %collective-permute-start.27 = (f32[2,256,256]{2,1,0:T(8,128)}, f32[2,256,256]{2,1,0:T(8,128)S(1)}, u32[]{:S(2)}, u32[]{:S(2)}) collective-permute-start(f32[2,256,256]{2,1,0:T(8,128)} %get-tuple-element.76), channel_id=1, source_target_pairs={{112,32},{0,2},{32,18},{80,48},{208,46},{160,226},{128,242},{240,6... | collective-permute-start | bytes 1572872 | tf_op jit(solution)/shard_map/ppermute | solution.py:339
  162.4 11.4 %collective-permute-start.28 = (f32[2,256,256]{2,1,0:T(8,128)}, f32[2,256,256]{2,1,0:T(8,128)S(1)}, u32[]{:S(2)}, u32[]{:S(2)}) collective-permute-start(f32[2,256,256]{2,1,0:T(8,128)} %get-tuple-element.77), channel_id=1, source_target_pairs={{112,2},{0,48},{32,32},{80,18},{208,226},{160,62},{128,46},{240,24... | collective-permute-start | bytes 1572872 | tf_op jit(solution)/shard_map/ppermute | solution.py:338
  193.6 16.5 %all-to-all-start.2 = ((f32[16,16,128]{2,1,0:T(8,128)}), f32[16,16,128]{2,1,0:T(8,128)S(1)}, u32[]{:S(2)}, u32[]{:S(2)}) async-start(f32[16,16,128]{2,1,0:T(8,128)} %broadcast_in_dim.24), calls=%async_computation.2 | async-start | bytes 262144 | tf_op jit(solution)/shard_map/all_to_all | solution.py:264
  (37 other events, 168.5 us)

commit v6 on v5

--- a/solution.py
+++ b/solution.py
@@ -164,36 +164,47 @@
             out[...] = jnp.where(index < 6, product, ready)
 
 
+def sum_kernel(*refs):
+    for color in range(2):
+        own, right, left, right2, left2 = refs[5 * color : 5 * color + 5]
+        refs[10 + color][0] = own[0] + right2[...] + left[0]
+        refs[10 + color][1] = own[1] + right[0] + left2[...]
+
+
 def finish_kernel(device, ahead, *refs):
-    ins, outs, sums = refs[:20], refs[20:28], refs[28]
+    ins, outs, sums = refs[:12], refs[12:20], refs[20]
     for color in range(2):
-        for group in range(2):
-            own, right, left, right2, left2 = ins[10 * color + 5 * group :][:5]
-            sums[2 * group] = own[0] + right2[...] + left[0]
-            sums[2 * group + 1] = own[1] + right[0] + left2[...]
+        early, own, right, left, right2, left2 = ins[6 * color : 6 * color + 6]
+        sums[0], sums[1] = early[0], early[1]
+        sums[2] = own[0] + right2[...] + left[0]
+        sums[3] = own[1] + right[0] + left2[...]
         for t in range(SIDE):
             outs[4 * color + t][...] = sums[ahead[device[0] * 8 + color * 4 + t]]
 
 
-def finish(device, ahead, parts):
-    steps = 4
+def by_slabs(kernel, scalars, parts, outs, scratch, steps=4):
     quarter = parts[0].shape[-1]
     slab = quarter // steps
-    smem = pl.BlockSpec(memory_space=pltpu.SMEM)
-    one = pl.BlockSpec((slab, quarter), lambda i: (i, 0))
-    second = pl.BlockSpec((1, slab, quarter), lambda i: (1, i, 0))
-    both = pl.BlockSpec((2, slab, quarter), lambda i: (0, i, 0))
+    specs = {
+        "one": pl.BlockSpec((slab, quarter), lambda i: (i, 0)),
+        "second": pl.BlockSpec((1, slab, quarter), lambda i: (1, i, 0)),
+        "both": pl.BlockSpec((2, slab, quarter), lambda i: (0, i, 0)),
+    }
+    pattern = ["both", "second", "second", "one", "one"]
+    if len(parts) == 12:
+        pattern = ["both"] + pattern
+    size = {"one": (quarter, quarter), "both": (2, quarter, quarter)}
     return pl.pallas_call(
-        finish_kernel,
+        kernel,
         grid=(steps,),
-        out_shape=[jax.ShapeDtypeStruct((quarter, quarter), jnp.float32)] * 8,
-        in_specs=[smem, smem] + 4 * [both, second, second, one, one],
-        out_specs=[one] * 8,
-        scratch_shapes=[pltpu.VMEM((4, slab, quarter), jnp.float32)],
+        out_shape=[jax.ShapeDtypeStruct(size[out], jnp.float32) for out in outs],
+        in_specs=[pl.BlockSpec(memory_space=pltpu.SMEM)] * len(scalars) + [specs[p] for p in 2 * pattern],
+        out_specs=[specs[out] for out in outs],
+        scratch_shapes=[pltpu.VMEM((4, slab, quarter), jnp.float32)] * scratch,
         cost_estimate=pl.CostEstimate(
-            flops=16 * quarter * quarter, bytes_accessed=128 * quarter * quarter, transcendentals=0
+            flops=8 * quarter * quarter, bytes_accessed=72 * quarter * quarter, transcendentals=0
         ),
-    )(device, ahead, *parts)
+    )(*scalars, *parts)
 
 
 def mirror_kernel(device, flags, *refs):
@@ -318,15 +329,17 @@
     )
     sums = [ring_sums(received[i], outs[5 * i + 2 : 5 * i + 4]) for i in range(2)]
     early_parts = [ring_end(outs[5 * i + 4], received[i], sums[i], axes[i]) for i in range(2)]
-    _, blocks = lax.optimization_barrier((sums, (below, below2, above2, diagonal)))
-    outs = chunks(late_kernel, late, blocks)
+    early_total = by_slabs(sum_kernel, (), early_parts[0] + early_parts[1], ["both"] * 2, 0)
+    outs = chunks(late_kernel, late, (below, below2, above2, diagonal))
     received = [ring_start(*outs[5 * i : 5 * i + 2], axes[i]) for i in range(2)]
     sums = [ring_sums(received[i], outs[5 * i + 2 : 5 * i + 4]) for i in range(2)]
     late_parts = [ring_end(outs[5 * i + 4], received[i], sums[i], axes[i]) for i in range(2)]
-    outs = finish(
-        device,
-        jnp.asarray(ahead.reshape(-1)),
-        early_parts[0] + late_parts[0] + early_parts[1] + late_parts[1],
+    outs = by_slabs(
+        finish_kernel,
+        (device, jnp.asarray(ahead.reshape(-1))),
+        (early_total[0], *late_parts[0], early_total[1], *late_parts[1]),
+        ["one"] * 8,
+        1,
     )
     parts = direct(outs[:4], shift_y) + direct(outs[4:], shift_x)
     one, two = kernel_call(

time: 226 us -> 213 us (0.942)
  starting transfers between devices: 72.5 us -> 63.4 us
  blocking collectives: 28 us -> 21.9 us
  Pallas kernels: 24.1 us -> 27.6 us
    ppermute x1, waiting for transfers between devices: 3.82 us -> 15.8 us  [vis_tiles(): two = lax.ppermute(two, ('row', 'col'), second)]
    ppermute x1, starting transfers between devices: 13.9 us -> 2.76 us  [vis_tiles(): two = lax.ppermute(two, ('row', 'col'), second)]
    ppermute x11, waiting for transfers between devices: 20.2 us -> 9.8 us  [shift_x(): return lax.ppermute(value, 'row', pairs)]
    all_to_all x1, blocking collectives: 17.7 us -> 11.6 us  [exchange(): return lax.all_to_all(copies, axis, 0, 0)]
    ppermute x1, starting transfers between devices: 1.92 us -> 6.08 us  [vis_tiles(): one = lax.ppermute(one, ('row', 'col'), first)]
    pallas_call x1 -> x2, Pallas kernels: 4.59 us -> 8.04 us  [by_slabs(): pl.pallas_call(kernel, grid=(steps,), out_shape=[jax.ShapeDtypeStruct(siz...]
    ppermute x1, waiting for transfers between devices: 3.09 us -> 0.01 us  [vis_tiles(): one = lax.ppermute(one, ('row', 'col'), first)]
    ppermute x11, starting transfers between devices: 17 us -> 13.9 us  [shift_y(): return lax.ppermute(value, 'row', pairs)]
  transfers between devices with their start and end apart: 31 -> 31, of which waited for: 20 -> 14; matrix products, arithmetic and copies ran while one was open for 2% -> 2% of each run, Pallas kernels for 2% -> 10%
where the time goes in v6:
time: 213 us; the launch traced here: 211 us
  waiting for transfers between devices  81.6 us (38%)
  starting transfers between devices  63.4 us (30%)
  Pallas kernels  27.6 us (13%)
  blocking collectives  21.9 us (10%)
  local copies, waits for them, and re-layouts  10.1 us (5%)
  other arithmetic  4.8 us (2%)
    pallas_call x4, Pallas kernels, kernel_call(): pl.pallas_call(kernel, out_shape=shapes, in_specs=[smem] * len(scalars) +...  19.6 us
    ppermute x1, waiting for transfers between devices, starting_gains(): share = lax.ppermute(initial_gains, ('row', 'col'), pairs)  19.5 us
    ppermute x11, waiting for transfers between devices, shift_y(): return lax.ppermute(value, 'row', pairs)  18.9 us
    all_to_all x2, starting transfers between devices, exchange(): return lax.all_to_all(copies, axis, 0, 0)  16.6 us
    ppermute x1, waiting for transfers between devices, vis_tiles(): two = lax.ppermute(two, ('row', 'col'), second)  15.8 us
    all_to_all x2, waiting for transfers between devices, exchange(): return lax.all_to_all(copies, axis, 0, 0)  15.6 us
    ppermute x11, starting transfers between devices, shift_y(): return lax.ppermute(value, 'row', pairs)  13.9 us
    ppermute x11, starting transfers between devices, shift_x(): return lax.ppermute(value, 'row', pairs)  12 us
  transfers between devices with their start and end apart: 31, of which 14 were waited for; matrix products, arithmetic and copies ran while one was open for 2% of the time, Pallas kernels for 10%

profile of v6, /device:TPU:64, one launch (start us, length us, event | category | flops | bytes accessed | tf_op | source)
XLA Modules:
  0.0 210.7 jit_solution(15175331180469481329)
XLA Ops:
  1.7 1.9 collective-permute-start.2
  3.6 7.8 %collective-permute-start = (f32[2,32]{1,0:T(2,128)S(1)}, f32[2,32]{1,0:T(2,128)S(1)}, u32[]{:S(2)}, u32[]{:S(2)}) collective-permute-start(f32[2,32]{1,0:T(2,128)S(1)} %copy-done.36), channel_id=1, source_target_pairs={{0,0},{2,16},{4,32},{6,48},{8,64},{10,80},{12,96},{14,112},{16,128... | collective-permute-start | bytes 776 | tf_op jit(solution)/shard_map/ppermute | solution.py:368
  11.5 19.5 %collective-permute-done = f32[2,32]{1,0:T(2,128)S(1)} collective-permute-done((f32[2,32]{1,0:T(2,128)S(1)}, f32[2,32]{1,0:T(2,128)S(1)}, u32[]{:S(2)}, u32[]{:S(2)}) %collective-permute-start) | collective-permute-done | bytes 288 | tf_op jit(solution)/shard_map/ppermute | solution.py:368
  31.6 9.5 %all-to-all-start = ((f32[16,2,32]{2,1,0:T(2,128)}), f32[16,2,32]{2,1,0:T(2,128)S(1)}, u32[]{:S(2)}, u32[]{:S(2)}) async-start(f32[16,2,32]{2,1,0:T(2,128)} %broadcast_in_dim.20), calls=%async_computation | async-start | bytes 32768 | tf_op jit(solution)/shard_map/all_to_all | solution.py:275
  41.1 7.6 %all-to-all-done = f32[16,2,32]{2,1,0:T(2,128)S(1)} async-done(((f32[16,2,32]{2,1,0:T(2,128)}), f32[16,2,32]{2,1,0:T(2,128)S(1)}, u32[]{:S(2)}, u32[]{:S(2)}) %all-to-all-start) | async-done | bytes 4128 | tf_op jit(solution)/shard_map/all_to_all | solution.py:275
  48.9 2.0 collective-permute-start.12
  51.6 6.0 %shard_map.82 = (f32[2,256,256]{2,1,0:T(8,128)}, f32[2,256,256]{2,1,0:T(8,128)}, f32[256,256]{1,0:T(8,128)}, f32[256,256]{1,0:T(8,128)}, f32[2,256,256]{2,1,0:T(...) custom-call(s32[2]{0:T(128)} %pad_add_fusion.device, ...), custom_call_target="tpu_custom_call" | custom-call | flops 2147483648 | bytes 7340032 | tf_op jit(solution)/shard_map/pallas_call | solution.py:227
  59.6 4.4 %shard_map.84.diagonal = f32[4,256,256]{2,1,0:T(8,128)} custom-call(bf16[512,1024]{1,0:T(8,128)(2,1)} %bitcast.92), custom_call_target="tpu_custom_call" | custom-call | flops 805306368 | bytes 2097152 | tf_op jit(solution)/shard_map/pallas_call | solution.py:227
  65.2 2.8 %collective-permute-done.8.refs_7_ = f32[2,256,256]{2,1,0:T(8,128)S(1)} collective-permute-done((f32[2,256,256]{2,1,0:T(8,128)}, f32[2,256,256]{2,1,0:T(8,128)S(1)}, u32[]{:S(2)}, u32[]{:S(2)}) %collective-permute-start.8) | collective-permute-done | bytes 524320 | tf_op jit(solution)/shard_map/ppermute | solution.py:248
  69.3 1.9 collective-permute-done.11.two
  72.4 6.4 %shard_map.85 = (f32[2,256,256]{2,1,0:T(8,128)}, f32[2,256,256]{2,1,0:T(8,128)}, f32[256,256]{1,0:T(8,128)}, f32[256,256]{1,0:T(8,128)}, f32[2,256,256]{2,1,0:T(...) custom-call(s32[2]{0:T(128)} %pad_add_fusion.device, ...), custom_call_target="tpu_custom_call" | custom-call | flops 2147483648 | bytes 8388608 | tf_op jit(solution)/shard_map/pallas_call | solution.py:227
  82.3 1.7 collective-permute-start.14
  84.1 5.0 %collective-permute-done.18.refs_9_ = f32[2,256,256]{2,1,0:T(8,128)S(1)} collective-permute-done((f32[2,256,256]{2,1,0:T(8,128)}, f32[2,256,256]{2,1,0:T(8,128)S(1)}, u32[]{:S(2)}, u32[]{:S(2)}) %collective-permute-start.18) | collective-permute-done | bytes 524320 | tf_op jit(solution)/shard_map/ppermute | solution.py:248
  89.7 6.2 %collective-permute-done.17.refs_8_ = f32[2,256,256]{2,1,0:T(8,128)S(1)} collective-permute-done((f32[2,256,256]{2,1,0:T(8,128)S(1)}, f32[2,256,256]{2,1,0:T(8,128)S(1)}, u32[]{:S(2)}, u32[]{:S(2)}) %collective-permute-start.17) | collective-permute-done | bytes 524320 | tf_op jit(solution)/shard_map/ppermute | solution.py:248
  98.9 3.4 %collective-permute-done.13.refs_2_ = f32[2,256,256]{2,1,0:T(8,128)S(1)} collective-permute-done((f32[2,256,256]{2,1,0:T(8,128)S(1)}, f32[2,256,256]{2,1,0:T(8,128)S(1)}, u32[]{:S(2)}, u32[]{:S(2)}) %collective-permute-start.13) | collective-permute-done | bytes 524320 | tf_op jit(solution)/shard_map/ppermute | solution.py:241
  102.3 2.7 %collective-permute-start.20 = (f32[256,256]{1,0:T(8,128)S(1)}, f32[256,256]{1,0:T(8,128)S(1)}, u32[]{:S(2)}, u32[]{:S(2)}) collective-permute-start(f32[256,256]{1,0:T(8,128)S(1)} %fusion.3), channel_id=1, source_target_pairs={{0,192},{16,208},{32,224},{48,240},{64,0},{80,16},{96,32},{112,48}... | collective-permute-start | bytes 786440 | tf_op jit(solution)/shard_map/ppermute | solution.py:248
  105.2 3.3 %collective-permute-start.16 = (f32[256,256]{1,0:T(8,128)S(1)}, f32[256,256]{1,0:T(8,128)S(1)}, u32[]{:S(2)}, u32[]{:S(2)}) collective-permute-start(f32[256,256]{1,0:T(8,128)S(1)} %fusion.5), channel_id=1, source_target_pairs={{0,48},{16,0},{32,16},{48,32},{64,112},{80,64},{96,80},{112,96},{1... | collective-permute-start | bytes 786440 | tf_op jit(solution)/shard_map/ppermute | solution.py:241
  110.0 3.8 %shard_map.83 = (f32[2,256,256]{2,1,0:T(8,128)}, f32[2,256,256]{2,1,0:T(8,128)}) custom-call(f32[2,256,256]{2,1,0:T(8,128)} %get-tuple-element.42.refs_0_, f32[2,256,256]{2,1,0:T(8,128)} %copy-done.8, f32[2,256,256]{2,1,0:T(8,128)} %copy-done.7, f32[256,256]{1,0:T(8,128)} %copy-done.26, f32[256,256]{1,0:T(8,128)} %copy-done.20, ...), custom_call_target="tpu_custom_call" | custom-call | flops 524288 | bytes 4718592 | tf_op jit(solution)/shard_map/pallas_call | solution.py:197
  113.9 2.2 %collective-permute-done.15.refs_4_ = f32[256,256]{1,0:T(8,128)S(1)} collective-permute-done((f32[256,256]{1,0:T(8,128)S(1)}, f32[256,256]{1,0:T(8,128)S(1)}, u32[]{:S(2)}, u32[]{:S(2)}) %collective-permute-start.15) | collective-permute-done | bytes 262176 | tf_op jit(solution)/shard_map/ppermute | solution.py:241
  116.8 4.2 %shard_map.86 = (f32[256,256]{1,0:T(8,128)}, f32[256,256]{1,0:T(8,128)}, f32[256,256]{1,0:T(8,128)}, f32[256,256]{1,0:T(8,128)}, f32[256,256]{1,0:T(8,128)}, /*i...) custom-call(s32[2]{0:T(128)} %pad_add_fusion.device, s32[1024]{0:T(1024)} %constant.47.clone.ahead, ...), custom_call_target="tpu_custom_call" | custom-call | flops 524288 | bytes 4718592 | tf_op jit(solution)/shard_map/pallas_call | solution.py:197
  121.1 4.6 %collective-permute-start.22 = (f32[256,256]{1,0:T(8,128)}, f32[256,256]{1,0:T(8,128)S(1)}, u32[]{:S(2)}, u32[]{:S(2)}) collective-permute-start(f32[256,256]{1,0:T(8,128)} %get-tuple-element.66), channel_id=1, source_target_pairs={{0,128},{16,144},{32,160},{48,176},{64,192},{80,208},{96,224},{112... | collective-permute-start | bytes 786440 | tf_op jit(solution)/shard_map/ppermute | solution.py:248
  125.7 2.0 collective-permute-start.25
  129.4 3.7 %collective-permute-done.22.refs_2_ = f32[256,256]{1,0:T(8,128)S(1)} collective-permute-done((f32[256,256]{1,0:T(8,128)}, f32[256,256]{1,0:T(8,128)S(1)}, u32[]{:S(2)}, u32[]{:S(2)}) %collective-permute-start.22) | collective-permute-done | bytes 262176 | tf_op jit(solution)/shard_map/ppermute | solution.py:248
  133.1 3.2 %collective-permute-done.24.refs_5_ = f32[256,256]{1,0:T(8,128)S(1)} collective-permute-done((f32[256,256]{1,0:T(8,128)}, f32[256,256]{1,0:T(8,128)S(1)}, u32[]{:S(2)}, u32[]{:S(2)}) %collective-permute-start.24) | collective-permute-done | bytes 262176 | tf_op jit(solution)/shard_map/ppermute | solution.py:241
  137.9 2.8 %shard_map.87 = (f32[2,256,256]{2,1,0:T(8,128)}, f32[2,256,256]{2,1,0:T(8,128)}) custom-call(s32[2]{0:T(128)} %pad_add_fusion.device, s32[256]{0:T(256)} %constant.48.clone.flags, f32[256,256]{1,0:T(8,128)} %get-tuple-element.64.refs_0_, f32[256,256]{1,0:T(8,128)} %copy-done.22, f32[256,256]{1,0:T(8,128)} %copy-done.24, f32[256,256]{1,0:T(8,128)} %copy-done.27, ...), custom_call_target="tpu_custom_call" | custom-call | bytes 3145728 | tf_op jit(solution)/shard_map/pallas_call | solution.py:227
  140.7 2.8 %collective-permute-start.27 = (f32[2,256,256]{2,1,0:T(8,128)}, f32[2,256,256]{2,1,0:T(8,128)S(1)}, u32[]{:S(2)}, u32[]{:S(2)}) collective-permute-start(f32[2,256,256]{2,1,0:T(8,128)} %get-tuple-element.72), channel_id=1, source_target_pairs={{112,32},{0,2},{32,18},{80,48},{208,46},{160,226},{128,242},{240,6... | collective-permute-start | bytes 1572872 | tf_op jit(solution)/shard_map/ppermute | solution.py:352
  143.5 6.1 %collective-permute-start.28 = (f32[2,256,256]{2,1,0:T(8,128)}, f32[2,256,256]{2,1,0:T(8,128)S(1)}, u32[]{:S(2)}, u32[]{:S(2)}) collective-permute-start(f32[2,256,256]{2,1,0:T(8,128)} %get-tuple-element.73), channel_id=1, source_target_pairs={{112,2},{0,48},{32,32},{80,18},{208,226},{160,62},{128,46},{240,24... | collective-permute-start | bytes 1572872 | tf_op jit(solution)/shard_map/ppermute | solution.py:351
  152.3 15.8 %collective-permute-done.27 = f32[2,256,256]{2,1,0:T(8,128)S(1)} collective-permute-done((f32[2,256,256]{2,1,0:T(8,128)}, f32[2,256,256]{2,1,0:T(8,128)S(1)}, u32[]{:S(2)}, u32[]{:S(2)}) %collective-permute-start.27) | collective-permute-done | bytes 524320 | tf_op jit(solution)/shard_map/ppermute | solution.py:352
  169.1 11.6 %all_to_all.20 = f32[8,6,128]{2,1,0:T(8,128)S(1)} all-to-all(f32[8,6,128]{2,1,0:T(8,128)S(1)} %broadcast_in_dim.22), channel_id=1, replica_groups=mesh['row'=16,'col'=8,'chan'=2] {'col'}, dimensions={0} | all-to-all | bytes 49152 | tf_op jit(solution)/shard_map/all_to_all | solution.py:275
  181.9 7.1 %all-to-all-start.2 = ((f32[16,16,128]{2,1,0:T(8,128)}), f32[16,16,128]{2,1,0:T(8,128)S(1)}, u32[]{:S(2)}, u32[]{:S(2)}) async-start(f32[16,16,128]{2,1,0:T(8,128)} %broadcast_in_dim.24), calls=%async_computation.2 | async-start | bytes 262144 | tf_op jit(solution)/shard_map/all_to_all | solution.py:275
  189.0 8.0 %all-to-all-done.2 = f32[16,16,128]{2,1,0:T(8,128)S(1)} async-done(((f32[16,16,128]{2,1,0:T(8,128)}), f32[16,16,128]{2,1,0:T(8,128)S(1)}, u32[]{:S(2)}, u32[]{:S(2)}) %all-to-all-start.2) | async-done | bytes 131104 | tf_op jit(solution)/shard_map/all_to_all | solution.py:275
  199.8 10.3 %all_to_all.21 = f32[8,3,32]{2,1,0:T(4,128)S(1)} all-to-all(f32[8,3,32]{2,1,0:T(4,128)S(1)} %maximum_bitcast_fusion), channel_id=1, replica_groups=mesh['row'=16,'col'=8,'chan'=2] {'col'}, dimensions={0} | all-to-all | bytes 6144 | tf_op jit(solution)/shard_map/all_to_all | solution.py:413
  (175 shorter events, 29.0 us)
Async XLA Ops:
  1.5 50.1 %copy-start.9 = (bf16[64,8,2,512]{3,1,2,0:T(8,128)(2,1)}, bf16[64,8,2,512]{3,1,2,0:T(8,128)(2,1)S(1)}, u32[]{:S(2)}) copy-start(bf16[64,8,2,512]{3,1,2,0:T(8,128)(2,1)S(1)} %copy.28) | copy-start | bytes 3145732
  1.5 47.3 %collective-permute-start.1 = (bf16[512,1024]{1,0:T(8,128)(2,1)S(1)}, bf16[512,1024]{1,0:T(8,128)(2,1)}, u32[]{:S(2)}, u32[]{:S(2)}) collective-permute-start(bf16[512,1024]{1,0:T(8,128)(2,1)S(1)} %bitcast.89), channel_id=1, source_target_pairs={{0,14},{2,0},{4,2},{6,4},{8,6},{10,8},{12,10},{14,12},{1,15},{3,1}... | collective-permute-start | bytes 3145736 | tf_op jit(solution)/shard_map/ppermute | solution.py:252
  1.7 47.1 %collective-permute-start.2 = (bf16[512,1024]{1,0:T(8,128)(2,1)S(1)}, bf16[512,1024]{1,0:T(8,128)(2,1)}, u32[]{:S(2)}, u32[]{:S(2)}) collective-permute-start(bf16[512,1024]{1,0:T(8,128)(2,1)S(1)} %bitcast.90), channel_id=1, source_target_pairs={{0,2},{2,4},{4,6},{6,8},{8,10},{10,12},{12,14},{14,0},{1,3},{3,5},... | collective-permute-start | bytes 3145736 | tf_op jit(solution)/shard_map/ppermute | solution.py:252
  3.6 27.4 %collective-permute-start = (f32[2,32]{1,0:T(2,128)S(1)}, f32[2,32]{1,0:T(2,128)S(1)}, u32[]{:S(2)}, u32[]{:S(2)}) collective-permute-start(f32[2,32]{1,0:T(2,128)S(1)} %copy-done.36), channel_id=1, source_target_pairs={{0,0},{2,16},{4,32},{6,48},{8,64},{10,80},{12,96},{14,112},{16,128... | collective-permute-start | bytes 776 | tf_op jit(solution)/shard_map/ppermute | solution.py:368
  31.6 17.1 %all-to-all-start = ((f32[16,2,32]{2,1,0:T(2,128)}), f32[16,2,32]{2,1,0:T(2,128)S(1)}, u32[]{:S(2)}, u32[]{:S(2)}) async-start(f32[16,2,32]{2,1,0:T(2,128)} %broadcast_in_dim.20), calls=%async_computation | async-start | bytes 32768 | tf_op jit(solution)/shard_map/all_to_all | solution.py:275
  48.8 22.4 %collective-permute-start.11 = (bf16[512,1024]{1,0:T(8,128)(2,1)}, bf16[512,1024]{1,0:T(8,128)(2,1)}, u32[]{:S(2)}, u32[]{:S(2)}) collective-permute-start(bf16[512,1024]{1,0:T(8,128)(2,1)} %collective-permute-done.2.two.one), channel_id=1, source_target_pairs={{0,2},{2,4},{4,6},{6,8},{8,10},{10,12},{12,14},{14,0},{1,3},{3,5},... | collective-permute-start | bytes 3145736 | tf_op jit(solution)/shard_map/ppermute | solution.py:252
  48.9 23.5 %collective-permute-start.12 = (bf16[512,1024]{1,0:T(8,128)(2,1)}, bf16[512,1024]{1,0:T(8,128)(2,1)}, u32[]{:S(2)}, u32[]{:S(2)}) collective-permute-start(bf16[512,1024]{1,0:T(8,128)(2,1)} %collective-permute-done.1.block), channel_id=1, source_target_pairs={{0,14},{2,0},{4,2},{6,4},{8,6},{10,8},{12,10},{14,12},{1,15},{3,1}... | collective-permute-start | bytes 3145736 | tf_op jit(solution)/shard_map/ppermute | solution.py:252
  57.6 10.4 %collective-permute-start.8 = (f32[2,256,256]{2,1,0:T(8,128)}, f32[2,256,256]{2,1,0:T(8,128)S(1)}, u32[]{:S(2)}, u32[]{:S(2)}) collective-permute-start(f32[2,256,256]{2,1,0:T(8,128)} %get-tuple-element.49), channel_id=1, source_target_pairs={{0,192},{16,208},{32,224},{48,240},{64,0},{80,16},{96,32},{112,48}... | collective-permute-start | bytes 1572872 | tf_op jit(solution)/shard_map/ppermute | solution.py:248
  58.7 20.9 %collective-permute-start.7 = (f32[2,256,256]{2,1,0:T(8,128)}, f32[2,256,256]{2,1,0:T(8,128)S(1)}, u32[]{:S(2)}, u32[]{:S(2)}) collective-permute-start(f32[2,256,256]{2,1,0:T(8,128)} %get-tuple-element.48), channel_id=1, source_target_pairs={{0,64},{16,80},{32,96},{48,112},{64,128},{80,144},{96,160},{112,17... | collective-permute-start | bytes 1572872 | tf_op jit(solution)/shard_map/ppermute | solution.py:248
  64.0 17.2 %collective-permute-start.4 = (f32[2,256,256]{2,1,0:T(8,128)}, f32[2,256,256]{2,1,0:T(8,128)S(1)}, u32[]{:S(2)}, u32[]{:S(2)}) collective-permute-start(f32[2,256,256]{2,1,0:T(8,128)} %get-tuple-element.44), channel_id=1, source_target_pairs={{0,48},{16,0},{32,16},{48,32},{64,112},{80,64},{96,80},{112,96},{1... | collective-permute-start | bytes 1572872 | tf_op jit(solution)/shard_map/ppermute | solution.py:241
  68.0 14.2 %collective-permute-start.3 = (f32[2,256,256]{2,1,0:T(8,128)}, f32[2,256,256]{2,1,0:T(8,128)S(1)}, u32[]{:S(2)}, u32[]{:S(2)}) collective-permute-start(f32[2,256,256]{2,1,0:T(8,128)} %get-tuple-element.43), channel_id=1, source_target_pairs={{0,16},{16,32},{32,48},{48,0},{64,80},{80,96},{96,112},{112,64},{1... | collective-permute-start | bytes 1572872 | tf_op jit(solution)/shard_map/ppermute | solution.py:241
  71.2 33.9 %collective-permute-start.10 = (f32[256,256]{1,0:T(8,128)}, f32[256,256]{1,0:T(8,128)S(1)}, u32[]{:S(2)}, u32[]{:S(2)}) collective-permute-start(f32[256,256]{1,0:T(8,128)} %fusion.7), channel_id=1, source_target_pairs={{0,192},{16,208},{32,224},{48,240},{64,0},{80,16},{96,32},{112,48}... | collective-permute-start | bytes 786440 | tf_op jit(solution)/shard_map/ppermute | solution.py:248
  78.8 10.2 %collective-permute-start.18 = (f32[2,256,256]{2,1,0:T(8,128)}, f32[2,256,256]{2,1,0:T(8,128)S(1)}, u32[]{:S(2)}, u32[]{:S(2)}) collective-permute-start(f32[2,256,256]{2,1,0:T(8,128)} %get-tuple-element.61), channel_id=1, source_target_pairs={{0,192},{16,208},{32,224},{48,240},{64,0},{80,16},{96,32},{112,48}... | collective-permute-start | bytes 1572872 | tf_op jit(solution)/shard_map/ppermute | solution.py:248
  79.7 25.5 %collective-permute-start.9 = (f32[256,256]{1,0:T(8,128)S(1)}, f32[256,256]{1,0:T(8,128)S(1)}, u32[]{:S(2)}, u32[]{:S(2)}) collective-permute-start(f32[256,256]{1,0:T(8,128)S(1)} %fusion.8), channel_id=1, source_target_pairs={{0,64},{16,80},{32,96},{48,112},{64,128},{80,144},{96,160},{112,17... | collective-permute-start | bytes 786440 | tf_op jit(solution)/shard_map/ppermute | solution.py:248
  81.2 14.7 %collective-permute-start.17 = (f32[2,256,256]{2,1,0:T(8,128)S(1)}, f32[2,256,256]{2,1,0:T(8,128)S(1)}, u32[]{:S(2)}, u32[]{:S(2)}) collective-permute-start(f32[2,256,256]{2,1,0:T(8,128)S(1)} %copy-done.35), channel_id=1, source_target_pairs={{0,64},{16,80},{32,96},{48,112},{64,128},{80,144},{96,160},{112,17... | collective-permute-start | bytes 1572872 | tf_op jit(solution)/shard_map/ppermute | solution.py:248
  82.3 15.6 %collective-permute-start.14 = (f32[2,256,256]{2,1,0:T(8,128)S(1)}, f32[2,256,256]{2,1,0:T(8,128)S(1)}, u32[]{:S(2)}, u32[]{:S(2)}) collective-permute-start(f32[2,256,256]{2,1,0:T(8,128)S(1)} %copy-done.34), channel_id=1, source_target_pairs={{0,48},{16,0},{32,16},{48,32},{64,112},{80,64},{96,80},{112,96},{1... | collective-permute-start | bytes 1572872 | tf_op jit(solution)/shard_map/ppermute | solution.py:241
  89.0 13.3 %collective-permute-start.13 = (f32[2,256,256]{2,1,0:T(8,128)S(1)}, f32[2,256,256]{2,1,0:T(8,128)S(1)}, u32[]{:S(2)}, u32[]{:S(2)}) collective-permute-start(f32[2,256,256]{2,1,0:T(8,128)S(1)} %copy-done.33), channel_id=1, source_target_pairs={{0,16},{16,32},{32,48},{48,0},{64,80},{80,96},{96,112},{112,64},{1... | collective-permute-start | bytes 1572872 | tf_op jit(solution)/shard_map/ppermute | solution.py:241
  96.0 12.5 %collective-permute-start.6 = (f32[256,256]{1,0:T(8,128)S(1)}, f32[256,256]{1,0:T(8,128)S(1)}, u32[]{:S(2)}, u32[]{:S(2)}) collective-permute-start(f32[256,256]{1,0:T(8,128)S(1)} %fusion.9), channel_id=1, source_target_pairs={{0,48},{16,0},{32,16},{48,32},{64,112},{80,64},{96,80},{112,96},{1... | collective-permute-start | bytes 786440 | tf_op jit(solution)/shard_map/ppermute | solution.py:241
  97.9 10.6 %collective-permute-start.5 = (f32[256,256]{1,0:T(8,128)S(1)}, f32[256,256]{1,0:T(8,128)S(1)}, u32[]{:S(2)}, u32[]{:S(2)}) collective-permute-start(f32[256,256]{1,0:T(8,128)S(1)} %fusion.10), channel_id=1, source_target_pairs={{0,16},{16,32},{32,48},{48,0},{64,80},{80,96},{96,112},{112,64},{1... | collective-permute-start | bytes 786440 | tf_op jit(solution)/shard_map/ppermute | solution.py:241
  102.3 11.5 %collective-permute-start.20 = (f32[256,256]{1,0:T(8,128)S(1)}, f32[256,256]{1,0:T(8,128)S(1)}, u32[]{:S(2)}, u32[]{:S(2)}) collective-permute-start(f32[256,256]{1,0:T(8,128)S(1)} %fusion.3), channel_id=1, source_target_pairs={{0,192},{16,208},{32,224},{48,240},{64,0},{80,16},{96,32},{112,48}... | collective-permute-start | bytes 786440 | tf_op jit(solution)/shard_map/ppermute | solution.py:248
  105.1 8.7 %collective-permute-start.19 = (f32[256,256]{1,0:T(8,128)}, f32[256,256]{1,0:T(8,128)S(1)}, u32[]{:S(2)}, u32[]{:S(2)}) collective-permute-start(f32[256,256]{1,0:T(8,128)} %fusion.4), channel_id=1, source_target_pairs={{0,64},{16,80},{32,96},{48,112},{64,128},{80,144},{96,160},{112,17... | collective-permute-start | bytes 786440 | tf_op jit(solution)/shard_map/ppermute | solution.py:248
  105.2 8.7 %collective-permute-start.16 = (f32[256,256]{1,0:T(8,128)S(1)}, f32[256,256]{1,0:T(8,128)S(1)}, u32[]{:S(2)}, u32[]{:S(2)}) collective-permute-start(f32[256,256]{1,0:T(8,128)S(1)} %fusion.5), channel_id=1, source_target_pairs={{0,48},{16,0},{32,16},{48,32},{64,112},{80,64},{96,80},{112,96},{1... | collective-permute-start | bytes 786440 | tf_op jit(solution)/shard_map/ppermute | solution.py:241
  108.5 7.6 %collective-permute-start.15 = (f32[256,256]{1,0:T(8,128)S(1)}, f32[256,256]{1,0:T(8,128)S(1)}, u32[]{:S(2)}, u32[]{:S(2)}) collective-permute-start(f32[256,256]{1,0:T(8,128)S(1)} %fusion.6), channel_id=1, source_target_pairs={{0,16},{16,32},{32,48},{48,0},{64,80},{80,96},{96,112},{112,64},{1... | collective-permute-start | bytes 786440 | tf_op jit(solution)/shard_map/ppermute | solution.py:241
  121.0 7.9 %collective-permute-start.21 = (f32[256,256]{1,0:T(8,128)}, f32[256,256]{1,0:T(8,128)S(1)}, u32[]{:S(2)}, u32[]{:S(2)}) collective-permute-start(f32[256,256]{1,0:T(8,128)} %get-tuple-element.65), channel_id=1, source_target_pairs={{0,64},{16,80},{32,96},{48,112},{64,128},{80,144},{96,160},{112,17... | collective-permute-start | bytes 786440 | tf_op jit(solution)/shard_map/ppermute | solution.py:248
  121.1 11.9 %collective-permute-start.22 = (f32[256,256]{1,0:T(8,128)}, f32[256,256]{1,0:T(8,128)S(1)}, u32[]{:S(2)}, u32[]{:S(2)}) collective-permute-start(f32[256,256]{1,0:T(8,128)} %get-tuple-element.66), channel_id=1, source_target_pairs={{0,128},{16,144},{32,160},{48,176},{64,192},{80,208},{96,224},{112... | collective-permute-start | bytes 786440 | tf_op jit(solution)/shard_map/ppermute | solution.py:248
  125.7 7.4 %collective-permute-start.23 = (f32[256,256]{1,0:T(8,128)}, f32[256,256]{1,0:T(8,128)S(1)}, u32[]{:S(2)}, u32[]{:S(2)}) collective-permute-start(f32[256,256]{1,0:T(8,128)} %get-tuple-element.67), channel_id=1, source_target_pairs={{0,192},{16,208},{32,224},{48,240},{64,0},{80,16},{96,32},{112,48}... | collective-permute-start | bytes 786440 | tf_op jit(solution)/shard_map/ppermute | solution.py:248
  125.7 10.6 %collective-permute-start.24 = (f32[256,256]{1,0:T(8,128)}, f32[256,256]{1,0:T(8,128)S(1)}, u32[]{:S(2)}, u32[]{:S(2)}) collective-permute-start(f32[256,256]{1,0:T(8,128)} %get-tuple-element.69), channel_id=1, source_target_pairs={{0,16},{16,32},{32,48},{48,0},{64,80},{80,96},{96,112},{112,64},{1... | collective-permute-start | bytes 786440 | tf_op jit(solution)/shard_map/ppermute | solution.py:241
  125.7 10.6 %collective-permute-start.25 = (f32[256,256]{1,0:T(8,128)}, f32[256,256]{1,0:T(8,128)S(1)}, u32[]{:S(2)}, u32[]{:S(2)}) collective-permute-start(f32[256,256]{1,0:T(8,128)} %get-tuple-element.70), channel_id=1, source_target_pairs={{0,32},{16,48},{32,0},{48,16},{64,96},{80,112},{96,64},{112,80},{1... | collective-permute-start | bytes 786440 | tf_op jit(solution)/shard_map/ppermute | solution.py:241
  128.9 8.3 %collective-permute-start.26 = (f32[256,256]{1,0:T(8,128)}, f32[256,256]{1,0:T(8,128)S(1)}, u32[]{:S(2)}, u32[]{:S(2)}) collective-permute-start(f32[256,256]{1,0:T(8,128)} %get-tuple-element.71), channel_id=1, source_target_pairs={{0,48},{16,0},{32,16},{48,32},{64,112},{80,64},{96,80},{112,96},{1... | collective-permute-start | bytes 786440 | tf_op jit(solution)/shard_map/ppermute | solution.py:241
  140.7 27.4 %collective-permute-start.27 = (f32[2,256,256]{2,1,0:T(8,128)}, f32[2,256,256]{2,1,0:T(8,128)S(1)}, u32[]{:S(2)}, u32[]{:S(2)}) collective-permute-start(f32[2,256,256]{2,1,0:T(8,128)} %get-tuple-element.72), channel_id=1, source_target_pairs={{112,32},{0,2},{32,18},{80,48},{208,46},{160,226},{128,242},{240,6... | collective-permute-start | bytes 1572872 | tf_op jit(solution)/shard_map/ppermute | solution.py:352
  143.5 24.6 %collective-permute-start.28 = (f32[2,256,256]{2,1,0:T(8,128)}, f32[2,256,256]{2,1,0:T(8,128)S(1)}, u32[]{:S(2)}, u32[]{:S(2)}) collective-permute-start(f32[2,256,256]{2,1,0:T(8,128)} %get-tuple-element.73), channel_id=1, source_target_pairs={{112,2},{0,48},{32,32},{80,18},{208,226},{160,62},{128,46},{240,24... | collective-permute-start | bytes 1572872 | tf_op jit(solution)/shard_map/ppermute | solution.py:351
  181.9 15.1 %all-to-all-start.2 = ((f32[16,16,128]{2,1,0:T(8,128)}), f32[16,16,128]{2,1,0:T(8,128)S(1)}, u32[]{:S(2)}, u32[]{:S(2)}) async-start(f32[16,16,128]{2,1,0:T(8,128)} %broadcast_in_dim.24), calls=%async_computation.2 | async-start | bytes 262144 | tf_op jit(solution)/shard_map/all_to_all | solution.py:275
  (39 other events, 165.1 us)

commit v7 on v6

--- a/solution.py
+++ b/solution.py
@@ -136,15 +136,14 @@
 
 
 def early_kernel(device, table, one, two, block, *refs):
-    outs, lefts, turned = refs[:10], refs[10], refs[11]
+    outs, lefts, turned = refs[:8], refs[8], refs[9]
     stack(lefts, one, two)
     turn(turned, block)
     for t, j in ORDER:
         for color, rhs in enumerate((block, turned)):
             index = table[device[0] * 16 + color * 8 + t * 2 + j]
             lhs = rows_of(lefts.at[index // 4], index // 2 % 2)
-            out = stores(*outs[5 * color : 5 * color + 5])[t, j]
-            out[...] = matmul(lhs, rows_of(rhs, index % 2))
+            outs[4 * color + t][j] = matmul(lhs, rows_of(rhs, index % 2))
 
 
 def late_kernel(device, table, one, two, block, diagonal, *refs):
@@ -166,9 +165,8 @@
 
 def sum_kernel(*refs):
     for color in range(2):
-        own, right, left, right2, left2 = refs[5 * color : 5 * color + 5]
-        refs[10 + color][0] = own[0] + right2[...] + left[0]
-        refs[10 + color][1] = own[1] + right[0] + left2[...]
+        own, one, two, three = refs[4 * color : 4 * color + 4]
+        refs[8 + color][...] = (own[...] + one[...]) + (two[...] + three[...])
 
 
 def finish_kernel(device, ahead, *refs):
@@ -190,9 +188,7 @@
         "second": pl.BlockSpec((1, slab, quarter), lambda i: (1, i, 0)),
         "both": pl.BlockSpec((2, slab, quarter), lambda i: (0, i, 0)),
     }
-    pattern = ["both", "second", "second", "one", "one"]
-    if len(parts) == 12:
-        pattern = ["both"] + pattern
+    pattern = ["both"] * 4 if len(parts) == 8 else ["both", "both", "second", "second", "one", "one"]
     size = {"one": (quarter, quarter), "both": (2, quarter, quarter)}
     return pl.pallas_call(
         kernel,
@@ -266,7 +262,8 @@
 
 
 def direct(outs, shift):
-    return (outs[0],) + tuple(shift(outs[t], t) for t in range(1, SIDE))
+    far = shift(outs[2], 2)
+    return outs[0], shift(outs[1], 1), far, shift(outs[3], 3)
 
 
 def exchange(parts, axis):
@@ -318,19 +315,17 @@
     shapes = 2 * ([(2, quarter, quarter)] * 2 + [(quarter, quarter)] * 2 + [(2, quarter, quarter)])
     axes = (shift_x, shift_y)
 
-    def chunks(kernel, table, blocks):
+    def chunks(kernel, table, blocks, shapes):
         scalars = device, jnp.asarray(table.reshape(-1))
         return kernel_call(kernel, scalars, blocks, shapes, 16 * product, stacks)
 
-    outs = chunks(early_kernel, early, (here, below, above))
-    received = [ring_start(*outs[5 * i : 5 * i + 2], axes[i]) for i in range(2)]
+    outs = chunks(early_kernel, early, (here, below, above), [(2, quarter, quarter)] * 8)
+    early_parts = [direct(outs[4 * i : 4 * i + 4], axes[i]) for i in range(2)]
     (diagonal,) = kernel_call(
         diagonal_kernel, (), (here,), [(4, quarter, quarter)], 6 * product, found
     )
-    sums = [ring_sums(received[i], outs[5 * i + 2 : 5 * i + 4]) for i in range(2)]
-    early_parts = [ring_end(outs[5 * i + 4], received[i], sums[i], axes[i]) for i in range(2)]
     early_total = by_slabs(sum_kernel, (), early_parts[0] + early_parts[1], ["both"] * 2, 0)
-    outs = chunks(late_kernel, late, (below, below2, above2, diagonal))
+    outs = chunks(late_kernel, late, (below, below2, above2, diagonal), shapes)
     received = [ring_start(*outs[5 * i : 5 * i + 2], axes[i]) for i in range(2)]
     sums = [ring_sums(received[i], outs[5 * i + 2 : 5 * i + 4]) for i in range(2)]
     late_parts = [ring_end(outs[5 * i + 4], received[i], sums[i], axes[i]) for i in range(2)]

time: 213 us -> 236 us (1.11)
  blocking collectives: 21.9 us -> 48.9 us
  starting transfers between devices: 63.4 us -> 47.6 us
  waiting for transfers between devices: 81.6 us -> 93.7 us
    all_to_all x1 -> x2, blocking collectives: 11.6 us -> 38.6 us  [exchange(): return lax.all_to_all(copies, axis, 0, 0)]
    ppermute x11 -> x10, waiting for transfers between devices: 9.8 us -> 28.8 us  [shift_x(): return lax.ppermute(value, 'row', pairs)]
    ppermute x4, waiting for transfers between devices: 1.91 us -> 15.3 us  [shift_z(): lax.ppermute(value, 'col', [(c, (c + step) % PLANES) for c in range(PLANE...]
    all_to_all x2 -> x1, starting transfers between devices: 16.6 us -> 4.1 us  [exchange(): return lax.all_to_all(copies, axis, 0, 0)]
    ppermute x11 -> x10, waiting for transfers between devices: 18.9 us -> 8.36 us  [shift_y(): return lax.ppermute(value, 'row', pairs)]
    all_to_all x2 -> x1, waiting for transfers between devices: 15.6 us -> 7.99 us  [exchange(): return lax.all_to_all(copies, axis, 0, 0)]
    ppermute x11 -> x10, starting transfers between devices: 13.9 us -> 11.4 us  [shift_y(): return lax.ppermute(value, 'row', pairs)]
    ppermute x11 -> x10, starting transfers between devices: 12 us -> 11 us  [shift_x(): return lax.ppermute(value, 'row', pairs)]
  transfers between devices with their start and end apart: 31 -> 28, of which waited for: 14 -> 14; matrix products, arithmetic and copies ran while one was open for 2% -> 2% of each run, Pallas kernels for 10% -> 6%
where the time goes in v7:
time: 236 us; the launch traced here: 233 us
  waiting for transfers between devices  93.7 us (40%)
  blocking collectives  48.9 us (21%)
  starting transfers between devices  47.6 us (20%)
  Pallas kernels  27.9 us (12%)
  local copies, waits for them, and re-layouts  9.38 us (4%)
  other arithmetic  4.59 us (2%)
    all_to_all x2, blocking collectives, exchange(): return lax.all_to_all(copies, axis, 0, 0)  38.6 us
    ppermute x10, waiting for transfers between devices, shift_x(): return lax.ppermute(value, 'row', pairs)  28.8 us
    pallas_call x4, Pallas kernels, kernel_call(): pl.pallas_call(kernel, out_shape=shapes, in_specs=[smem] * len(scalars) +...  19.6 us
    ppermute x1, waiting for transfers between devices, starting_gains(): share = lax.ppermute(initial_gains, ('row', 'col'), pairs)  19.5 us
    ppermute x4, waiting for transfers between devices, shift_z(): lax.ppermute(value, 'col', [(c, (c + step) % PLANES) for c in range(PLANE...  15.3 us
    ppermute x1, waiting for transfers between devices, vis_tiles(): two = lax.ppermute(two, ('row', 'col'), second)  13.7 us
    ppermute x10, starting transfers between devices, shift_y(): return lax.ppermute(value, 'row', pairs)  11.4 us
    ppermute x10, starting transfers between devices, shift_x(): return lax.ppermute(value, 'row', pairs)  11 us
  transfers between devices with their start and end apart: 28, of which 14 were waited for; matrix products, arithmetic and copies ran while one was open for 2% of the time, Pallas kernels for 6%

profile of v7, /device:TPU:64, one launch (start us, length us, event | category | flops | bytes accessed | tf_op | source)
XLA Modules:
  0.0 233.3 jit_solution(6581067624287009256)
XLA Ops:
  0.0 1.5 copy.28
  1.7 1.9 collective-permute-start.2
  3.6 7.8 %collective-permute-start = (f32[2,32]{1,0:T(2,128)S(1)}, f32[2,32]{1,0:T(2,128)S(1)}, u32[]{:S(2)}, u32[]{:S(2)}) collective-permute-start(f32[2,32]{1,0:T(2,128)S(1)} %copy-done.30), channel_id=1, source_target_pairs={{0,0},{2,16},{4,32},{6,48},{8,64},{10,80},{12,96},{14,112},{16,128... | collective-permute-start | bytes 776 | tf_op jit(solution)/shard_map/ppermute | solution.py:363
  11.5 19.5 %collective-permute-done = f32[2,32]{1,0:T(2,128)S(1)} collective-permute-done((f32[2,32]{1,0:T(2,128)S(1)}, f32[2,32]{1,0:T(2,128)S(1)}, u32[]{:S(2)}, u32[]{:S(2)}) %collective-permute-start) | collective-permute-done | bytes 288 | tf_op jit(solution)/shard_map/ppermute | solution.py:363
  31.0 16.9 %all_to_all.20 = f32[16,2,32]{2,1,0:T(2,128)S(1)} all-to-all(f32[16,2,32]{2,1,0:T(2,128)S(1)} %broadcast_in_dim.20), channel_id=1, replica_groups=mesh['row'=16,'col'=8,'chan'=2] {'row'}, dimensions={0} | all-to-all | bytes 8192 | tf_op jit(solution)/shard_map/all_to_all | solution.py:272
  48.1 2.0 collective-permute-start.10
  50.1 4.4 %shard_map.84.diagonal = f32[4,256,256]{2,1,0:T(8,128)} custom-call(bf16[512,1024]{1,0:T(8,128)(2,1)} %bitcast.75), custom_call_target="tpu_custom_call" | custom-call | flops 805306368 | bytes 2097152 | tf_op jit(solution)/shard_map/pallas_call | solution.py:223
  55.1 15.3 %collective-permute-done.9.two = bf16[512,1024]{1,0:T(8,128)(2,1)} collective-permute-done((bf16[512,1024]{1,0:T(8,128)(2,1)}, bf16[512,1024]{1,0:T(8,128)(2,1)}, u32[]{:S(2)}, u32[]{:S(2)}) %collective-permute-start.9) | collective-permute-done | bytes 1048608 | tf_op jit(solution)/shard_map/ppermute | solution.py:248
  70.4 6.3 %shard_map.85 = (f32[2,256,256]{2,1,0:T(8,128)}, f32[2,256,256]{2,1,0:T(8,128)}, f32[256,256]{1,0:T(8,128)}, f32[256,256]{1,0:T(8,128)}, f32[2,256,256]{2,1,0:T(...) custom-call(s32[2]{0:T(128)} %pad_add_fusion.device, ...), custom_call_target="tpu_custom_call" | custom-call | flops 2147483648 | bytes 8388608 | tf_op jit(solution)/shard_map/pallas_call | solution.py:223
  78.0 6.0 %shard_map.82 = (f32[2,256,256]{2,1,0:T(8,128)}, f32[2,256,256]{2,1,0:T(8,128)}, f32[2,256,256]{2,1,0:T(8,128)}, f32[2,256,256]{2,1,0:T(8,128)}, f32[2,256,256]{...) custom-call(s32[2]{0:T(128)} %pad_add_fusion.device, ...), custom_call_target="tpu_custom_call" | custom-call | flops 2147483648 | bytes 7340032 | tf_op jit(solution)/shard_map/pallas_call | solution.py:223
  85.5 2.7 %collective-permute-start.12 = (f32[2,256,256]{2,1,0:T(8,128)S(1)}, f32[2,256,256]{2,1,0:T(8,128)S(1)}, u32[]{:S(2)}, u32[]{:S(2)}) collective-permute-start(f32[2,256,256]{2,1,0:T(8,128)S(1)} %copy-done.28), channel_id=1, source_target_pairs={{0,48},{16,0},{32,16},{48,32},{64,112},{80,64},{96,80},{112,96},{1... | collective-permute-start | bytes 1572872 | tf_op jit(solution)/shard_map/ppermute | solution.py:237
  88.2 1.5 collective-permute-start.4
  89.8 10.5 %collective-permute-done.3.refs_1_ = f32[2,256,256]{2,1,0:T(8,128)S(1)} collective-permute-done((f32[2,256,256]{2,1,0:T(8,128)}, f32[2,256,256]{2,1,0:T(8,128)S(1)}, u32[]{:S(2)}, u32[]{:S(2)}) %collective-permute-start.3) | collective-permute-done | bytes 524320 | tf_op jit(solution)/shard_map/ppermute | solution.py:237
  101.3 9.6 %collective-permute-done.12.refs_3_ = f32[2,256,256]{2,1,0:T(8,128)S(1)} collective-permute-done((f32[2,256,256]{2,1,0:T(8,128)S(1)}, f32[2,256,256]{2,1,0:T(8,128)S(1)}, u32[]{:S(2)}, u32[]{:S(2)}) %collective-permute-start.12) | collective-permute-done | bytes 524320 | tf_op jit(solution)/shard_map/ppermute | solution.py:237
  113.0 4.6 %collective-permute-done.11.refs_2_ = f32[2,256,256]{2,1,0:T(8,128)S(1)} collective-permute-done((f32[2,256,256]{2,1,0:T(8,128)S(1)}, f32[2,256,256]{2,1,0:T(8,128)S(1)}, u32[]{:S(2)}, u32[]{:S(2)}) %collective-permute-start.11) | collective-permute-done | bytes 524320 | tf_op jit(solution)/shard_map/ppermute | solution.py:237
  122.0 2.5 %collective-permute-done.7.refs_6_ = f32[2,256,256]{2,1,0:T(8,128)} collective-permute-done((f32[2,256,256]{2,1,0:T(8,128)S(1)}, f32[2,256,256]{2,1,0:T(8,128)}, u32[]{:S(2)}, u32[]{:S(2)}) %collective-permute-start.7) | collective-permute-done | bytes 524320 | tf_op jit(solution)/shard_map/ppermute | solution.py:244
  124.5 4.2 %collective-permute-done.8.refs_7_ = f32[2,256,256]{2,1,0:T(8,128)S(1)} collective-permute-done((f32[2,256,256]{2,1,0:T(8,128)S(1)}, f32[2,256,256]{2,1,0:T(8,128)S(1)}, u32[]{:S(2)}, u32[]{:S(2)}) %collective-permute-start.8) | collective-permute-done | bytes 524320 | tf_op jit(solution)/shard_map/ppermute | solution.py:244
  129.5 4.1 %shard_map.83 = (f32[2,256,256]{2,1,0:T(8,128)}, f32[2,256,256]{2,1,0:T(8,128)}) custom-call(f32[2,256,256]{2,1,0:T(8,128)} %get-tuple-element.40.refs_0_, f32[2,256,256]{2,1,0:T(8,128)} %copy-done.6, f32[2,256,256]{2,1,0:T(8,128)} %copy-done.7, f32[2,256,256]{2,1,0:T(8,128)} %collective-permute-done.5.refs_3_, f32[2,256,256]{2,1,0:T(8,128)} %get-tuple-element.44.refs_4_, ...), custom_call_target="tpu_custom_call" | custom-call | flops 524288 | bytes 4718592 | tf_op jit(solution)/shard_map/pallas_call | solution.py:193
  134.6 4.2 %shard_map.86 = (f32[256,256]{1,0:T(8,128)}, f32[256,256]{1,0:T(8,128)}, f32[256,256]{1,0:T(8,128)}, f32[256,256]{1,0:T(8,128)}, f32[256,256]{1,0:T(8,128)}, /*i...) custom-call(s32[2]{0:T(128)} %pad_add_fusion.device, s32[1024]{0:T(1024)} %constant.47.clone.ahead, ...), custom_call_target="tpu_custom_call" | custom-call | flops 524288 | bytes 4718592 | tf_op jit(solution)/shard_map/pallas_call | solution.py:193
  139.7 3.3 %collective-permute-start.20 = (f32[256,256]{1,0:T(8,128)}, f32[256,256]{1,0:T(8,128)S(1)}, u32[]{:S(2)}, u32[]{:S(2)}) collective-permute-start(f32[256,256]{1,0:T(8,128)} %get-tuple-element.62), channel_id=1, source_target_pairs={{0,128},{16,144},{32,160},{48,176},{64,192},{80,208},{96,224},{112... | collective-permute-start | bytes 786440 | tf_op jit(solution)/shard_map/ppermute | solution.py:244
  143.0 3.6 %collective-permute-start.23 = (f32[256,256]{1,0:T(8,128)}, f32[256,256]{1,0:T(8,128)S(1)}, u32[]{:S(2)}, u32[]{:S(2)}) collective-permute-start(f32[256,256]{1,0:T(8,128)} %get-tuple-element.66), channel_id=1, source_target_pairs={{0,32},{16,48},{32,0},{48,16},{64,96},{80,112},{96,64},{112,80},{1... | collective-permute-start | bytes 786440 | tf_op jit(solution)/shard_map/ppermute | solution.py:237
  146.7 2.1 collective-permute-start.24
  148.8 1.5 collective-permute-done.20.refs_2_
  150.8 3.1 %collective-permute-done.23.refs_6_ = f32[256,256]{1,0:T(8,128)S(1)} collective-permute-done((f32[256,256]{1,0:T(8,128)}, f32[256,256]{1,0:T(8,128)S(1)}, u32[]{:S(2)}, u32[]{:S(2)}) %collective-permute-start.23) | collective-permute-done | bytes 262176 | tf_op jit(solution)/shard_map/ppermute | solution.py:237
  155.1 2.8 %shard_map.87 = (f32[2,256,256]{2,1,0:T(8,128)}, f32[2,256,256]{2,1,0:T(8,128)}) custom-call(s32[2]{0:T(128)} %pad_add_fusion.device, s32[256]{0:T(256)} %constant.48.clone.flags, f32[256,256]{1,0:T(8,128)} %get-tuple-element.60.refs_0_, f32[256,256]{1,0:T(8,128)} %copy-done.15, f32[256,256]{1,0:T(8,128)} %copy-done.16, f32[256,256]{1,0:T(8,128)} %copy-done.19, ...), custom_call_target="tpu_custom_call" | custom-call | bytes 3145728 | tf_op jit(solution)/shard_map/pallas_call | solution.py:223
  157.9 5.1 %collective-permute-start.25 = (f32[2,256,256]{2,1,0:T(8,128)}, f32[2,256,256]{2,1,0:T(8,128)S(1)}, u32[]{:S(2)}, u32[]{:S(2)}) collective-permute-start(f32[2,256,256]{2,1,0:T(8,128)} %get-tuple-element.68), channel_id=1, source_target_pairs={{112,32},{0,2},{32,18},{80,48},{208,46},{160,226},{128,242},{240,6... | collective-permute-start | bytes 1572872 | tf_op jit(solution)/shard_map/ppermute | solution.py:347
  163.0 4.0 %collective-permute-start.26 = (f32[2,256,256]{2,1,0:T(8,128)}, f32[2,256,256]{2,1,0:T(8,128)S(1)}, u32[]{:S(2)}, u32[]{:S(2)}) collective-permute-start(f32[2,256,256]{2,1,0:T(8,128)} %get-tuple-element.69), channel_id=1, source_target_pairs={{112,2},{0,48},{32,32},{80,18},{208,226},{160,62},{128,46},{240,24... | collective-permute-start | bytes 1572872 | tf_op jit(solution)/shard_map/ppermute | solution.py:346
  169.8 13.7 %collective-permute-done.25 = f32[2,256,256]{2,1,0:T(8,128)S(1)} collective-permute-done((f32[2,256,256]{2,1,0:T(8,128)}, f32[2,256,256]{2,1,0:T(8,128)S(1)}, u32[]{:S(2)}, u32[]{:S(2)}) %collective-permute-start.25) | collective-permute-done | bytes 524320 | tf_op jit(solution)/shard_map/ppermute | solution.py:347
  184.5 21.8 %all_to_all.21 = f32[8,6,128]{2,1,0:T(8,128)S(1)} all-to-all(f32[8,6,128]{2,1,0:T(8,128)S(1)} %broadcast_in_dim.22), channel_id=1, replica_groups=mesh['row'=16,'col'=8,'chan'=2] {'col'}, dimensions={0} | all-to-all | bytes 49152 | tf_op jit(solution)/shard_map/all_to_all | solution.py:272
  207.4 4.1 %all-to-all-start.2 = ((f32[16,16,128]{2,1,0:T(8,128)}), f32[16,16,128]{2,1,0:T(8,128)S(1)}, u32[]{:S(2)}, u32[]{:S(2)}) async-start(f32[16,16,128]{2,1,0:T(8,128)} %broadcast_in_dim.24), calls=%async_computation.2 | async-start | bytes 262144 | tf_op jit(solution)/shard_map/all_to_all | solution.py:272
  211.5 8.0 %all-to-all-done.2 = f32[16,16,128]{2,1,0:T(8,128)S(1)} async-done(((f32[16,16,128]{2,1,0:T(8,128)}), f32[16,16,128]{2,1,0:T(8,128)S(1)}, u32[]{:S(2)}, u32[]{:S(2)}) %all-to-all-start.2) | async-done | bytes 131104 | tf_op jit(solution)/shard_map/all_to_all | solution.py:272
  222.4 10.3 %all_to_all.22 = f32[8,3,32]{2,1,0:T(4,128)S(1)} all-to-all(f32[8,3,32]{2,1,0:T(4,128)S(1)} %maximum_bitcast_fusion), channel_id=1, replica_groups=mesh['row'=16,'col'=8,'chan'=2] {'col'}, dimensions={0} | all-to-all | bytes 6144 | tf_op jit(solution)/shard_map/all_to_all | solution.py:408
  (154 shorter events, 23.1 us)
Async XLA Ops:
  1.5 48.6 %copy-start.5 = (bf16[64,8,2,512]{3,1,2,0:T(8,128)(2,1)}, bf16[64,8,2,512]{3,1,2,0:T(8,128)(2,1)S(1)}, u32[]{:S(2)}) copy-start(bf16[64,8,2,512]{3,1,2,0:T(8,128)(2,1)S(1)} %copy.28) | copy-start | bytes 3145732
  1.5 46.5 %collective-permute-start.1 = (bf16[512,1024]{1,0:T(8,128)(2,1)S(1)}, bf16[512,1024]{1,0:T(8,128)(2,1)S(1)}, u32[]{:S(2)}, u32[]{:S(2)}) collective-permute-start(bf16[512,1024]{1,0:T(8,128)(2,1)S(1)} %bitcast.73), channel_id=1, source_target_pairs={{0,14},{2,0},{4,2},{6,4},{8,6},{10,8},{12,10},{14,12},{1,15},{3,1}... | collective-permute-start | bytes 3145736 | tf_op jit(solution)/shard_map/ppermute | solution.py:248
  1.7 46.3 %collective-permute-start.2 = (bf16[512,1024]{1,0:T(8,128)(2,1)S(1)}, bf16[512,1024]{1,0:T(8,128)(2,1)}, u32[]{:S(2)}, u32[]{:S(2)}) collective-permute-start(bf16[512,1024]{1,0:T(8,128)(2,1)S(1)} %bitcast.74), channel_id=1, source_target_pairs={{0,2},{2,4},{4,6},{6,8},{8,10},{10,12},{12,14},{14,0},{1,3},{3,5},... | collective-permute-start | bytes 3145736 | tf_op jit(solution)/shard_map/ppermute | solution.py:248
  3.6 27.4 %collective-permute-start = (f32[2,32]{1,0:T(2,128)S(1)}, f32[2,32]{1,0:T(2,128)S(1)}, u32[]{:S(2)}, u32[]{:S(2)}) collective-permute-start(f32[2,32]{1,0:T(2,128)S(1)} %copy-done.30), channel_id=1, source_target_pairs={{0,0},{2,16},{4,32},{6,48},{8,64},{10,80},{12,96},{14,112},{16,128... | collective-permute-start | bytes 776 | tf_op jit(solution)/shard_map/ppermute | solution.py:363
  48.0 22.4 %collective-permute-start.9 = (bf16[512,1024]{1,0:T(8,128)(2,1)}, bf16[512,1024]{1,0:T(8,128)(2,1)}, u32[]{:S(2)}, u32[]{:S(2)}) collective-permute-start(bf16[512,1024]{1,0:T(8,128)(2,1)} %collective-permute-done.2.two.one), channel_id=1, source_target_pairs={{0,2},{2,4},{4,6},{6,8},{8,10},{10,12},{12,14},{14,0},{1,3},{3,5},... | collective-permute-start | bytes 3145736 | tf_op jit(solution)/shard_map/ppermute | solution.py:248
  48.1 22.3 %collective-permute-start.10 = (bf16[512,1024]{1,0:T(8,128)(2,1)S(1)}, bf16[512,1024]{1,0:T(8,128)(2,1)}, u32[]{:S(2)}, u32[]{:S(2)}) collective-permute-start(bf16[512,1024]{1,0:T(8,128)(2,1)S(1)} %collective-permute-done.1.block), channel_id=1, source_target_pairs={{0,14},{2,0},{4,2},{6,4},{8,6},{10,8},{12,10},{14,12},{1,15},{3,1}... | collective-permute-start | bytes 3145736 | tf_op jit(solution)/shard_map/ppermute | solution.py:248
  76.8 11.4 %collective-permute-start.16 = (f32[2,256,256]{2,1,0:T(8,128)}, f32[2,256,256]{2,1,0:T(8,128)S(1)}, u32[]{:S(2)}, u32[]{:S(2)}) collective-permute-start(f32[2,256,256]{2,1,0:T(8,128)} %get-tuple-element.57), channel_id=1, source_target_pairs={{0,192},{16,208},{32,224},{48,240},{64,0},{80,16},{96,32},{112,48}... | collective-permute-start | bytes 1572872 | tf_op jit(solution)/shard_map/ppermute | solution.py:244
  84.0 26.9 %copy-start.26 = (f32[2,256,256]{2,1,0:T(8,128)S(1)}, f32[2,256,256]{2,1,0:T(8,128)}, u32[]{:S(2)}) copy-start(f32[2,256,256]{2,1,0:T(8,128)} %get-tuple-element.46) | copy-start | bytes 1572868
  84.0 16.3 %collective-permute-start.3 = (f32[2,256,256]{2,1,0:T(8,128)}, f32[2,256,256]{2,1,0:T(8,128)S(1)}, u32[]{:S(2)}, u32[]{:S(2)}) collective-permute-start(f32[2,256,256]{2,1,0:T(8,128)} %get-tuple-element.41), channel_id=1, source_target_pairs={{0,16},{16,32},{32,48},{48,0},{64,80},{80,96},{96,112},{112,64},{1... | collective-permute-start | bytes 1572872 | tf_op jit(solution)/shard_map/ppermute | solution.py:237
  84.7 15.7 %collective-permute-start.15 = (f32[2,256,256]{2,1,0:T(8,128)S(1)}, f32[2,256,256]{2,1,0:T(8,128)S(1)}, u32[]{:S(2)}, u32[]{:S(2)}) collective-permute-start(f32[2,256,256]{2,1,0:T(8,128)S(1)} %copy-done.29), channel_id=1, source_target_pairs={{0,64},{16,80},{32,96},{48,112},{64,128},{80,144},{96,160},{112,17... | collective-permute-start | bytes 1572872 | tf_op jit(solution)/shard_map/ppermute | solution.py:244
  85.5 25.4 %collective-permute-start.12 = (f32[2,256,256]{2,1,0:T(8,128)S(1)}, f32[2,256,256]{2,1,0:T(8,128)S(1)}, u32[]{:S(2)}, u32[]{:S(2)}) collective-permute-start(f32[2,256,256]{2,1,0:T(8,128)S(1)} %copy-done.28), channel_id=1, source_target_pairs={{0,48},{16,0},{32,16},{48,32},{64,112},{80,64},{96,80},{112,96},{1... | collective-permute-start | bytes 1572872 | tf_op jit(solution)/shard_map/ppermute | solution.py:237
  88.2 29.4 %collective-permute-start.11 = (f32[2,256,256]{2,1,0:T(8,128)S(1)}, f32[2,256,256]{2,1,0:T(8,128)S(1)}, u32[]{:S(2)}, u32[]{:S(2)}) collective-permute-start(f32[2,256,256]{2,1,0:T(8,128)S(1)} %copy-done.27), channel_id=1, source_target_pairs={{0,16},{16,32},{32,48},{48,0},{64,80},{80,96},{96,112},{112,64},{1... | collective-permute-start | bytes 1572872 | tf_op jit(solution)/shard_map/ppermute | solution.py:237
  88.2 24.8 %copy-start.1 = (f32[2,256,256]{2,1,0:T(8,128)}, f32[2,256,256]{2,1,0:T(8,128)S(1)}, u32[]{:S(2)}) copy-start(f32[2,256,256]{2,1,0:T(8,128)S(1)} %collective-permute-done.16.refs_9_) | copy-start | bytes 1572868
  88.2 31.2 %collective-permute-start.4 = (f32[2,256,256]{2,1,0:T(8,128)}, f32[2,256,256]{2,1,0:T(8,128)S(1)}, u32[]{:S(2)}, u32[]{:S(2)}) collective-permute-start(f32[2,256,256]{2,1,0:T(8,128)} %get-tuple-element.42), channel_id=1, source_target_pairs={{0,32},{16,48},{32,0},{48,16},{64,96},{80,112},{96,64},{112,80},{1... | collective-permute-start | bytes 1572872 | tf_op jit(solution)/shard_map/ppermute | solution.py:237
  89.8 27.8 %copy-start.25 = (f32[2,256,256]{2,1,0:T(8,128)S(1)}, f32[2,256,256]{2,1,0:T(8,128)}, u32[]{:S(2)}) copy-start(f32[2,256,256]{2,1,0:T(8,128)} %get-tuple-element.47) | copy-start | bytes 1572868
  100.3 20.5 %collective-permute-start.5 = (f32[2,256,256]{2,1,0:T(8,128)}, f32[2,256,256]{2,1,0:T(8,128)}, u32[]{:S(2)}, u32[]{:S(2)}) collective-permute-start(f32[2,256,256]{2,1,0:T(8,128)} %get-tuple-element.43), channel_id=1, source_target_pairs={{0,48},{16,0},{32,16},{48,32},{64,112},{80,64},{96,80},{112,96},{1... | collective-permute-start | bytes 1572872 | tf_op jit(solution)/shard_map/ppermute | solution.py:237
  100.3 21.2 %collective-permute-start.6 = (f32[2,256,256]{2,1,0:T(8,128)}, f32[2,256,256]{2,1,0:T(8,128)}, u32[]{:S(2)}, u32[]{:S(2)}) collective-permute-start(f32[2,256,256]{2,1,0:T(8,128)} %get-tuple-element.45), channel_id=1, source_target_pairs={{0,64},{16,80},{32,96},{48,112},{64,128},{80,144},{96,160},{112,17... | collective-permute-start | bytes 1572872 | tf_op jit(solution)/shard_map/ppermute | solution.py:244
  110.9 13.6 %collective-permute-start.7 = (f32[2,256,256]{2,1,0:T(8,128)S(1)}, f32[2,256,256]{2,1,0:T(8,128)}, u32[]{:S(2)}, u32[]{:S(2)}) collective-permute-start(f32[2,256,256]{2,1,0:T(8,128)S(1)} %copy-done.26), channel_id=1, source_target_pairs={{0,128},{16,144},{32,160},{48,176},{64,192},{80,208},{96,224},{112... | collective-permute-start | bytes 1572872 | tf_op jit(solution)/shard_map/ppermute | solution.py:244
  117.7 11.1 %collective-permute-start.8 = (f32[2,256,256]{2,1,0:T(8,128)S(1)}, f32[2,256,256]{2,1,0:T(8,128)S(1)}, u32[]{:S(2)}, u32[]{:S(2)}) collective-permute-start(f32[2,256,256]{2,1,0:T(8,128)S(1)} %copy-done.25), channel_id=1, source_target_pairs={{0,192},{16,208},{32,224},{48,240},{64,0},{80,16},{96,32},{112,48}... | collective-permute-start | bytes 1572872 | tf_op jit(solution)/shard_map/ppermute | solution.py:244
  119.5 14.2 %collective-permute-start.18 = (f32[256,256]{1,0:T(8,128)S(1)}, f32[256,256]{1,0:T(8,128)S(1)}, u32[]{:S(2)}, u32[]{:S(2)}) collective-permute-start(f32[256,256]{1,0:T(8,128)S(1)} %fusion.3), channel_id=1, source_target_pairs={{0,192},{16,208},{32,224},{48,240},{64,0},{80,16},{96,32},{112,48}... | collective-permute-start | bytes 786440 | tf_op jit(solution)/shard_map/ppermute | solution.py:244
  120.9 12.8 %collective-permute-start.17 = (f32[256,256]{1,0:T(8,128)}, f32[256,256]{1,0:T(8,128)S(1)}, u32[]{:S(2)}, u32[]{:S(2)}) collective-permute-start(f32[256,256]{1,0:T(8,128)} %fusion.4), channel_id=1, source_target_pairs={{0,64},{16,80},{32,96},{48,112},{64,128},{80,144},{96,160},{112,17... | collective-permute-start | bytes 786440 | tf_op jit(solution)/shard_map/ppermute | solution.py:244
  121.6 12.1 %collective-permute-start.14 = (f32[256,256]{1,0:T(8,128)}, f32[256,256]{1,0:T(8,128)S(1)}, u32[]{:S(2)}, u32[]{:S(2)}) collective-permute-start(f32[256,256]{1,0:T(8,128)} %fusion.5), channel_id=1, source_target_pairs={{0,48},{16,0},{32,16},{48,32},{64,112},{80,64},{96,80},{112,96},{1... | collective-permute-start | bytes 786440 | tf_op jit(solution)/shard_map/ppermute | solution.py:237
  124.5 9.1 %collective-permute-start.13 = (f32[256,256]{1,0:T(8,128)S(1)}, f32[256,256]{1,0:T(8,128)S(1)}, u32[]{:S(2)}, u32[]{:S(2)}) collective-permute-start(f32[256,256]{1,0:T(8,128)S(1)} %fusion.6), channel_id=1, source_target_pairs={{0,16},{16,32},{32,48},{48,0},{64,80},{80,96},{96,112},{112,64},{1... | collective-permute-start | bytes 786440 | tf_op jit(solution)/shard_map/ppermute | solution.py:237
  138.8 7.9 %collective-permute-start.19 = (f32[256,256]{1,0:T(8,128)}, f32[256,256]{1,0:T(8,128)S(1)}, u32[]{:S(2)}, u32[]{:S(2)}) collective-permute-start(f32[256,256]{1,0:T(8,128)} %get-tuple-element.61), channel_id=1, source_target_pairs={{0,64},{16,80},{32,96},{48,112},{64,128},{80,144},{96,160},{112,17... | collective-permute-start | bytes 786440 | tf_op jit(solution)/shard_map/ppermute | solution.py:244
  139.7 10.6 %collective-permute-start.20 = (f32[256,256]{1,0:T(8,128)}, f32[256,256]{1,0:T(8,128)S(1)}, u32[]{:S(2)}, u32[]{:S(2)}) collective-permute-start(f32[256,256]{1,0:T(8,128)} %get-tuple-element.62), channel_id=1, source_target_pairs={{0,128},{16,144},{32,160},{48,176},{64,192},{80,208},{96,224},{112... | collective-permute-start | bytes 786440 | tf_op jit(solution)/shard_map/ppermute | solution.py:244
  143.0 7.4 %collective-permute-start.21 = (f32[256,256]{1,0:T(8,128)}, f32[256,256]{1,0:T(8,128)S(1)}, u32[]{:S(2)}, u32[]{:S(2)}) collective-permute-start(f32[256,256]{1,0:T(8,128)} %get-tuple-element.63), channel_id=1, source_target_pairs={{0,192},{16,208},{32,224},{48,240},{64,0},{80,16},{96,32},{112,48}... | collective-permute-start | bytes 786440 | tf_op jit(solution)/shard_map/ppermute | solution.py:244
  143.0 7.8 %collective-permute-start.22 = (f32[256,256]{1,0:T(8,128)}, f32[256,256]{1,0:T(8,128)S(1)}, u32[]{:S(2)}, u32[]{:S(2)}) collective-permute-start(f32[256,256]{1,0:T(8,128)} %get-tuple-element.65), channel_id=1, source_target_pairs={{0,16},{16,32},{32,48},{48,0},{64,80},{80,96},{96,112},{112,64},{1... | collective-permute-start | bytes 786440 | tf_op jit(solution)/shard_map/ppermute | solution.py:237
  143.0 10.9 %collective-permute-start.23 = (f32[256,256]{1,0:T(8,128)}, f32[256,256]{1,0:T(8,128)S(1)}, u32[]{:S(2)}, u32[]{:S(2)}) collective-permute-start(f32[256,256]{1,0:T(8,128)} %get-tuple-element.66), channel_id=1, source_target_pairs={{0,32},{16,48},{32,0},{48,16},{64,96},{80,112},{96,64},{112,80},{1... | collective-permute-start | bytes 786440 | tf_op jit(solution)/shard_map/ppermute | solution.py:237
  146.7 7.8 %collective-permute-start.24 = (f32[256,256]{1,0:T(8,128)}, f32[256,256]{1,0:T(8,128)S(1)}, u32[]{:S(2)}, u32[]{:S(2)}) collective-permute-start(f32[256,256]{1,0:T(8,128)} %get-tuple-element.67), channel_id=1, source_target_pairs={{0,48},{16,0},{32,16},{48,32},{64,112},{80,64},{96,80},{112,96},{1... | collective-permute-start | bytes 786440 | tf_op jit(solution)/shard_map/ppermute | solution.py:237
  157.9 25.5 %collective-permute-start.25 = (f32[2,256,256]{2,1,0:T(8,128)}, f32[2,256,256]{2,1,0:T(8,128)S(1)}, u32[]{:S(2)}, u32[]{:S(2)}) collective-permute-start(f32[2,256,256]{2,1,0:T(8,128)} %get-tuple-element.68), channel_id=1, source_target_pairs={{112,32},{0,2},{32,18},{80,48},{208,46},{160,226},{128,242},{240,6... | collective-permute-start | bytes 1572872 | tf_op jit(solution)/shard_map/ppermute | solution.py:347
  163.0 20.5 %collective-permute-start.26 = (f32[2,256,256]{2,1,0:T(8,128)}, f32[2,256,256]{2,1,0:T(8,128)S(1)}, u32[]{:S(2)}, u32[]{:S(2)}) collective-permute-start(f32[2,256,256]{2,1,0:T(8,128)} %get-tuple-element.69), channel_id=1, source_target_pairs={{112,2},{0,48},{32,32},{80,18},{208,226},{160,62},{128,46},{240,24... | collective-permute-start | bytes 1572872 | tf_op jit(solution)/shard_map/ppermute | solution.py:346
  207.4 12.1 %all-to-all-start.2 = ((f32[16,16,128]{2,1,0:T(8,128)}), f32[16,16,128]{2,1,0:T(8,128)S(1)}, u32[]{:S(2)}, u32[]{:S(2)}) async-start(f32[16,16,128]{2,1,0:T(8,128)} %broadcast_in_dim.24), calls=%async_computation.2 | async-start | bytes 262144 | tf_op jit(solution)/shard_map/all_to_all | solution.py:272
  (30 other events, 178.0 us)

commit v8 on v6

--- a/solution.py
+++ b/solution.py
@@ -370,7 +370,6 @@
 
 
 def body(samples, sky_model, initial_gains):
-    row_count = lax.axis_size("row")
     column_count = lax.axis_size("col")
     row_index = lax.axis_index("row")
     column_index = lax.axis_index("col")
@@ -398,14 +397,15 @@
     gain = sums[:2] / sums[2:]
 
     parts = rows_to_columns(weight_real, weight_imag, power, gain)
-    message = jnp.concatenate([parts.reshape(-1), gain.reshape(-1)])
-    message = message.reshape(-1, 128)
-    received = exchange(message, "row").reshape(row_count, -1)
-    sums = jnp.sum(received[:, : 3 * block_column], axis=0).reshape(3, block_column)
-    previous = lax.dynamic_slice_in_dim(
-        received[:, 3 * block_column :], column_index * blocks, blocks, 0
-    )
-    previous = previous.reshape(blocks, 2, block_row).transpose(1, 0, 2).reshape(2, block_column)
+    lanes = 128
+    message = jnp.concatenate([parts.reshape(-1, lanes), gain.reshape(-1, lanes)])
+    received = exchange(message, "row")
+    count = parts.size // lanes
+    sums = jnp.sum(received, axis=0)[:count].reshape(3, block_column)
+    previous = lax.dynamic_slice(
+        received, (column_index * blocks, count, 0), (blocks, gain.size // lanes, lanes)
+    )
+    previous = previous.reshape(blocks, 2, -1, lanes).transpose(1, 0, 2, 3).reshape(2, block_column)
     gain = 0.5 * (sums[:2] / sums[2:] + previous)
 
     parts = columns_to_rows(weight_real, weight_imag, power, gain)

time: 213 us -> 211 us (level)
    unnamed x79 -> x75, local copies, waits for them, and re-layouts: 5.7 us -> 5.06 us
where the time goes in v8:
time: 211 us; the launch traced here: 209 us
  waiting for transfers between devices  81.8 us (39%)
  starting transfers between devices  62.8 us (30%)
  Pallas kernels  27.6 us (13%)
  blocking collectives  22.1 us (10%)
  local copies, waits for them, and re-layouts  8.22 us (4%)
  other arithmetic  4.74 us (2%)
    pallas_call x4, Pallas kernels, kernel_call(): pl.pallas_call(kernel, out_shape=shapes, in_specs=[smem] * len(scalars) +...  19.6 us
    ppermute x1, waiting for transfers between devices, starting_gains(): share = lax.ppermute(initial_gains, ('row', 'col'), pairs)  19.5 us
    ppermute x11, waiting for transfers between devices, shift_y(): return lax.ppermute(value, 'row', pairs)  19.3 us
    all_to_all x2, starting transfers between devices, exchange(): return lax.all_to_all(copies, axis, 0, 0)  16.6 us
    ppermute x1, waiting for transfers between devices, vis_tiles(): two = lax.ppermute(two, ('row', 'col'), second)  15.5 us
    all_to_all x2, waiting for transfers between devices, exchange(): return lax.all_to_all(copies, axis, 0, 0)  15.4 us
    ppermute x11, starting transfers between devices, shift_y(): return lax.ppermute(value, 'row', pairs)  13.7 us
    all_to_all x1, blocking collectives, exchange(): return lax.all_to_all(copies, axis, 0, 0)  11.8 us
  transfers between devices with their start and end apart: 31, of which 14 were waited for; matrix products, arithmetic and copies ran while one was open for 2% of the time, Pallas kernels for 10%

profile of v8, /device:TPU:64, one launch (start us, length us, event | category | flops | bytes accessed | tf_op | source)
XLA Modules:
  0.0 208.5 jit_solution(11286814515788830292)
XLA Ops:
  1.7 1.9 collective-permute-start.2
  3.6 7.8 %collective-permute-start = (f32[2,32]{1,0:T(2,128)S(1)}, f32[2,32]{1,0:T(2,128)S(1)}, u32[]{:S(2)}, u32[]{:S(2)}) collective-permute-start(f32[2,32]{1,0:T(2,128)S(1)} %copy-done.35), channel_id=1, source_target_pairs={{0,0},{2,16},{4,32},{6,48},{8,64},{10,80},{12,96},{14,112},{16,128... | collective-permute-start | bytes 776 | tf_op jit(solution)/shard_map/ppermute | solution.py:368
  11.5 19.5 %collective-permute-done = f32[2,32]{1,0:T(2,128)S(1)} collective-permute-done((f32[2,32]{1,0:T(2,128)S(1)}, f32[2,32]{1,0:T(2,128)S(1)}, u32[]{:S(2)}, u32[]{:S(2)}) %collective-permute-start) | collective-permute-done | bytes 288 | tf_op jit(solution)/shard_map/ppermute | solution.py:368
  31.6 9.5 %all-to-all-start = ((f32[16,2,32]{2,1,0:T(2,128)}), f32[16,2,32]{2,1,0:T(2,128)S(1)}, u32[]{:S(2)}, u32[]{:S(2)}) async-start(f32[16,2,32]{2,1,0:T(2,128)} %broadcast_in_dim.8), calls=%async_computation | async-start | bytes 32768 | tf_op jit(solution)/shard_map/all_to_all | solution.py:275
  41.1 7.4 %all-to-all-done = f32[16,2,32]{2,1,0:T(2,128)S(1)} async-done(((f32[16,2,32]{2,1,0:T(2,128)}), f32[16,2,32]{2,1,0:T(2,128)S(1)}, u32[]{:S(2)}, u32[]{:S(2)}) %all-to-all-start) | async-done | bytes 4128 | tf_op jit(solution)/shard_map/all_to_all | solution.py:275
  48.7 2.0 collective-permute-start.12
  51.4 6.0 %shard_map.82 = (f32[2,256,256]{2,1,0:T(8,128)}, f32[2,256,256]{2,1,0:T(8,128)}, f32[256,256]{1,0:T(8,128)}, f32[256,256]{1,0:T(8,128)}, f32[2,256,256]{2,1,0:T(...) custom-call(s32[2]{0:T(128)} %pad_add_fusion.device, ...), custom_call_target="tpu_custom_call" | custom-call | flops 2147483648 | bytes 7340032 | tf_op jit(solution)/shard_map/pallas_call | solution.py:227
  59.4 4.4 %shard_map.84.diagonal = f32[4,256,256]{2,1,0:T(8,128)} custom-call(bf16[512,1024]{1,0:T(8,128)(2,1)} %bitcast.84), custom_call_target="tpu_custom_call" | custom-call | flops 805306368 | bytes 2097152 | tf_op jit(solution)/shard_map/pallas_call | solution.py:227
  65.1 2.8 %collective-permute-done.8.refs_7_ = f32[2,256,256]{2,1,0:T(8,128)S(1)} collective-permute-done((f32[2,256,256]{2,1,0:T(8,128)}, f32[2,256,256]{2,1,0:T(8,128)S(1)}, u32[]{:S(2)}, u32[]{:S(2)}) %collective-permute-start.8) | collective-permute-done | bytes 524320 | tf_op jit(solution)/shard_map/ppermute | solution.py:248
  69.2 2.0 collective-permute-done.11.two
  72.2 6.4 %shard_map.85 = (f32[2,256,256]{2,1,0:T(8,128)}, f32[2,256,256]{2,1,0:T(8,128)}, f32[256,256]{1,0:T(8,128)}, f32[256,256]{1,0:T(8,128)}, f32[2,256,256]{2,1,0:T(...) custom-call(s32[2]{0:T(128)} %pad_add_fusion.device, ...), custom_call_target="tpu_custom_call" | custom-call | flops 2147483648 | bytes 8388608 | tf_op jit(solution)/shard_map/pallas_call | solution.py:227
  82.3 1.5 collective-permute-start.14
  83.8 5.2 %collective-permute-done.18.refs_9_ = f32[2,256,256]{2,1,0:T(8,128)S(1)} collective-permute-done((f32[2,256,256]{2,1,0:T(8,128)}, f32[2,256,256]{2,1,0:T(8,128)S(1)}, u32[]{:S(2)}, u32[]{:S(2)}) %collective-permute-start.18) | collective-permute-done | bytes 524320 | tf_op jit(solution)/shard_map/ppermute | solution.py:248
  89.7 6.3 %collective-permute-done.17.refs_8_ = f32[2,256,256]{2,1,0:T(8,128)S(1)} collective-permute-done((f32[2,256,256]{2,1,0:T(8,128)S(1)}, f32[2,256,256]{2,1,0:T(8,128)S(1)}, u32[]{:S(2)}, u32[]{:S(2)}) %collective-permute-start.17) | collective-permute-done | bytes 524320 | tf_op jit(solution)/shard_map/ppermute | solution.py:248
  98.9 3.6 %collective-permute-done.13.refs_2_ = f32[2,256,256]{2,1,0:T(8,128)S(1)} collective-permute-done((f32[2,256,256]{2,1,0:T(8,128)S(1)}, f32[2,256,256]{2,1,0:T(8,128)S(1)}, u32[]{:S(2)}, u32[]{:S(2)}) %collective-permute-start.13) | collective-permute-done | bytes 524320 | tf_op jit(solution)/shard_map/ppermute | solution.py:241
  102.5 2.2 %collective-permute-start.20 = (f32[256,256]{1,0:T(8,128)S(1)}, f32[256,256]{1,0:T(8,128)S(1)}, u32[]{:S(2)}, u32[]{:S(2)}) collective-permute-start(f32[256,256]{1,0:T(8,128)S(1)} %fusion.3), channel_id=1, source_target_pairs={{0,192},{16,208},{32,224},{48,240},{64,0},{80,16},{96,32},{112,48}... | collective-permute-start | bytes 786440 | tf_op jit(solution)/shard_map/ppermute | solution.py:248
  105.1 3.1 %collective-permute-start.16 = (f32[256,256]{1,0:T(8,128)S(1)}, f32[256,256]{1,0:T(8,128)S(1)}, u32[]{:S(2)}, u32[]{:S(2)}) collective-permute-start(f32[256,256]{1,0:T(8,128)S(1)} %fusion.5), channel_id=1, source_target_pairs={{0,48},{16,0},{32,16},{48,32},{64,112},{80,64},{96,80},{112,96},{1... | collective-permute-start | bytes 786440 | tf_op jit(solution)/shard_map/ppermute | solution.py:241
  109.7 3.8 %shard_map.83 = (f32[2,256,256]{2,1,0:T(8,128)}, f32[2,256,256]{2,1,0:T(8,128)}) custom-call(f32[2,256,256]{2,1,0:T(8,128)} %get-tuple-element.42.refs_0_, f32[2,256,256]{2,1,0:T(8,128)} %copy-done.8, f32[2,256,256]{2,1,0:T(8,128)} %copy-done.7, f32[256,256]{1,0:T(8,128)} %copy-done.26, f32[256,256]{1,0:T(8,128)} %copy-done.20, ...), custom_call_target="tpu_custom_call" | custom-call | flops 524288 | bytes 4718592 | tf_op jit(solution)/shard_map/pallas_call | solution.py:197
  113.6 2.3 %collective-permute-done.15.refs_4_ = f32[256,256]{1,0:T(8,128)S(1)} collective-permute-done((f32[256,256]{1,0:T(8,128)S(1)}, f32[256,256]{1,0:T(8,128)S(1)}, u32[]{:S(2)}, u32[]{:S(2)}) %collective-permute-start.15) | collective-permute-done | bytes 262176 | tf_op jit(solution)/shard_map/ppermute | solution.py:241
  116.6 4.2 %shard_map.86 = (f32[256,256]{1,0:T(8,128)}, f32[256,256]{1,0:T(8,128)}, f32[256,256]{1,0:T(8,128)}, f32[256,256]{1,0:T(8,128)}, f32[256,256]{1,0:T(8,128)}, /*i...) custom-call(s32[2]{0:T(128)} %pad_add_fusion.device, s32[1024]{0:T(1024)} %constant.49.clone.ahead, ...), custom_call_target="tpu_custom_call" | custom-call | flops 524288 | bytes 4718592 | tf_op jit(solution)/shard_map/pallas_call | solution.py:197
  120.9 4.6 %collective-permute-start.22 = (f32[256,256]{1,0:T(8,128)}, f32[256,256]{1,0:T(8,128)S(1)}, u32[]{:S(2)}, u32[]{:S(2)}) collective-permute-start(f32[256,256]{1,0:T(8,128)} %get-tuple-element.66), channel_id=1, source_target_pairs={{0,128},{16,144},{32,160},{48,176},{64,192},{80,208},{96,224},{112... | collective-permute-start | bytes 786440 | tf_op jit(solution)/shard_map/ppermute | solution.py:248
  125.5 1.9 collective-permute-start.25
  129.2 3.7 %collective-permute-done.22.refs_2_ = f32[256,256]{1,0:T(8,128)S(1)} collective-permute-done((f32[256,256]{1,0:T(8,128)}, f32[256,256]{1,0:T(8,128)S(1)}, u32[]{:S(2)}, u32[]{:S(2)}) %collective-permute-start.22) | collective-permute-done | bytes 262176 | tf_op jit(solution)/shard_map/ppermute | solution.py:248
  132.9 3.2 %collective-permute-done.24.refs_5_ = f32[256,256]{1,0:T(8,128)S(1)} collective-permute-done((f32[256,256]{1,0:T(8,128)}, f32[256,256]{1,0:T(8,128)S(1)}, u32[]{:S(2)}, u32[]{:S(2)}) %collective-permute-start.24) | collective-permute-done | bytes 262176 | tf_op jit(solution)/shard_map/ppermute | solution.py:241
  137.7 2.8 %shard_map.87 = (f32[2,256,256]{2,1,0:T(8,128)}, f32[2,256,256]{2,1,0:T(8,128)}) custom-call(s32[2]{0:T(128)} %pad_add_fusion.device, s32[256]{0:T(256)} %constant.50.clone.flags, f32[256,256]{1,0:T(8,128)} %get-tuple-element.64.refs_0_, f32[256,256]{1,0:T(8,128)} %copy-done.22, f32[256,256]{1,0:T(8,128)} %copy-done.24, f32[256,256]{1,0:T(8,128)} %copy-done.27, ...), custom_call_target="tpu_custom_call" | custom-call | bytes 3145728 | tf_op jit(solution)/shard_map/pallas_call | solution.py:227
  140.5 2.7 %collective-permute-start.27 = (f32[2,256,256]{2,1,0:T(8,128)}, f32[2,256,256]{2,1,0:T(8,128)S(1)}, u32[]{:S(2)}, u32[]{:S(2)}) collective-permute-start(f32[2,256,256]{2,1,0:T(8,128)} %get-tuple-element.72), channel_id=1, source_target_pairs={{112,32},{0,2},{32,18},{80,48},{208,46},{160,226},{128,242},{240,6... | collective-permute-start | bytes 1572872 | tf_op jit(solution)/shard_map/ppermute | solution.py:352
  143.2 6.2 %collective-permute-start.28 = (f32[2,256,256]{2,1,0:T(8,128)}, f32[2,256,256]{2,1,0:T(8,128)S(1)}, u32[]{:S(2)}, u32[]{:S(2)}) collective-permute-start(f32[2,256,256]{2,1,0:T(8,128)} %get-tuple-element.73), channel_id=1, source_target_pairs={{112,2},{0,48},{32,32},{80,18},{208,226},{160,62},{128,46},{240,24... | collective-permute-start | bytes 1572872 | tf_op jit(solution)/shard_map/ppermute | solution.py:351
  152.1 15.5 %collective-permute-done.27 = f32[2,256,256]{2,1,0:T(8,128)S(1)} collective-permute-done((f32[2,256,256]{2,1,0:T(8,128)}, f32[2,256,256]{2,1,0:T(8,128)S(1)}, u32[]{:S(2)}, u32[]{:S(2)}) %collective-permute-start.27) | collective-permute-done | bytes 524320 | tf_op jit(solution)/shard_map/ppermute | solution.py:352
  168.6 11.8 %all_to_all.20 = f32[8,6,128]{2,1,0:T(8,128)S(1)} all-to-all(f32[8,6,128]{2,1,0:T(8,128)S(1)} %broadcast_in_dim.10), channel_id=1, replica_groups=mesh['row'=16,'col'=8,'chan'=2] {'col'}, dimensions={0} | all-to-all | bytes 49152 | tf_op jit(solution)/shard_map/all_to_all | solution.py:275
  181.6 7.1 %all-to-all-start.2 = ((f32[16,16,128]{2,1,0:T(8,128)}), f32[16,16,128]{2,1,0:T(8,128)S(1)}, u32[]{:S(2)}, u32[]{:S(2)}) async-start(f32[16,16,128]{2,1,0:T(8,128)} %broadcast_in_dim.22), calls=%async_computation.2 | async-start | bytes 262144 | tf_op jit(solution)/shard_map/all_to_all | solution.py:275
  188.7 8.0 %all-to-all-done.2 = f32[16,16,128]{2,1,0:T(8,128)S(1)} async-done(((f32[16,16,128]{2,1,0:T(8,128)}), f32[16,16,128]{2,1,0:T(8,128)S(1)}, u32[]{:S(2)}, u32[]{:S(2)}) %all-to-all-start.2) | async-done | bytes 131104 | tf_op jit(solution)/shard_map/all_to_all | solution.py:275
  197.6 10.3 %all_to_all.21 = f32[8,3,32]{2,1,0:T(4,128)S(1)} all-to-all(f32[8,3,32]{2,1,0:T(4,128)S(1)} %maximum_bitcast_fusion), channel_id=1, replica_groups=mesh['row'=16,'col'=8,'chan'=2] {'col'}, dimensions={0} | all-to-all | bytes 6144 | tf_op jit(solution)/shard_map/all_to_all | solution.py:413
  (169 shorter events, 27.5 us)
Async XLA Ops:
  1.5 49.9 %copy-start.9 = (bf16[64,8,2,512]{3,1,2,0:T(8,128)(2,1)}, bf16[64,8,2,512]{3,1,2,0:T(8,128)(2,1)S(1)}, u32[]{:S(2)}) copy-start(bf16[64,8,2,512]{3,1,2,0:T(8,128)(2,1)S(1)} %copy.34) | copy-start | bytes 3145732
  1.5 47.1 %collective-permute-start.1 = (bf16[512,1024]{1,0:T(8,128)(2,1)S(1)}, bf16[512,1024]{1,0:T(8,128)(2,1)}, u32[]{:S(2)}, u32[]{:S(2)}) collective-permute-start(bf16[512,1024]{1,0:T(8,128)(2,1)S(1)} %bitcast.81), channel_id=1, source_target_pairs={{0,14},{2,0},{4,2},{6,4},{8,6},{10,8},{12,10},{14,12},{1,15},{3,1}... | collective-permute-start | bytes 3145736 | tf_op jit(solution)/shard_map/ppermute | solution.py:252
  1.7 47.0 %collective-permute-start.2 = (bf16[512,1024]{1,0:T(8,128)(2,1)S(1)}, bf16[512,1024]{1,0:T(8,128)(2,1)}, u32[]{:S(2)}, u32[]{:S(2)}) collective-permute-start(bf16[512,1024]{1,0:T(8,128)(2,1)S(1)} %bitcast.82), channel_id=1, source_target_pairs={{0,2},{2,4},{4,6},{6,8},{8,10},{10,12},{12,14},{14,0},{1,3},{3,5},... | collective-permute-start | bytes 3145736 | tf_op jit(solution)/shard_map/ppermute | solution.py:252
  3.6 27.4 %collective-permute-start = (f32[2,32]{1,0:T(2,128)S(1)}, f32[2,32]{1,0:T(2,128)S(1)}, u32[]{:S(2)}, u32[]{:S(2)}) collective-permute-start(f32[2,32]{1,0:T(2,128)S(1)} %copy-done.35), channel_id=1, source_target_pairs={{0,0},{2,16},{4,32},{6,48},{8,64},{10,80},{12,96},{14,112},{16,128... | collective-permute-start | bytes 776 | tf_op jit(solution)/shard_map/ppermute | solution.py:368
  31.6 16.9 %all-to-all-start = ((f32[16,2,32]{2,1,0:T(2,128)}), f32[16,2,32]{2,1,0:T(2,128)S(1)}, u32[]{:S(2)}, u32[]{:S(2)}) async-start(f32[16,2,32]{2,1,0:T(2,128)} %broadcast_in_dim.8), calls=%async_computation | async-start | bytes 32768 | tf_op jit(solution)/shard_map/all_to_all | solution.py:275
  48.6 22.6 %collective-permute-start.11 = (bf16[512,1024]{1,0:T(8,128)(2,1)}, bf16[512,1024]{1,0:T(8,128)(2,1)}, u32[]{:S(2)}, u32[]{:S(2)}) collective-permute-start(bf16[512,1024]{1,0:T(8,128)(2,1)} %collective-permute-done.2.two.one), channel_id=1, source_target_pairs={{0,2},{2,4},{4,6},{6,8},{8,10},{10,12},{12,14},{14,0},{1,3},{3,5},... | collective-permute-start | bytes 3145736 | tf_op jit(solution)/shard_map/ppermute | solution.py:252
  48.7 23.5 %collective-permute-start.12 = (bf16[512,1024]{1,0:T(8,128)(2,1)}, bf16[512,1024]{1,0:T(8,128)(2,1)}, u32[]{:S(2)}, u32[]{:S(2)}) collective-permute-start(bf16[512,1024]{1,0:T(8,128)(2,1)} %collective-permute-done.1.block), channel_id=1, source_target_pairs={{0,14},{2,0},{4,2},{6,4},{8,6},{10,8},{12,10},{14,12},{1,15},{3,1}... | collective-permute-start | bytes 3145736 | tf_op jit(solution)/shard_map/ppermute | solution.py:252
  57.3 10.6 %collective-permute-start.8 = (f32[2,256,256]{2,1,0:T(8,128)}, f32[2,256,256]{2,1,0:T(8,128)S(1)}, u32[]{:S(2)}, u32[]{:S(2)}) collective-permute-start(f32[2,256,256]{2,1,0:T(8,128)} %get-tuple-element.49), channel_id=1, source_target_pairs={{0,192},{16,208},{32,224},{48,240},{64,0},{80,16},{96,32},{112,48}... | collective-permute-start | bytes 1572872 | tf_op jit(solution)/shard_map/ppermute | solution.py:248
  58.7 21.0 %collective-permute-start.7 = (f32[2,256,256]{2,1,0:T(8,128)}, f32[2,256,256]{2,1,0:T(8,128)S(1)}, u32[]{:S(2)}, u32[]{:S(2)}) collective-permute-start(f32[2,256,256]{2,1,0:T(8,128)} %get-tuple-element.48), channel_id=1, source_target_pairs={{0,64},{16,80},{32,96},{48,112},{64,128},{80,144},{96,160},{112,17... | collective-permute-start | bytes 1572872 | tf_op jit(solution)/shard_map/ppermute | solution.py:248
  63.8 17.3 %collective-permute-start.4 = (f32[2,256,256]{2,1,0:T(8,128)}, f32[2,256,256]{2,1,0:T(8,128)S(1)}, u32[]{:S(2)}, u32[]{:S(2)}) collective-permute-start(f32[2,256,256]{2,1,0:T(8,128)} %get-tuple-element.44), channel_id=1, source_target_pairs={{0,48},{16,0},{32,16},{48,32},{64,112},{80,64},{96,80},{112,96},{1... | collective-permute-start | bytes 1572872 | tf_op jit(solution)/shard_map/ppermute | solution.py:241
  67.9 14.3 %collective-permute-start.3 = (f32[2,256,256]{2,1,0:T(8,128)}, f32[2,256,256]{2,1,0:T(8,128)S(1)}, u32[]{:S(2)}, u32[]{:S(2)}) collective-permute-start(f32[2,256,256]{2,1,0:T(8,128)} %get-tuple-element.43), channel_id=1, source_target_pairs={{0,16},{16,32},{32,48},{48,0},{64,80},{80,96},{96,112},{112,64},{1... | collective-permute-start | bytes 1572872 | tf_op jit(solution)/shard_map/ppermute | solution.py:241
  71.2 33.5 %collective-permute-start.10 = (f32[256,256]{1,0:T(8,128)}, f32[256,256]{1,0:T(8,128)S(1)}, u32[]{:S(2)}, u32[]{:S(2)}) collective-permute-start(f32[256,256]{1,0:T(8,128)} %fusion.7), channel_id=1, source_target_pairs={{0,192},{16,208},{32,224},{48,240},{64,0},{80,16},{96,32},{112,48}... | collective-permute-start | bytes 786440 | tf_op jit(solution)/shard_map/ppermute | solution.py:248
  78.6 10.4 %collective-permute-start.18 = (f32[2,256,256]{2,1,0:T(8,128)}, f32[2,256,256]{2,1,0:T(8,128)S(1)}, u32[]{:S(2)}, u32[]{:S(2)}) collective-permute-start(f32[2,256,256]{2,1,0:T(8,128)} %get-tuple-element.61), channel_id=1, source_target_pairs={{0,192},{16,208},{32,224},{48,240},{64,0},{80,16},{96,32},{112,48}... | collective-permute-start | bytes 1572872 | tf_op jit(solution)/shard_map/ppermute | solution.py:248
  79.7 25.4 %collective-permute-start.9 = (f32[256,256]{1,0:T(8,128)S(1)}, f32[256,256]{1,0:T(8,128)S(1)}, u32[]{:S(2)}, u32[]{:S(2)}) collective-permute-start(f32[256,256]{1,0:T(8,128)S(1)} %fusion.8), channel_id=1, source_target_pairs={{0,64},{16,80},{32,96},{48,112},{64,128},{80,144},{96,160},{112,17... | collective-permute-start | bytes 786440 | tf_op jit(solution)/shard_map/ppermute | solution.py:248
  81.1 14.9 %collective-permute-start.17 = (f32[2,256,256]{2,1,0:T(8,128)S(1)}, f32[2,256,256]{2,1,0:T(8,128)S(1)}, u32[]{:S(2)}, u32[]{:S(2)}) collective-permute-start(f32[2,256,256]{2,1,0:T(8,128)S(1)} %copy-done.34), channel_id=1, source_target_pairs={{0,64},{16,80},{32,96},{48,112},{64,128},{80,144},{96,160},{112,17... | collective-permute-start | bytes 1572872 | tf_op jit(solution)/shard_map/ppermute | solution.py:248
  82.3 15.6 %collective-permute-start.14 = (f32[2,256,256]{2,1,0:T(8,128)S(1)}, f32[2,256,256]{2,1,0:T(8,128)S(1)}, u32[]{:S(2)}, u32[]{:S(2)}) collective-permute-start(f32[2,256,256]{2,1,0:T(8,128)S(1)} %copy-done.33), channel_id=1, source_target_pairs={{0,48},{16,0},{32,16},{48,32},{64,112},{80,64},{96,80},{112,96},{1... | collective-permute-start | bytes 1572872 | tf_op jit(solution)/shard_map/ppermute | solution.py:241
  89.0 13.5 %collective-permute-start.13 = (f32[2,256,256]{2,1,0:T(8,128)S(1)}, f32[2,256,256]{2,1,0:T(8,128)S(1)}, u32[]{:S(2)}, u32[]{:S(2)}) collective-permute-start(f32[2,256,256]{2,1,0:T(8,128)S(1)} %copy-done.32), channel_id=1, source_target_pairs={{0,16},{16,32},{32,48},{48,0},{64,80},{80,96},{96,112},{112,64},{1... | collective-permute-start | bytes 1572872 | tf_op jit(solution)/shard_map/ppermute | solution.py:241
  96.0 12.3 %collective-permute-start.6 = (f32[256,256]{1,0:T(8,128)S(1)}, f32[256,256]{1,0:T(8,128)S(1)}, u32[]{:S(2)}, u32[]{:S(2)}) collective-permute-start(f32[256,256]{1,0:T(8,128)S(1)} %fusion.9), channel_id=1, source_target_pairs={{0,48},{16,0},{32,16},{48,32},{64,112},{80,64},{96,80},{112,96},{1... | collective-permute-start | bytes 786440 | tf_op jit(solution)/shard_map/ppermute | solution.py:241
  97.9 10.4 %collective-permute-start.5 = (f32[256,256]{1,0:T(8,128)S(1)}, f32[256,256]{1,0:T(8,128)S(1)}, u32[]{:S(2)}, u32[]{:S(2)}) collective-permute-start(f32[256,256]{1,0:T(8,128)S(1)} %fusion.10), channel_id=1, source_target_pairs={{0,16},{16,32},{32,48},{48,0},{64,80},{80,96},{96,112},{112,64},{1... | collective-permute-start | bytes 786440 | tf_op jit(solution)/shard_map/ppermute | solution.py:241
  102.5 11.0 %collective-permute-start.20 = (f32[256,256]{1,0:T(8,128)S(1)}, f32[256,256]{1,0:T(8,128)S(1)}, u32[]{:S(2)}, u32[]{:S(2)}) collective-permute-start(f32[256,256]{1,0:T(8,128)S(1)} %fusion.3), channel_id=1, source_target_pairs={{0,192},{16,208},{32,224},{48,240},{64,0},{80,16},{96,32},{112,48}... | collective-permute-start | bytes 786440 | tf_op jit(solution)/shard_map/ppermute | solution.py:248
  104.8 8.8 %collective-permute-start.19 = (f32[256,256]{1,0:T(8,128)}, f32[256,256]{1,0:T(8,128)S(1)}, u32[]{:S(2)}, u32[]{:S(2)}) collective-permute-start(f32[256,256]{1,0:T(8,128)} %fusion.4), channel_id=1, source_target_pairs={{0,64},{16,80},{32,96},{48,112},{64,128},{80,144},{96,160},{112,17... | collective-permute-start | bytes 786440 | tf_op jit(solution)/shard_map/ppermute | solution.py:248
  105.1 8.4 %collective-permute-start.16 = (f32[256,256]{1,0:T(8,128)S(1)}, f32[256,256]{1,0:T(8,128)S(1)}, u32[]{:S(2)}, u32[]{:S(2)}) collective-permute-start(f32[256,256]{1,0:T(8,128)S(1)} %fusion.5), channel_id=1, source_target_pairs={{0,48},{16,0},{32,16},{48,32},{64,112},{80,64},{96,80},{112,96},{1... | collective-permute-start | bytes 786440 | tf_op jit(solution)/shard_map/ppermute | solution.py:241
  108.3 7.6 %collective-permute-start.15 = (f32[256,256]{1,0:T(8,128)S(1)}, f32[256,256]{1,0:T(8,128)S(1)}, u32[]{:S(2)}, u32[]{:S(2)}) collective-permute-start(f32[256,256]{1,0:T(8,128)S(1)} %fusion.6), channel_id=1, source_target_pairs={{0,16},{16,32},{32,48},{48,0},{64,80},{80,96},{96,112},{112,64},{1... | collective-permute-start | bytes 786440 | tf_op jit(solution)/shard_map/ppermute | solution.py:241
  120.8 7.9 %collective-permute-start.21 = (f32[256,256]{1,0:T(8,128)}, f32[256,256]{1,0:T(8,128)S(1)}, u32[]{:S(2)}, u32[]{:S(2)}) collective-permute-start(f32[256,256]{1,0:T(8,128)} %get-tuple-element.65), channel_id=1, source_target_pairs={{0,64},{16,80},{32,96},{48,112},{64,128},{80,144},{96,160},{112,17... | collective-permute-start | bytes 786440 | tf_op jit(solution)/shard_map/ppermute | solution.py:248
  120.9 11.9 %collective-permute-start.22 = (f32[256,256]{1,0:T(8,128)}, f32[256,256]{1,0:T(8,128)S(1)}, u32[]{:S(2)}, u32[]{:S(2)}) collective-permute-start(f32[256,256]{1,0:T(8,128)} %get-tuple-element.66), channel_id=1, source_target_pairs={{0,128},{16,144},{32,160},{48,176},{64,192},{80,208},{96,224},{112... | collective-permute-start | bytes 786440 | tf_op jit(solution)/shard_map/ppermute | solution.py:248
  125.5 7.4 %collective-permute-start.23 = (f32[256,256]{1,0:T(8,128)}, f32[256,256]{1,0:T(8,128)S(1)}, u32[]{:S(2)}, u32[]{:S(2)}) collective-permute-start(f32[256,256]{1,0:T(8,128)} %get-tuple-element.67), channel_id=1, source_target_pairs={{0,192},{16,208},{32,224},{48,240},{64,0},{80,16},{96,32},{112,48}... | collective-permute-start | bytes 786440 | tf_op jit(solution)/shard_map/ppermute | solution.py:248
  125.5 10.6 %collective-permute-start.24 = (f32[256,256]{1,0:T(8,128)}, f32[256,256]{1,0:T(8,128)S(1)}, u32[]{:S(2)}, u32[]{:S(2)}) collective-permute-start(f32[256,256]{1,0:T(8,128)} %get-tuple-element.69), channel_id=1, source_target_pairs={{0,16},{16,32},{32,48},{48,0},{64,80},{80,96},{96,112},{112,64},{1... | collective-permute-start | bytes 786440 | tf_op jit(solution)/shard_map/ppermute | solution.py:241
  125.5 10.6 %collective-permute-start.25 = (f32[256,256]{1,0:T(8,128)}, f32[256,256]{1,0:T(8,128)S(1)}, u32[]{:S(2)}, u32[]{:S(2)}) collective-permute-start(f32[256,256]{1,0:T(8,128)} %get-tuple-element.70), channel_id=1, source_target_pairs={{0,32},{16,48},{32,0},{48,16},{64,96},{80,112},{96,64},{112,80},{1... | collective-permute-start | bytes 786440 | tf_op jit(solution)/shard_map/ppermute | solution.py:241
  128.7 8.3 %collective-permute-start.26 = (f32[256,256]{1,0:T(8,128)}, f32[256,256]{1,0:T(8,128)S(1)}, u32[]{:S(2)}, u32[]{:S(2)}) collective-permute-start(f32[256,256]{1,0:T(8,128)} %get-tuple-element.71), channel_id=1, source_target_pairs={{0,48},{16,0},{32,16},{48,32},{64,112},{80,64},{96,80},{112,96},{1... | collective-permute-start | bytes 786440 | tf_op jit(solution)/shard_map/ppermute | solution.py:241
  140.5 27.1 %collective-permute-start.27 = (f32[2,256,256]{2,1,0:T(8,128)}, f32[2,256,256]{2,1,0:T(8,128)S(1)}, u32[]{:S(2)}, u32[]{:S(2)}) collective-permute-start(f32[2,256,256]{2,1,0:T(8,128)} %get-tuple-element.72), channel_id=1, source_target_pairs={{112,32},{0,2},{32,18},{80,48},{208,46},{160,226},{128,242},{240,6... | collective-permute-start | bytes 1572872 | tf_op jit(solution)/shard_map/ppermute | solution.py:352
  143.2 24.4 %collective-permute-start.28 = (f32[2,256,256]{2,1,0:T(8,128)}, f32[2,256,256]{2,1,0:T(8,128)S(1)}, u32[]{:S(2)}, u32[]{:S(2)}) collective-permute-start(f32[2,256,256]{2,1,0:T(8,128)} %get-tuple-element.73), channel_id=1, source_target_pairs={{112,2},{0,48},{32,32},{80,18},{208,226},{160,62},{128,46},{240,24... | collective-permute-start | bytes 1572872 | tf_op jit(solution)/shard_map/ppermute | solution.py:351
  181.6 15.1 %all-to-all-start.2 = ((f32[16,16,128]{2,1,0:T(8,128)}), f32[16,16,128]{2,1,0:T(8,128)S(1)}, u32[]{:S(2)}, u32[]{:S(2)}) async-start(f32[16,16,128]{2,1,0:T(8,128)} %broadcast_in_dim.22), calls=%async_computation.2 | async-start | bytes 262144 | tf_op jit(solution)/shard_map/all_to_all | solution.py:275
  (36 other events, 162.2 us)

commit v9 on v8

--- a/solution.py
+++ b/solution.py
@@ -299,13 +299,12 @@
     )
 
 
-def vis_tiles(samples, gain):
+def vis_tiles(here, gain):
     row_index = lax.axis_index("row")
     column_index = lax.axis_index("col")
     first, second, early, late, ahead, flags, half = tables()
     device_index = row_index * PLANES + column_index
     device = jnp.stack([device_index, column_index]).astype(jnp.int32)
-    here = samples.reshape(samples.shape[0], -1)
     antennas, times = here.shape
     quarter = antennas // 2
     product = 2 * quarter * quarter * times
@@ -377,8 +376,10 @@
     block_row = sky_model.shape[0]
     share_size = initial_gains.shape[1]
     blocks = block_column // block_row
-    gain = starting_gains(initial_gains)
-    vis_real, vis_imag, gain = vis_tiles(samples, gain)
+    flattened = samples.reshape(block_column, -1)
+    flattened, first_gains = lax.optimization_barrier((flattened, initial_gains))
+    gain = starting_gains(first_gains)
+    vis_real, vis_imag, gain = vis_tiles(flattened, gain)
     model_real = sky_model[:, 0, :].astype(jnp.float32)
     model_imag = sky_model[:, 1, :].astype(jnp.float32)
     global_rows = row_index * block_row + lax.broadcasted_iota(

time: 211 us -> 211 us (level)
  no operation moved by 1% of the time
where the time goes in v9:
time: 211 us; the launch traced here: 209 us
  waiting for transfers between devices  81.8 us (39%)
  starting transfers between devices  62.8 us (30%)
  Pallas kernels  27.6 us (13%)
  blocking collectives  22.1 us (10%)
  local copies, waits for them, and re-layouts  8.22 us (4%)
  other arithmetic  4.74 us (2%)
    pallas_call x4, Pallas kernels, kernel_call(): pl.pallas_call(kernel, out_shape=shapes, in_specs=[smem] * len(scalars) +...  19.6 us
    ppermute x1, waiting for transfers between devices, starting_gains(): share = lax.ppermute(initial_gains, ('row', 'col'), pairs)  19.5 us
    ppermute x11, waiting for transfers between devices, shift_y(): return lax.ppermute(value, 'row', pairs)  19.3 us
    all_to_all x2, starting transfers between devices, exchange(): return lax.all_to_all(copies, axis, 0, 0)  16.6 us
    ppermute x1, waiting for transfers between devices, vis_tiles(): two = lax.ppermute(two, ('row', 'col'), second)  15.5 us
    all_to_all x2, waiting for transfers between devices, exchange(): return lax.all_to_all(copies, axis, 0, 0)  15.4 us
    ppermute x11, starting transfers between devices, shift_y(): return lax.ppermute(value, 'row', pairs)  13.7 us
    all_to_all x1, blocking collectives, exchange(): return lax.all_to_all(copies, axis, 0, 0)  11.8 us
  transfers between devices with their start and end apart: 31, of which 14 were waited for; matrix products, arithmetic and copies ran while one was open for 2% of the time, Pallas kernels for 10%

profile of v9, /device:TPU:64, one launch (start us, length us, event | category | flops | bytes accessed | tf_op | source)
XLA Modules:
  0.0 208.5 jit_solution(11286814515788830292)
XLA Ops:
  1.7 1.9 collective-permute-start.2
  3.6 7.8 %collective-permute-start = (f32[2,32]{1,0:T(2,128)S(1)}, f32[2,32]{1,0:T(2,128)S(1)}, u32[]{:S(2)}, u32[]{:S(2)}) collective-permute-start(f32[2,32]{1,0:T(2,128)S(1)} %copy-done.35), channel_id=1, source_target_pairs={{0,0},{2,16},{4,32},{6,48},{8,64},{10,80},{12,96},{14,112},{16,128... | collective-permute-start | bytes 776 | tf_op jit(solution)/shard_map/ppermute | solution.py:367
  11.5 19.5 %collective-permute-done = f32[2,32]{1,0:T(2,128)S(1)} collective-permute-done((f32[2,32]{1,0:T(2,128)S(1)}, f32[2,32]{1,0:T(2,128)S(1)}, u32[]{:S(2)}, u32[]{:S(2)}) %collective-permute-start) | collective-permute-done | bytes 288 | tf_op jit(solution)/shard_map/ppermute | solution.py:367
  31.6 9.5 %all-to-all-start = ((f32[16,2,32]{2,1,0:T(2,128)}), f32[16,2,32]{2,1,0:T(2,128)S(1)}, u32[]{:S(2)}, u32[]{:S(2)}) async-start(f32[16,2,32]{2,1,0:T(2,128)} %broadcast_in_dim.8), calls=%async_computation | async-start | bytes 32768 | tf_op jit(solution)/shard_map/all_to_all | solution.py:275
  41.1 7.4 %all-to-all-done = f32[16,2,32]{2,1,0:T(2,128)S(1)} async-done(((f32[16,2,32]{2,1,0:T(2,128)}), f32[16,2,32]{2,1,0:T(2,128)S(1)}, u32[]{:S(2)}, u32[]{:S(2)}) %all-to-all-start) | async-done | bytes 4128 | tf_op jit(solution)/shard_map/all_to_all | solution.py:275
  48.7 2.0 collective-permute-start.12
  51.4 6.0 %shard_map.82 = (f32[2,256,256]{2,1,0:T(8,128)}, f32[2,256,256]{2,1,0:T(8,128)}, f32[256,256]{1,0:T(8,128)}, f32[256,256]{1,0:T(8,128)}, f32[2,256,256]{2,1,0:T(...) custom-call(s32[2]{0:T(128)} %pad_add_fusion.device, ...), custom_call_target="tpu_custom_call" | custom-call | flops 2147483648 | bytes 7340032 | tf_op jit(solution)/shard_map/pallas_call | solution.py:227
  59.4 4.4 %shard_map.84.diagonal = f32[4,256,256]{2,1,0:T(8,128)} custom-call(bf16[512,1024]{1,0:T(8,128)(2,1)} %bitcast.84), custom_call_target="tpu_custom_call" | custom-call | flops 805306368 | bytes 2097152 | tf_op jit(solution)/shard_map/pallas_call | solution.py:227
  65.1 2.8 %collective-permute-done.8.refs_7_ = f32[2,256,256]{2,1,0:T(8,128)S(1)} collective-permute-done((f32[2,256,256]{2,1,0:T(8,128)}, f32[2,256,256]{2,1,0:T(8,128)S(1)}, u32[]{:S(2)}, u32[]{:S(2)}) %collective-permute-start.8) | collective-permute-done | bytes 524320 | tf_op jit(solution)/shard_map/ppermute | solution.py:248
  69.2 2.0 collective-permute-done.11.two
  72.2 6.4 %shard_map.85 = (f32[2,256,256]{2,1,0:T(8,128)}, f32[2,256,256]{2,1,0:T(8,128)}, f32[256,256]{1,0:T(8,128)}, f32[256,256]{1,0:T(8,128)}, f32[2,256,256]{2,1,0:T(...) custom-call(s32[2]{0:T(128)} %pad_add_fusion.device, ...), custom_call_target="tpu_custom_call" | custom-call | flops 2147483648 | bytes 8388608 | tf_op jit(solution)/shard_map/pallas_call | solution.py:227
  82.3 1.5 collective-permute-start.14
  83.8 5.2 %collective-permute-done.18.refs_9_ = f32[2,256,256]{2,1,0:T(8,128)S(1)} collective-permute-done((f32[2,256,256]{2,1,0:T(8,128)}, f32[2,256,256]{2,1,0:T(8,128)S(1)}, u32[]{:S(2)}, u32[]{:S(2)}) %collective-permute-start.18) | collective-permute-done | bytes 524320 | tf_op jit(solution)/shard_map/ppermute | solution.py:248
  89.7 6.3 %collective-permute-done.17.refs_8_ = f32[2,256,256]{2,1,0:T(8,128)S(1)} collective-permute-done((f32[2,256,256]{2,1,0:T(8,128)S(1)}, f32[2,256,256]{2,1,0:T(8,128)S(1)}, u32[]{:S(2)}, u32[]{:S(2)}) %collective-permute-start.17) | collective-permute-done | bytes 524320 | tf_op jit(solution)/shard_map/ppermute | solution.py:248
  98.9 3.6 %collective-permute-done.13.refs_2_ = f32[2,256,256]{2,1,0:T(8,128)S(1)} collective-permute-done((f32[2,256,256]{2,1,0:T(8,128)S(1)}, f32[2,256,256]{2,1,0:T(8,128)S(1)}, u32[]{:S(2)}, u32[]{:S(2)}) %collective-permute-start.13) | collective-permute-done | bytes 524320 | tf_op jit(solution)/shard_map/ppermute | solution.py:241
  102.5 2.2 %collective-permute-start.20 = (f32[256,256]{1,0:T(8,128)S(1)}, f32[256,256]{1,0:T(8,128)S(1)}, u32[]{:S(2)}, u32[]{:S(2)}) collective-permute-start(f32[256,256]{1,0:T(8,128)S(1)} %fusion.3), channel_id=1, source_target_pairs={{0,192},{16,208},{32,224},{48,240},{64,0},{80,16},{96,32},{112,48}... | collective-permute-start | bytes 786440 | tf_op jit(solution)/shard_map/ppermute | solution.py:248
  105.1 3.1 %collective-permute-start.16 = (f32[256,256]{1,0:T(8,128)S(1)}, f32[256,256]{1,0:T(8,128)S(1)}, u32[]{:S(2)}, u32[]{:S(2)}) collective-permute-start(f32[256,256]{1,0:T(8,128)S(1)} %fusion.5), channel_id=1, source_target_pairs={{0,48},{16,0},{32,16},{48,32},{64,112},{80,64},{96,80},{112,96},{1... | collective-permute-start | bytes 786440 | tf_op jit(solution)/shard_map/ppermute | solution.py:241
  109.7 3.8 %shard_map.83 = (f32[2,256,256]{2,1,0:T(8,128)}, f32[2,256,256]{2,1,0:T(8,128)}) custom-call(f32[2,256,256]{2,1,0:T(8,128)} %get-tuple-element.46.refs_0_, f32[2,256,256]{2,1,0:T(8,128)} %copy-done.8, f32[2,256,256]{2,1,0:T(8,128)} %copy-done.7, f32[256,256]{1,0:T(8,128)} %copy-done.26, f32[256,256]{1,0:T(8,128)} %copy-done.20, ...), custom_call_target="tpu_custom_call" | custom-call | flops 524288 | bytes 4718592 | tf_op jit(solution)/shard_map/pallas_call | solution.py:197
  113.6 2.3 %collective-permute-done.15.refs_4_ = f32[256,256]{1,0:T(8,128)S(1)} collective-permute-done((f32[256,256]{1,0:T(8,128)S(1)}, f32[256,256]{1,0:T(8,128)S(1)}, u32[]{:S(2)}, u32[]{:S(2)}) %collective-permute-start.15) | collective-permute-done | bytes 262176 | tf_op jit(solution)/shard_map/ppermute | solution.py:241
  116.6 4.2 %shard_map.86 = (f32[256,256]{1,0:T(8,128)}, f32[256,256]{1,0:T(8,128)}, f32[256,256]{1,0:T(8,128)}, f32[256,256]{1,0:T(8,128)}, f32[256,256]{1,0:T(8,128)}, /*i...) custom-call(s32[2]{0:T(128)} %pad_add_fusion.device, s32[1024]{0:T(1024)} %constant.49.clone.ahead, ...), custom_call_target="tpu_custom_call" | custom-call | flops 524288 | bytes 4718592 | tf_op jit(solution)/shard_map/pallas_call | solution.py:197
  120.9 4.6 %collective-permute-start.22 = (f32[256,256]{1,0:T(8,128)}, f32[256,256]{1,0:T(8,128)S(1)}, u32[]{:S(2)}, u32[]{:S(2)}) collective-permute-start(f32[256,256]{1,0:T(8,128)} %get-tuple-element.70), channel_id=1, source_target_pairs={{0,128},{16,144},{32,160},{48,176},{64,192},{80,208},{96,224},{112... | collective-permute-start | bytes 786440 | tf_op jit(solution)/shard_map/ppermute | solution.py:248
  125.5 1.9 collective-permute-start.25
  129.2 3.7 %collective-permute-done.22.refs_2_ = f32[256,256]{1,0:T(8,128)S(1)} collective-permute-done((f32[256,256]{1,0:T(8,128)}, f32[256,256]{1,0:T(8,128)S(1)}, u32[]{:S(2)}, u32[]{:S(2)}) %collective-permute-start.22) | collective-permute-done | bytes 262176 | tf_op jit(solution)/shard_map/ppermute | solution.py:248
  132.9 3.2 %collective-permute-done.24.refs_5_ = f32[256,256]{1,0:T(8,128)S(1)} collective-permute-done((f32[256,256]{1,0:T(8,128)}, f32[256,256]{1,0:T(8,128)S(1)}, u32[]{:S(2)}, u32[]{:S(2)}) %collective-permute-start.24) | collective-permute-done | bytes 262176 | tf_op jit(solution)/shard_map/ppermute | solution.py:241
  137.7 2.8 %shard_map.87 = (f32[2,256,256]{2,1,0:T(8,128)}, f32[2,256,256]{2,1,0:T(8,128)}) custom-call(s32[2]{0:T(128)} %pad_add_fusion.device, s32[256]{0:T(256)} %constant.50.clone.flags, f32[256,256]{1,0:T(8,128)} %get-tuple-element.68.refs_0_, f32[256,256]{1,0:T(8,128)} %copy-done.22, f32[256,256]{1,0:T(8,128)} %copy-done.24, f32[256,256]{1,0:T(8,128)} %copy-done.27, ...), custom_call_target="tpu_custom_call" | custom-call | bytes 3145728 | tf_op jit(solution)/shard_map/pallas_call | solution.py:227
  140.5 2.7 %collective-permute-start.27 = (f32[2,256,256]{2,1,0:T(8,128)}, f32[2,256,256]{2,1,0:T(8,128)S(1)}, u32[]{:S(2)}, u32[]{:S(2)}) collective-permute-start(f32[2,256,256]{2,1,0:T(8,128)} %get-tuple-element.76), channel_id=1, source_target_pairs={{112,32},{0,2},{32,18},{80,48},{208,46},{160,226},{128,242},{240,6... | collective-permute-start | bytes 1572872 | tf_op jit(solution)/shard_map/ppermute | solution.py:351
  143.2 6.2 %collective-permute-start.28 = (f32[2,256,256]{2,1,0:T(8,128)}, f32[2,256,256]{2,1,0:T(8,128)S(1)}, u32[]{:S(2)}, u32[]{:S(2)}) collective-permute-start(f32[2,256,256]{2,1,0:T(8,128)} %get-tuple-element.77), channel_id=1, source_target_pairs={{112,2},{0,48},{32,32},{80,18},{208,226},{160,62},{128,46},{240,24... | collective-permute-start | bytes 1572872 | tf_op jit(solution)/shard_map/ppermute | solution.py:350
  152.1 15.5 %collective-permute-done.27 = f32[2,256,256]{2,1,0:T(8,128)S(1)} collective-permute-done((f32[2,256,256]{2,1,0:T(8,128)}, f32[2,256,256]{2,1,0:T(8,128)S(1)}, u32[]{:S(2)}, u32[]{:S(2)}) %collective-permute-start.27) | collective-permute-done | bytes 524320 | tf_op jit(solution)/shard_map/ppermute | solution.py:351
  168.6 11.8 %all_to_all.20 = f32[8,6,128]{2,1,0:T(8,128)S(1)} all-to-all(f32[8,6,128]{2,1,0:T(8,128)S(1)} %broadcast_in_dim.10), channel_id=1, replica_groups=mesh['row'=16,'col'=8,'chan'=2] {'col'}, dimensions={0} | all-to-all | bytes 49152 | tf_op jit(solution)/shard_map/all_to_all | solution.py:275
  181.6 7.1 %all-to-all-start.2 = ((f32[16,16,128]{2,1,0:T(8,128)}), f32[16,16,128]{2,1,0:T(8,128)S(1)}, u32[]{:S(2)}, u32[]{:S(2)}) async-start(f32[16,16,128]{2,1,0:T(8,128)} %broadcast_in_dim.22), calls=%async_computation.2 | async-start | bytes 262144 | tf_op jit(solution)/shard_map/all_to_all | solution.py:275
  188.7 8.0 %all-to-all-done.2 = f32[16,16,128]{2,1,0:T(8,128)S(1)} async-done(((f32[16,16,128]{2,1,0:T(8,128)}), f32[16,16,128]{2,1,0:T(8,128)S(1)}, u32[]{:S(2)}, u32[]{:S(2)}) %all-to-all-start.2) | async-done | bytes 131104 | tf_op jit(solution)/shard_map/all_to_all | solution.py:275
  197.6 10.3 %all_to_all.21 = f32[8,3,32]{2,1,0:T(4,128)S(1)} all-to-all(f32[8,3,32]{2,1,0:T(4,128)S(1)} %maximum_bitcast_fusion), channel_id=1, replica_groups=mesh['row'=16,'col'=8,'chan'=2] {'col'}, dimensions={0} | all-to-all | bytes 6144 | tf_op jit(solution)/shard_map/all_to_all | solution.py:414
  (169 shorter events, 27.5 us)
Async XLA Ops:
  1.5 49.9 %copy-start.9 = (bf16[64,8,2,512]{3,1,2,0:T(8,128)(2,1)}, bf16[64,8,2,512]{3,1,2,0:T(8,128)(2,1)S(1)}, u32[]{:S(2)}) copy-start(bf16[64,8,2,512]{3,1,2,0:T(8,128)(2,1)S(1)} %copy.34) | copy-start | bytes 3145732
  1.5 47.1 %collective-permute-start.1 = (bf16[512,1024]{1,0:T(8,128)(2,1)S(1)}, bf16[512,1024]{1,0:T(8,128)(2,1)}, u32[]{:S(2)}, u32[]{:S(2)}) collective-permute-start(bf16[512,1024]{1,0:T(8,128)(2,1)S(1)} %bitcast.81), channel_id=1, source_target_pairs={{0,14},{2,0},{4,2},{6,4},{8,6},{10,8},{12,10},{14,12},{1,15},{3,1}... | collective-permute-start | bytes 3145736 | tf_op jit(solution)/shard_map/ppermute | solution.py:252
  1.7 47.0 %collective-permute-start.2 = (bf16[512,1024]{1,0:T(8,128)(2,1)S(1)}, bf16[512,1024]{1,0:T(8,128)(2,1)}, u32[]{:S(2)}, u32[]{:S(2)}) collective-permute-start(bf16[512,1024]{1,0:T(8,128)(2,1)S(1)} %bitcast.82), channel_id=1, source_target_pairs={{0,2},{2,4},{4,6},{6,8},{8,10},{10,12},{12,14},{14,0},{1,3},{3,5},... | collective-permute-start | bytes 3145736 | tf_op jit(solution)/shard_map/ppermute | solution.py:252
  3.6 27.4 %collective-permute-start = (f32[2,32]{1,0:T(2,128)S(1)}, f32[2,32]{1,0:T(2,128)S(1)}, u32[]{:S(2)}, u32[]{:S(2)}) collective-permute-start(f32[2,32]{1,0:T(2,128)S(1)} %copy-done.35), channel_id=1, source_target_pairs={{0,0},{2,16},{4,32},{6,48},{8,64},{10,80},{12,96},{14,112},{16,128... | collective-permute-start | bytes 776 | tf_op jit(solution)/shard_map/ppermute | solution.py:367
  31.6 16.9 %all-to-all-start = ((f32[16,2,32]{2,1,0:T(2,128)}), f32[16,2,32]{2,1,0:T(2,128)S(1)}, u32[]{:S(2)}, u32[]{:S(2)}) async-start(f32[16,2,32]{2,1,0:T(2,128)} %broadcast_in_dim.8), calls=%async_computation | async-start | bytes 32768 | tf_op jit(solution)/shard_map/all_to_all | solution.py:275
  48.6 22.6 %collective-permute-start.11 = (bf16[512,1024]{1,0:T(8,128)(2,1)}, bf16[512,1024]{1,0:T(8,128)(2,1)}, u32[]{:S(2)}, u32[]{:S(2)}) collective-permute-start(bf16[512,1024]{1,0:T(8,128)(2,1)} %collective-permute-done.2.two.one), channel_id=1, source_target_pairs={{0,2},{2,4},{4,6},{6,8},{8,10},{10,12},{12,14},{14,0},{1,3},{3,5},... | collective-permute-start | bytes 3145736 | tf_op jit(solution)/shard_map/ppermute | solution.py:252
  48.7 23.5 %collective-permute-start.12 = (bf16[512,1024]{1,0:T(8,128)(2,1)}, bf16[512,1024]{1,0:T(8,128)(2,1)}, u32[]{:S(2)}, u32[]{:S(2)}) collective-permute-start(bf16[512,1024]{1,0:T(8,128)(2,1)} %collective-permute-done.1.block), channel_id=1, source_target_pairs={{0,14},{2,0},{4,2},{6,4},{8,6},{10,8},{12,10},{14,12},{1,15},{3,1}... | collective-permute-start | bytes 3145736 | tf_op jit(solution)/shard_map/ppermute | solution.py:252
  57.3 10.6 %collective-permute-start.8 = (f32[2,256,256]{2,1,0:T(8,128)}, f32[2,256,256]{2,1,0:T(8,128)S(1)}, u32[]{:S(2)}, u32[]{:S(2)}) collective-permute-start(f32[2,256,256]{2,1,0:T(8,128)} %get-tuple-element.53), channel_id=1, source_target_pairs={{0,192},{16,208},{32,224},{48,240},{64,0},{80,16},{96,32},{112,48}... | collective-permute-start | bytes 1572872 | tf_op jit(solution)/shard_map/ppermute | solution.py:248
  58.7 21.0 %collective-permute-start.7 = (f32[2,256,256]{2,1,0:T(8,128)}, f32[2,256,256]{2,1,0:T(8,128)S(1)}, u32[]{:S(2)}, u32[]{:S(2)}) collective-permute-start(f32[2,256,256]{2,1,0:T(8,128)} %get-tuple-element.52), channel_id=1, source_target_pairs={{0,64},{16,80},{32,96},{48,112},{64,128},{80,144},{96,160},{112,17... | collective-permute-start | bytes 1572872 | tf_op jit(solution)/shard_map/ppermute | solution.py:248
  63.8 17.3 %collective-permute-start.4 = (f32[2,256,256]{2,1,0:T(8,128)}, f32[2,256,256]{2,1,0:T(8,128)S(1)}, u32[]{:S(2)}, u32[]{:S(2)}) collective-permute-start(f32[2,256,256]{2,1,0:T(8,128)} %get-tuple-element.48), channel_id=1, source_target_pairs={{0,48},{16,0},{32,16},{48,32},{64,112},{80,64},{96,80},{112,96},{1... | collective-permute-start | bytes 1572872 | tf_op jit(solution)/shard_map/ppermute | solution.py:241
  67.9 14.3 %collective-permute-start.3 = (f32[2,256,256]{2,1,0:T(8,128)}, f32[2,256,256]{2,1,0:T(8,128)S(1)}, u32[]{:S(2)}, u32[]{:S(2)}) collective-permute-start(f32[2,256,256]{2,1,0:T(8,128)} %get-tuple-element.47), channel_id=1, source_target_pairs={{0,16},{16,32},{32,48},{48,0},{64,80},{80,96},{96,112},{112,64},{1... | collective-permute-start | bytes 1572872 | tf_op jit(solution)/shard_map/ppermute | solution.py:241
  71.2 33.5 %collective-permute-start.10 = (f32[256,256]{1,0:T(8,128)}, f32[256,256]{1,0:T(8,128)S(1)}, u32[]{:S(2)}, u32[]{:S(2)}) collective-permute-start(f32[256,256]{1,0:T(8,128)} %fusion.7), channel_id=1, source_target_pairs={{0,192},{16,208},{32,224},{48,240},{64,0},{80,16},{96,32},{112,48}... | collective-permute-start | bytes 786440 | tf_op jit(solution)/shard_map/ppermute | solution.py:248
  78.6 10.4 %collective-permute-start.18 = (f32[2,256,256]{2,1,0:T(8,128)}, f32[2,256,256]{2,1,0:T(8,128)S(1)}, u32[]{:S(2)}, u32[]{:S(2)}) collective-permute-start(f32[2,256,256]{2,1,0:T(8,128)} %get-tuple-element.65), channel_id=1, source_target_pairs={{0,192},{16,208},{32,224},{48,240},{64,0},{80,16},{96,32},{112,48}... | collective-permute-start | bytes 1572872 | tf_op jit(solution)/shard_map/ppermute | solution.py:248
  79.7 25.4 %collective-permute-start.9 = (f32[256,256]{1,0:T(8,128)S(1)}, f32[256,256]{1,0:T(8,128)S(1)}, u32[]{:S(2)}, u32[]{:S(2)}) collective-permute-start(f32[256,256]{1,0:T(8,128)S(1)} %fusion.8), channel_id=1, source_target_pairs={{0,64},{16,80},{32,96},{48,112},{64,128},{80,144},{96,160},{112,17... | collective-permute-start | bytes 786440 | tf_op jit(solution)/shard_map/ppermute | solution.py:248
  81.1 14.9 %collective-permute-start.17 = (f32[2,256,256]{2,1,0:T(8,128)S(1)}, f32[2,256,256]{2,1,0:T(8,128)S(1)}, u32[]{:S(2)}, u32[]{:S(2)}) collective-permute-start(f32[2,256,256]{2,1,0:T(8,128)S(1)} %copy-done.34), channel_id=1, source_target_pairs={{0,64},{16,80},{32,96},{48,112},{64,128},{80,144},{96,160},{112,17... | collective-permute-start | bytes 1572872 | tf_op jit(solution)/shard_map/ppermute | solution.py:248
  82.3 15.6 %collective-permute-start.14 = (f32[2,256,256]{2,1,0:T(8,128)S(1)}, f32[2,256,256]{2,1,0:T(8,128)S(1)}, u32[]{:S(2)}, u32[]{:S(2)}) collective-permute-start(f32[2,256,256]{2,1,0:T(8,128)S(1)} %copy-done.33), channel_id=1, source_target_pairs={{0,48},{16,0},{32,16},{48,32},{64,112},{80,64},{96,80},{112,96},{1... | collective-permute-start | bytes 1572872 | tf_op jit(solution)/shard_map/ppermute | solution.py:241
  89.0 13.5 %collective-permute-start.13 = (f32[2,256,256]{2,1,0:T(8,128)S(1)}, f32[2,256,256]{2,1,0:T(8,128)S(1)}, u32[]{:S(2)}, u32[]{:S(2)}) collective-permute-start(f32[2,256,256]{2,1,0:T(8,128)S(1)} %copy-done.32), channel_id=1, source_target_pairs={{0,16},{16,32},{32,48},{48,0},{64,80},{80,96},{96,112},{112,64},{1... | collective-permute-start | bytes 1572872 | tf_op jit(solution)/shard_map/ppermute | solution.py:241
  96.0 12.3 %collective-permute-start.6 = (f32[256,256]{1,0:T(8,128)S(1)}, f32[256,256]{1,0:T(8,128)S(1)}, u32[]{:S(2)}, u32[]{:S(2)}) collective-permute-start(f32[256,256]{1,0:T(8,128)S(1)} %fusion.9), channel_id=1, source_target_pairs={{0,48},{16,0},{32,16},{48,32},{64,112},{80,64},{96,80},{112,96},{1... | collective-permute-start | bytes 786440 | tf_op jit(solution)/shard_map/ppermute | solution.py:241
  97.9 10.4 %collective-permute-start.5 = (f32[256,256]{1,0:T(8,128)S(1)}, f32[256,256]{1,0:T(8,128)S(1)}, u32[]{:S(2)}, u32[]{:S(2)}) collective-permute-start(f32[256,256]{1,0:T(8,128)S(1)} %fusion.10), channel_id=1, source_target_pairs={{0,16},{16,32},{32,48},{48,0},{64,80},{80,96},{96,112},{112,64},{1... | collective-permute-start | bytes 786440 | tf_op jit(solution)/shard_map/ppermute | solution.py:241
  102.5 11.0 %collective-permute-start.20 = (f32[256,256]{1,0:T(8,128)S(1)}, f32[256,256]{1,0:T(8,128)S(1)}, u32[]{:S(2)}, u32[]{:S(2)}) collective-permute-start(f32[256,256]{1,0:T(8,128)S(1)} %fusion.3), channel_id=1, source_target_pairs={{0,192},{16,208},{32,224},{48,240},{64,0},{80,16},{96,32},{112,48}... | collective-permute-start | bytes 786440 | tf_op jit(solution)/shard_map/ppermute | solution.py:248
  104.8 8.8 %collective-permute-start.19 = (f32[256,256]{1,0:T(8,128)}, f32[256,256]{1,0:T(8,128)S(1)}, u32[]{:S(2)}, u32[]{:S(2)}) collective-permute-start(f32[256,256]{1,0:T(8,128)} %fusion.4), channel_id=1, source_target_pairs={{0,64},{16,80},{32,96},{48,112},{64,128},{80,144},{96,160},{112,17... | collective-permute-start | bytes 786440 | tf_op jit(solution)/shard_map/ppermute | solution.py:248
  105.1 8.4 %collective-permute-start.16 = (f32[256,256]{1,0:T(8,128)S(1)}, f32[256,256]{1,0:T(8,128)S(1)}, u32[]{:S(2)}, u32[]{:S(2)}) collective-permute-start(f32[256,256]{1,0:T(8,128)S(1)} %fusion.5), channel_id=1, source_target_pairs={{0,48},{16,0},{32,16},{48,32},{64,112},{80,64},{96,80},{112,96},{1... | collective-permute-start | bytes 786440 | tf_op jit(solution)/shard_map/ppermute | solution.py:241
  108.3 7.6 %collective-permute-start.15 = (f32[256,256]{1,0:T(8,128)S(1)}, f32[256,256]{1,0:T(8,128)S(1)}, u32[]{:S(2)}, u32[]{:S(2)}) collective-permute-start(f32[256,256]{1,0:T(8,128)S(1)} %fusion.6), channel_id=1, source_target_pairs={{0,16},{16,32},{32,48},{48,0},{64,80},{80,96},{96,112},{112,64},{1... | collective-permute-start | bytes 786440 | tf_op jit(solution)/shard_map/ppermute | solution.py:241
  120.8 7.9 %collective-permute-start.21 = (f32[256,256]{1,0:T(8,128)}, f32[256,256]{1,0:T(8,128)S(1)}, u32[]{:S(2)}, u32[]{:S(2)}) collective-permute-start(f32[256,256]{1,0:T(8,128)} %get-tuple-element.69), channel_id=1, source_target_pairs={{0,64},{16,80},{32,96},{48,112},{64,128},{80,144},{96,160},{112,17... | collective-permute-start | bytes 786440 | tf_op jit(solution)/shard_map/ppermute | solution.py:248
  120.9 11.9 %collective-permute-start.22 = (f32[256,256]{1,0:T(8,128)}, f32[256,256]{1,0:T(8,128)S(1)}, u32[]{:S(2)}, u32[]{:S(2)}) collective-permute-start(f32[256,256]{1,0:T(8,128)} %get-tuple-element.70), channel_id=1, source_target_pairs={{0,128},{16,144},{32,160},{48,176},{64,192},{80,208},{96,224},{112... | collective-permute-start | bytes 786440 | tf_op jit(solution)/shard_map/ppermute | solution.py:248
  125.5 7.4 %collective-permute-start.23 = (f32[256,256]{1,0:T(8,128)}, f32[256,256]{1,0:T(8,128)S(1)}, u32[]{:S(2)}, u32[]{:S(2)}) collective-permute-start(f32[256,256]{1,0:T(8,128)} %get-tuple-element.71), channel_id=1, source_target_pairs={{0,192},{16,208},{32,224},{48,240},{64,0},{80,16},{96,32},{112,48}... | collective-permute-start | bytes 786440 | tf_op jit(solution)/shard_map/ppermute | solution.py:248
  125.5 10.6 %collective-permute-start.24 = (f32[256,256]{1,0:T(8,128)}, f32[256,256]{1,0:T(8,128)S(1)}, u32[]{:S(2)}, u32[]{:S(2)}) collective-permute-start(f32[256,256]{1,0:T(8,128)} %get-tuple-element.73), channel_id=1, source_target_pairs={{0,16},{16,32},{32,48},{48,0},{64,80},{80,96},{96,112},{112,64},{1... | collective-permute-start | bytes 786440 | tf_op jit(solution)/shard_map/ppermute | solution.py:241
  125.5 10.6 %collective-permute-start.25 = (f32[256,256]{1,0:T(8,128)}, f32[256,256]{1,0:T(8,128)S(1)}, u32[]{:S(2)}, u32[]{:S(2)}) collective-permute-start(f32[256,256]{1,0:T(8,128)} %get-tuple-element.74), channel_id=1, source_target_pairs={{0,32},{16,48},{32,0},{48,16},{64,96},{80,112},{96,64},{112,80},{1... | collective-permute-start | bytes 786440 | tf_op jit(solution)/shard_map/ppermute | solution.py:241
  128.7 8.3 %collective-permute-start.26 = (f32[256,256]{1,0:T(8,128)}, f32[256,256]{1,0:T(8,128)S(1)}, u32[]{:S(2)}, u32[]{:S(2)}) collective-permute-start(f32[256,256]{1,0:T(8,128)} %get-tuple-element.75), channel_id=1, source_target_pairs={{0,48},{16,0},{32,16},{48,32},{64,112},{80,64},{96,80},{112,96},{1... | collective-permute-start | bytes 786440 | tf_op jit(solution)/shard_map/ppermute | solution.py:241
  140.5 27.1 %collective-permute-start.27 = (f32[2,256,256]{2,1,0:T(8,128)}, f32[2,256,256]{2,1,0:T(8,128)S(1)}, u32[]{:S(2)}, u32[]{:S(2)}) collective-permute-start(f32[2,256,256]{2,1,0:T(8,128)} %get-tuple-element.76), channel_id=1, source_target_pairs={{112,32},{0,2},{32,18},{80,48},{208,46},{160,226},{128,242},{240,6... | collective-permute-start | bytes 1572872 | tf_op jit(solution)/shard_map/ppermute | solution.py:351
  143.2 24.4 %collective-permute-start.28 = (f32[2,256,256]{2,1,0:T(8,128)}, f32[2,256,256]{2,1,0:T(8,128)S(1)}, u32[]{:S(2)}, u32[]{:S(2)}) collective-permute-start(f32[2,256,256]{2,1,0:T(8,128)} %get-tuple-element.77), channel_id=1, source_target_pairs={{112,2},{0,48},{32,32},{80,18},{208,226},{160,62},{128,46},{240,24... | collective-permute-start | bytes 1572872 | tf_op jit(solution)/shard_map/ppermute | solution.py:350
  181.6 15.1 %all-to-all-start.2 = ((f32[16,16,128]{2,1,0:T(8,128)}), f32[16,16,128]{2,1,0:T(8,128)S(1)}, u32[]{:S(2)}, u32[]{:S(2)}) async-start(f32[16,16,128]{2,1,0:T(8,128)} %broadcast_in_dim.22), calls=%async_computation.2 | async-start | bytes 262144 | tf_op jit(solution)/shard_map/all_to_all | solution.py:275
  (36 other events, 162.2 us)
